TPU v7x, 128 devices: a whole 4x4x4 slice. The times are simulated.
128 devices in a mesh: blk: 64 (over y, z, x_lo, core), col: 2 (over x_hi).
Axes of the slice: x: 4 (x_hi: 2, x_lo: 2; x = x_hi * 2 + x_lo), y: 4, z: 4, core: 2. Of those that a mesh axis runs over, the one named last changes fastest.
Arguments:
- encodings: bfloat16 [32768, 1024], P(('blk', 'col')), may hold values from -8 to 8
- first_weight: bfloat16 [1024, 512], replicated, may hold values from -0.1875 to 0.1875
- second_weight: bfloat16 [512, 32], replicated, may hold values from -0.25 to 0.25
- inv_scale: float32 [32], replicated, may hold values from 0.2 to 0.8
- outputscale: float32 [1], replicated, may hold values from 0.5 to 2
- noise: float32 [1], replicated, may hold values from 0.2 to 2
- rhs: float32 [32, 32768], P('col', 'blk'), may hold values from -12 to 12
Outputs:
- solution: float32 [32, 32768], P('col', 'blk')
- residual: float32 [32, 32768], P('col', 'blk')
All inputs are finite; a program needn't handle non-finite values.
Results may differ from a plain program's by a relative error of at most 0.0079.
Values sent between devices are 32-bit elements; how exact they have to be, the bound alone decides.
No kernel may reach another device: no remote copies, remote signals or barrier semaphores. Data moves between devices by JAX's collectives and lax.ppermute only.
A program may use at most 64 MiB of HBM per device.

v0:
```python
import jax
import jax.numpy as jnp
from jax import lax
from jax.sharding import PartitionSpec as P


def sent_to_all(x, axis):
    length = lax.axis_size(axis)
    return lax.all_to_all(jnp.broadcast_to(x[None], (length, *x.shape)), axis, 0, 0, tiled=True)


def over_copies(x, axis):
    everything = sent_to_all(x, axis)
    return jnp.sum(everything, axis=0)


def together(arrays, axis):
    line, at, outs = (jnp.concatenate([a.reshape(-1) for a in arrays]), 0, [])
    so_far = over_copies(line, axis)
    for a in arrays:
        outs.append(so_far[at : at + a.size].reshape(a.shape))
        at += a.size
    return tuple(outs)


def laid_out(parts, dim):
    shape = list(parts.shape[1:])
    shape[dim] *= parts.shape[0]
    return jnp.moveaxis(parts, 0, dim).reshape(shape)


def gather_directly(x, axis, dim):
    return laid_out(sent_to_all(x, axis), dim)


def in_one_piece(arrays, axis, dim, along):
    widths = [a.shape[along] for a in arrays]
    both = jnp.concatenate(arrays, axis=along)
    out = lax.all_gather(both, axis, axis=dim, tiled=True)
    return tuple(jnp.split(out, [sum(widths[:k]) for k in range(1, len(widths))], axis=along))


def both_sums(residual, images):
    return together(
        (jnp.sum(residual * residual, axis=1), jnp.sum(residual * images, axis=1)), "blk"
    )


def split_blocks(values, width):
    count = values.shape[1] // width
    return values.reshape(values.shape[0], count, width).transpose(1, 0, 2)


def on_device(encodings, first_weight, second_weight, inv_scale, outputscale, noise, rhs):
    hidden = jnp.maximum(
        jnp.dot(encodings, first_weight, preferred_element_type=jnp.float32), 0.0
    ).astype(jnp.bfloat16)
    features = (
        jnp.einsum("hf,nh->fn", second_weight, hidden, preferred_element_type=jnp.float32)
        * inv_scale[:, None]
    )
    paired = gather_directly(features, "col", 1)
    shard_width = paired.shape[1]
    row_norms = jnp.sum(features * features, axis=0)
    kernel_scale = outputscale[0]
    nugget = noise[0]
    residual = rhs
    moving = lax.all_gather(residual, "col", axis=0, tiled=True)
    initial = jnp.zeros((moving.shape[0], features.shape[1]), jnp.float32)
    shard_pieces = in_one_piece((paired, moving), "blk", 1, 0)

    def advance(running, blocks):
        feat_block, dir_block = blocks
        cross = lax.dot_general(
            features, feat_block, (((0,), (0,)), ((), ())), precision=lax.Precision.HIGHEST
        )
        distance = (
            row_norms[:, None] + jnp.sum(feat_block * feat_block, axis=0)[None, :] - 2.0 * cross
        )
        kernel_tile = kernel_scale * jnp.exp(-0.5 * distance)
        added = lax.dot_general(
            dir_block, kernel_tile, (((1,), (1,)), ((), ())), precision=lax.Precision.HIGHEST
        )
        return (running + added, None)

    images = lax.scan(
        advance,
        initial,
        (split_blocks(shard_pieces[0], shard_width), split_blocks(shard_pieces[1], shard_width)),
    )[0]
    images = lax.all_to_all(images, "col", split_axis=0, concat_axis=1, tiled=True)
    images = images + nugget * residual
    norm_now, product = both_sums(residual, images)
    step_size = norm_now / product
    direction = residual
    solution = step_size[:, None] * direction
    residual = residual - step_size[:, None] * images
    return (solution, residual)


def solution(mesh):
    placed = (P(("blk", "col"), None), P(), P(), P(), P(), P(), P("col", "blk"))
    return jax.shard_map(
        on_device,
        mesh=mesh,
        in_specs=placed,
        out_specs=(P("col", "blk"), P("col", "blk")),
        check_vma=False,
    )
```

profile of v0, /device:TPU:1, one launch (start us, length us, event | category | flops | bytes accessed | tf_op | source)
XLA Modules:
  0.0 463.2 jit_solution(12560361973119428891)
XLA Ops:
  10.7 4.8 %all-to-all-start = ((f32[2,32,256]{2,1,0:T(8,128)}), f32[2,32,256]{2,1,0:T(8,128)S(1)}, u32[]{:S(2)}, u32[]{:S(2)}) async-start(f32[2,32,256]{2,1,0:T(8,128)} %broadcast_in_dim.7), calls=%async_computation | async-start | bytes 131072 | tf_op jit(solution)/shard_map/all_to_all | solution.py:9
  15.5 5.2 %all_gather.6 = f32[32,512]{1,0:T(8,128)S(1)} all-gather(f32[16,512]{1,0:T(8,128)} %param.15), channel_id=1, replica_groups=mesh['blk'=64,'col'=2] {'col'}, dimensions={0}, use_global_device_ids=true | all-gather | bytes 98304 | tf_op jit(solution)/shard_map/all_gather | solution.py:68
  21.4 116.1 %all-gather.2.cloned.1.call-done = f32[64,32768]{1,0:T(8,128)} async-done(((f32[64,512]{1,0:T(8,128)}), f32[64,32768]{1,0:T(8,128)}) %all-gather.2.cloned.1.call-update) | async-done | bytes 8388624 | tf_op jit(solution)/shard_map/all_gather | solution.py:39
  137.6 4.1 fusion.11
  141.6 4.4 copy.35
  146.0 4.4 copy.36
  150.4 282.2 %while.11 = (s32[]{:T(128)}, f32[32,256]{1,0:T(8,128)}, f32[64,32,512]{2,0,1:T(8,128)}, f32[]{:T(128)}, f32[256]{0:T(256)S(1)}, /*index=5*/f32[64,32,512]{2,0,1:T(8,128)}, f32[32,256]{1,0:T(8,128)S(1)}, s32[]{:T(128)}, s32[]{:T(128)}) while((s32[]{:T(128)}, f32[32,256]{1,0:T(8,128)}, f32[64,32,512]{2,0,1:T(8,128)}, f32[]{:T(128)}, ...), condition=%wide.region_4.5_spmd.clone, body=%wide.region_2.4_spmd.clone.sunk | while | flops 101367296 | bytes 1610863 | solution.py:86
  156.8 1.7 convolution_add_fusion.2
  161.2 1.7 convolution_add_fusion.2
  165.6 1.7 convolution_add_fusion.2
  170.0 1.7 convolution_add_fusion.2
  174.5 1.7 convolution_add_fusion.2
  178.9 1.7 convolution_add_fusion.2
  183.3 1.7 convolution_add_fusion.2
  187.7 1.7 convolution_add_fusion.2
  192.1 1.7 convolution_add_fusion.2
  196.6 1.7 convolution_add_fusion.2
  201.0 1.7 convolution_add_fusion.2
  205.4 1.7 convolution_add_fusion.2
  209.8 1.7 convolution_add_fusion.2
  214.2 1.7 convolution_add_fusion.2
  240.8 1.7 convolution_add_fusion.2
  254.0 1.7 convolution_add_fusion.2
  289.4 1.7 convolution_add_fusion.2
  324.8 1.7 convolution_add_fusion.2
  338.0 1.7 convolution_add_fusion.2
  373.4 1.7 convolution_add_fusion.2
  408.8 1.7 convolution_add_fusion.2
  422.0 1.7 convolution_add_fusion.2
  432.6 3.7 all-to-all-start.1
  437.0 3.7 all-to-all-done.1
  440.9 14.6 %all_to_all.30 = f32[64,1,32]{2,1,0:T(1,128)S(1)} all-to-all(f32[64,1,32]{2,1,0:T(1,128)S(1)} %broadcast_in_dim.10), channel_id=1, replica_groups=mesh['blk'=64,'col'=2] {'blk'}, dimensions={0} | all-to-all | bytes 16384 | tf_op jit(solution)/shard_map/all_to_all | solution.py:9
  (253 shorter events, 248.3 us)
Async XLA Ops:
  7.2 1.2 copy-start
  10.7 10.0 %all-to-all-start = ((f32[2,32,256]{2,1,0:T(8,128)}), f32[2,32,256]{2,1,0:T(8,128)S(1)}, u32[]{:S(2)}, u32[]{:S(2)}) async-start(f32[2,32,256]{2,1,0:T(8,128)} %broadcast_in_dim.7), calls=%async_computation | async-start | bytes 131072 | tf_op jit(solution)/shard_map/all_to_all | solution.py:9
  15.5 122.1 %all-gather.2.cloned.1.call-start = ((), (), s32[]{:S(2)}) async-start(), calls=%async_computation.3 | async-start | bytes 8519680 | tf_op jit(solution)/shard_map/all_gather | solution.py:39
  150.4 290.3 %copy-start.1 = (f32[16,512]{1,0:T(8,128)S(1)}, f32[16,512]{1,0:T(8,128)}, u32[]{:S(2)}) copy-start(f32[16,512]{1,0:T(8,128)} %param.15) | copy-start | bytes 98308
  432.6 8.0 %all-to-all-start.1 = ((f32[2,16,256]{2,1,0:T(8,128)}), f32[2,16,256]{2,1,0:T(8,128)S(1)}, u32[]{:S(2)}, u32[]{:S(2)}) async-start(f32[2,16,256]{2,1,0:T(8,128)} %bitcast.5), calls=%async_computation.1 | async-start | bytes 65536 | tf_op jit(solution)/shard_map/all_to_all | solution.py:91
Sparse Core Ops, SparseCore 0:
  21.5 115.9 all-gather.1
where the time goes:
time: 470 us; the launch traced here: 463 us
  matrix products  197 us (42%)
  waiting for transfers between devices  120 us (26%)
  local copies, waits for them, and re-layouts  98.8 us (21%)
  blocking collectives  19.8 us (4%)
  between operations  14.7 us (3%)
  starting transfers between devices  8.59 us (2%)
    all_gather x1, waiting for transfers between devices, in_one_piece(): out = lax.all_gather(both, axis, axis=dim, tiled=True)  116 us
    dot_general x64, matrix products, advance(): lax.dot_general(dir_block, kernel_tile, (((1,), (1,)), ((), ())), precisi...  110 us
    dot_general x64, matrix products, advance(): lax.dot_general(features, feat_block, (((0,), (0,)), ((), ())), precision...  85.3 us
    dynamic_slice x64, local copies, waits for them, and re-layouts, on_device(): lax.scan(advance, initial, (split_blocks(shard_pieces[0], shard_width), s...  84 us
    all_to_all x1, blocking collectives, sent_to_all(): lax.all_to_all(jnp.broadcast_to(x[None], (length, *x.shape)), axis, 0, 0,...  14.6 us
    unnamed x6, local copies, waits for them, and re-layouts  9.99 us
  transfers between devices with their start and end apart: 3, of which 2 were waited for; matrix products, arithmetic and copies ran while one was open for 0% of the time, Pallas kernels for 0%

commit v1 on v0

v1 whole, which is shorter than its diff:
```python
import jax
import jax.numpy as jnp
from jax import lax
from jax.experimental import pallas as pl
from jax.experimental.pallas import tpu as pltpu
from jax.sharding import Mesh
from jax.sharding import PartitionSpec as P

F32, BF16 = jnp.float32, jnp.bfloat16
ROOT_LOG2E = 1.2011224087864498
CHIPS = 32
PEERS = 64
P_SETS = 8
WIDTH = 32
DEPTH = 256


def halves(x):
    high = x.astype(BF16)
    return high, (x - high.astype(F32)).astype(BF16)


def pack_kernel(enc_ref, w1_ref, w2_ref, inv_ref, rhs_ref, out_ref, set_ref):
    hidden = jnp.maximum(
        jnp.dot(enc_ref[...], w1_ref[...], preferred_element_type=F32), 0.0
    ).astype(BF16)
    features = lax.dot_general(
        w2_ref[...], hidden, (((0,), (1,)), ((), ())), preferred_element_type=F32
    )
    n = features.shape[0]
    diagonal = lax.broadcasted_iota(jnp.int32, (n, n), 0) == lax.broadcasted_iota(
        jnp.int32, (n, n), 1
    )
    inv = jnp.sum(
        jnp.where(diagonal, jnp.broadcast_to(inv_ref[...], (n, n)), 0.0), axis=1, keepdims=True
    )
    features = features * inv * ROOT_LOG2E
    half = rhs_ref.shape[1] // 2
    for p in range(P_SETS):
        at = slice(WIDTH * p, WIDTH * (p + 1))
        late = slice(half + WIDTH * p, half + WIDTH * (p + 1))
        set_ref[p] = jnp.concatenate(
            [features[:16, at], features[16:, at], rhs_ref[:, at], rhs_ref[:, late]], axis=1
        )
    for k in range(PEERS):
        out_ref[k, :16] = set_ref[k // P_SETS]
        out_ref[k, 16:] = set_ref[k % P_SETS]


def points_of(ref, k, lo):
    a0, a1 = ref[2 * k, lo : lo + 16], ref[2 * k + 1, lo : lo + 16]
    b0, b1 = ref[CHIPS + 2 * k, lo : lo + 16], ref[CHIPS + 2 * k + 1, lo : lo + 16]
    four = (a0, b0, a1, b1)
    features = jnp.concatenate(
        [
            jnp.concatenate([x[:, :32] for x in four], axis=1),
            jnp.concatenate([x[:, 32:64] for x in four], axis=1),
        ],
        axis=0,
    )
    columns = jnp.concatenate(
        [
            jnp.concatenate([a0[:, 64:], a1[:, 64:]], axis=1),
            jnp.concatenate([b0[:, 64:], b1[:, 64:]], axis=1),
        ],
        axis=0,
    )
    return features, columns


def operand(features, left):
    y1, y2 = halves(features)
    kept = y1.astype(F32) + y2.astype(F32)
    norm = -0.5 * jnp.sum(kept * kept, axis=0, keepdims=True)
    n1 = norm.astype(BF16).astype(F32)
    n2 = (norm - n1).astype(BF16).astype(F32)
    n3 = norm - n1 - n2
    row = lax.broadcasted_iota(jnp.int32, (16, features.shape[1]), 0)
    own, other = (3, 0) if left else (0, 3)
    tail = jnp.where(
        row == own,
        n1,
        jnp.where(
            row == own + 1,
            n2,
            jnp.where(
                row == own + 2, n3, jnp.where((row >= other) & (row < other + 3), 1.0, 0.0)
            ),
        ),
    ).astype(BF16)
    blank = jnp.zeros((DEPTH - 144, features.shape[1]), BF16)
    parts = [y1, y1, y2, y2] if left else [y1, y2, y1, y2]
    return jnp.concatenate(parts + [tail, blank], axis=0)


def product_kernel(own_ref, other_ref, out_ref, left_ref, right_ref, vec_ref, rows_ref, acc_ref):
    tiles = CHIPS // 2

    def prepare(k, _):
        features, columns = points_of(own_ref, k, 0)
        at = pl.ds(pl.multiple_of(k * 128, 128), 128)
        left_ref[at, :] = operand(features, True).T
        rows_ref[k] = columns
        for n, (ref, lo) in enumerate(((own_ref, 16), (other_ref, 0))):
            features, columns = points_of(ref, k, lo)
            at = pl.ds(pl.multiple_of((n * tiles + k) * 128, 128), 128)
            right_ref[:, at] = operand(features, False)
            v1, v2 = halves(columns)
            vec_ref[at, :] = jnp.concatenate([v1, v2], axis=0).T
        return 0

    lax.fori_loop(0, tiles, prepare, 0)
    acc_ref[...] = jnp.zeros_like(acc_ref)

    def multiply(j, _):
        at = pl.ds(pl.multiple_of(j * 256, 256), 256)
        right = right_ref[:, at]
        vec = vec_ref[at, :]
        for r in range(left_ref.shape[0] // 256):
            rows = slice(256 * r, 256 * (r + 1))
            exponent = jnp.dot(left_ref[rows, :], right, preferred_element_type=F32)
            tile = jnp.exp2(exponent).astype(BF16)
            acc_ref[rows, :] += jnp.dot(tile, vec, preferred_element_type=F32)
        return 0

    lax.fori_loop(0, right_ref.shape[1] // 256, multiply, 0)

    product = jnp.zeros((32, 128), F32)
    square = jnp.zeros((32, 128), F32)
    for k in range(tiles):
        both = acc_ref[128 * k : 128 * (k + 1), :].T
        image = both[:32] + both[32:]
        rows = rows_ref[k]
        product = product + rows * image
        square = square + rows * rows
        for xh in range(2):
            top, low = image[16 * xh : 16 * xh + 8], image[16 * xh + 8 : 16 * xh + 16]
            for chip in range(2):
                at = slice(64 * chip, 64 * (chip + 1))
                out_ref[CHIPS * xh + 2 * k + chip, :8] = jnp.concatenate(
                    [top[:, at], low[:, at]], axis=1
                )
    product = jnp.sum(product, axis=1, keepdims=True)
    square = jnp.sum(square, axis=1, keepdims=True) * (P_SETS / PEERS)
    lane = lax.broadcasted_iota(jnp.int32, (8, 128), 1)
    for xh in range(2):
        sums = jnp.zeros((8, 128), F32)
        for n, x in enumerate((product, square)):
            for a in range(2):
                lo = 16 * xh + 8 * a
                sums = jnp.where(lane == 2 * n + a, x[lo : lo + 8], sums)
        out_ref[CHIPS * xh : CHIPS * (xh + 1), 8:] = jnp.broadcast_to(sums, (CHIPS, 8, 128))


def finish_kernel(got_ref, own_ref, other_ref, rhs_ref, scale_ref, noise_ref, sol_ref, res_ref):
    scale, noise = scale_ref[0], noise_ref[0]
    sums = own_ref[...] + other_ref[...]
    product = jnp.concatenate([sums[:, 0:1], sums[:, 1:2]], axis=0)
    square = jnp.concatenate([sums[:, 2:3], sums[:, 3:4]], axis=0)
    step = square / (scale * product + noise * square)
    per = PEERS // P_SETS
    parts = []
    for p in range(P_SETS):
        part = got_ref[per * p, :8]
        for q in range(1, per):
            part = part + got_ref[per * p + q, :8]
        parts.append(part)
    image = jnp.concatenate(
        [
            jnp.concatenate(
                [x[:, lo + 32 * h : lo + 32 * h + 32] for h in range(2) for x in parts], axis=1
            )
            for lo in (0, 64)
        ],
        axis=0,
    )
    direction = rhs_ref[...]
    sol_ref[...] = step * direction
    res_ref[...] = direction - step * (scale * image + noise * direction)


def on_device(encodings, first_weight, second_weight, inv_scale, outputscale, noise, rhs):
    sent = pl.pallas_call(
        pack_kernel,
        out_shape=jax.ShapeDtypeStruct((PEERS, 32, 128), F32),
        scratch_shapes=[pltpu.VMEM((P_SETS, 16, 128), F32)],
        name="features",
    )(encodings, first_weight, second_weight, inv_scale.reshape(1, -1), rhs)
    own = lax.all_to_all(sent, ("xh", "g"), 0, 0, tiled=True)
    other = lax.ppermute(own[:, 16:], "c", [(0, 1), (1, 0)])
    rows, columns = CHIPS * 64, 2 * CHIPS * 64
    partial = pl.pallas_call(
        product_kernel,
        out_shape=jax.ShapeDtypeStruct((PEERS, 16, 128), F32),
        scratch_shapes=[
            pltpu.VMEM((rows, DEPTH), BF16),
            pltpu.VMEM((DEPTH, columns), BF16),
            pltpu.VMEM((columns, 64), BF16),
            pltpu.VMEM((CHIPS // 2, 32, 128), F32),
            pltpu.VMEM((rows, 64), F32),
        ],
        compiler_params=pltpu.CompilerParams(vmem_limit_bytes=32 << 20),
        name="kernel_product",
    )(own, other)
    got = lax.all_to_all(partial, ("xh", "g"), 0, 0, tiled=True)
    sums = jnp.sum(got[:, 8:], axis=0)
    far = lax.ppermute(sums, "c", [(0, 1), (1, 0)])
    vmem, smem = pl.BlockSpec(memory_space=pltpu.VMEM), pl.BlockSpec(memory_space=pltpu.SMEM)
    return pl.pallas_call(
        finish_kernel,
        out_shape=(jax.ShapeDtypeStruct(rhs.shape, F32),) * 2,
        in_specs=[vmem, vmem, vmem, vmem, smem, smem],
        name="update",
    )(got, sums, far, rhs, outputscale, noise)


def solution(mesh):
    split = Mesh(mesh.devices.reshape(CHIPS, 2, 2), ("g", "c", "xh"))
    vectors = P("xh", ("g", "c"))
    return jax.shard_map(
        on_device,
        mesh=split,
        in_specs=(P(("g", "c", "xh"), None), P(), P(), P(), P(), P(), vectors),
        out_specs=(vectors, vectors),
        check_vma=False,
    )
```

time: 470 us -> 80 us (0.17); the launches traced: 463 us -> 79.6 us
  matrix products: 197 us -> 0 us
  waiting for transfers between devices: 120 us -> 1.54 us
  local copies, waits for them, and re-layouts: 98.8 us -> 2.14 us
  blocking collectives: 19.8 us -> 44.9 us
  Pallas kernels: 0 us -> 23.9 us
  between operations: 14.7 us -> 1.98 us
    dot_general x129 -> x0, matrix products: 197 us -> none  [the longest x64 110 us: advance(): lax.dot_general(dir_block, kernel_tile, (((1,), (1,)), ((), ())), precisi...]
    all_gather x1 -> x0, waiting for transfers between devices: 116 us -> none  [in_one_piece(): out = lax.all_gather(both, axis, axis=dim, tiled=True)]
    dynamic_slice x64 -> x0, local copies, waits for them, and re-layouts: 84 us -> none  [on_device(): lax.scan(advance, initial, (split_blocks(shard_pieces[0], shard_width), s...]
    all_to_all x1 -> x2, blocking collectives: 14.6 us -> 44.9 us  [the longest x1 28.2 us: on_device(): own = lax.all_to_all(sent, ('xh', 'g'), 0, 0, tiled=True)]
    pallas_call x0 -> x3, Pallas kernels: none -> 23.9 us  [the longest x1 18.9 us: on_device(): pl.pallas_call(product_kernel, out_shape=jax.ShapeDtypeStruct((PEERS, 16,...]
    all_to_all x2 -> x0, starting transfers between devices: 8.59 us -> none  [the longest x1 4.84 us: sent_to_all(): lax.all_to_all(jnp.broadcast_to(x[None], (length, *x.shape)), axis, 0, 0,...]
    unnamed x6 -> x7, local copies, waits for them, and re-layouts: 9.99 us -> 2.11 us
    all_gather x1 -> x0, blocking collectives: 5.19 us -> none  [on_device(): moving = lax.all_gather(residual, 'col', axis=0, tiled=True)]
  transfers between devices with their start and end apart: 3 -> 2, of which waited for: 2 -> 1; matrix products, arithmetic and copies ran while one was open for 0% -> 0% of each run, Pallas kernels for 0% -> 0%
where the time goes in v1:
time: 80 us; the launch traced here: 79.6 us
  blocking collectives  44.9 us (56%)
  Pallas kernels  23.9 us (30%)
  starting transfers between devices  5.11 us (6%)
  local copies, waits for them, and re-layouts  2.14 us (3%)
  between operations  1.98 us (2%)
  waiting for transfers between devices  1.54 us (2%)
    all_to_all x1, blocking collectives, on_device(): own = lax.all_to_all(sent, ('xh', 'g'), 0, 0, tiled=True)  28.2 us
    pallas_call x1, Pallas kernels, on_device(): pl.pallas_call(product_kernel, out_shape=jax.ShapeDtypeStruct((PEERS, 16,...  18.9 us
    all_to_all x1, blocking collectives, on_device(): got = lax.all_to_all(partial, ('xh', 'g'), 0, 0, tiled=True)  16.6 us
    pallas_call x1, Pallas kernels, on_device(): pl.pallas_call(pack_kernel, out_shape=jax.ShapeDtypeStruct((PEERS, 32, 12...  3.07 us
    ppermute x1, starting transfers between devices, on_device(): other = lax.ppermute(own[:, 16:], 'c', [(0, 1), (1, 0)])  2.66 us
    ppermute x1, starting transfers between devices, on_device(): far = lax.ppermute(sums, 'c', [(0, 1), (1, 0)])  2.45 us
    unnamed x7, local copies, waits for them, and re-layouts  2.11 us
    pallas_call x1, Pallas kernels, on_device(): pl.pallas_call(finish_kernel, out_shape=(jax.ShapeDtypeStruct(rhs.shape,...  1.96 us
  transfers between devices with their start and end apart: 2, of which 1 were waited for; matrix products, arithmetic and copies ran while one was open for 0% of the time, Pallas kernels for 0%

profile of v1, /device:TPU:1, one launch (start us, length us, event | category | flops | bytes accessed | tf_op | source)
XLA Modules:
  0.0 79.6 jit_solution(14948412984136215072)
XLA Ops:
  0.6 1.5 %copy.9.w2_ref = bf16[512,32]{1,0:T(8,128)(2,1)} copy(bf16[512,32]{0,1:T(8,128)(2,1)} %param.9) | data formatting | bytes 65536 | tf_op args[2]
  2.1 3.1 %features.1 = f32[64,32,128]{2,1,0:T(8,128)} custom-call(bf16[256,1024]{1,0:T(8,128)(2,1)} %enc_ref.1, bf16[1024,512]{1,0:T(8,128)(2,1)} %w1_ref.1, bf16[512,32]{1,0:T(8,128)(2,1)} %copy.9.w2_ref, f32[1,32]{1,0:T(1,128)} %bitcast.1, f32[16,512]{1,0:T(8,128)} %rhs_ref.3), custom_call_target="tpu_custom_call" | custom-call | tf_op jit(solution)/shard_map/features/pallas_call | solution.py:183
  5.2 28.2 %all_to_all.10.own_ref = f32[64,32,128]{2,1,0:T(8,128)S(1)} all-to-all(f32[64,32,128]{2,1,0:T(8,128)} %features.1), channel_id=1, replica_groups=mesh['g'=32,'c'=2,'xh'=2] {'xh','g'}, dimensions={0} | all-to-all | bytes 2097152 | tf_op jit(solution)/shard_map/all_to_all | solution.py:189
  33.5 2.7 %collective-permute-start = (f32[64,16,128]{2,1,0:T(8,128)S(1)}, f32[64,16,128]{2,1,0:T(8,128)S(1)}, u32[]{:S(2)}, u32[]{:S(2)}) collective-permute-start(f32[64,16,128]{2,1,0:T(8,128)S(1)} %slice.8), channel_id=1, source_target_pairs={{0,2},{2,0},{1,3},{3,1},{4,6},{6,4},{5,7},{7,5},{8,10},{10,8},{9,1... | collective-permute-start | bytes 1572872 | tf_op jit(solution)/shard_map/ppermute | solution.py:190
  36.2 1.5 %collective-permute-done.other_ref = f32[64,16,128]{2,1,0:T(8,128)S(1)} collective-permute-done((f32[64,16,128]{2,1,0:T(8,128)S(1)}, f32[64,16,128]{2,1,0:T(8,128)S(1)}, u32[]{:S(2)}, u32[]{:S(2)}) %collective-permute-start) | collective-permute-done | bytes 524320 | tf_op jit(solution)/shard_map/ppermute | solution.py:190
  37.7 18.9 %kernel_product.1 = f32[64,16,128]{2,1,0:T(8,128)S(1)} custom-call(f32[64,32,128]{2,1,0:T(8,128)S(1)} %all_to_all.10.own_ref, f32[64,16,128]{2,1,0:T(8,128)S(1)} %collective-permute-done.other_ref), custom_call_target="tpu_custom_call" | custom-call | tf_op jit(solution)/shard_map/kernel_product/pallas_call | solution.py:192
  56.6 16.6 %all_to_all.11.got_ref = f32[64,16,128]{2,1,0:T(8,128)S(1)} all-to-all(f32[64,16,128]{2,1,0:T(8,128)S(1)} %kernel_product.1), channel_id=1, replica_groups=mesh['g'=32,'c'=2,'xh'=2] {'xh','g'}, dimensions={0} | all-to-all | bytes 1048576 | tf_op jit(solution)/shard_map/all_to_all | solution.py:205
  73.2 0.0 copy-start
  73.2 0.1 slice_reduce_fusion.own_ref
  73.3 0.0 copy-start.1
  73.3 2.5 %collective-permute-start.1 = (f32[8,128]{1,0:T(8,128)S(1)}, f32[8,128]{1,0:T(8,128)S(1)}, u32[]{:S(2)}, u32[]{:S(2)}) collective-permute-start(f32[8,128]{1,0:T(8,128)S(1)} %slice_reduce_fusion.own_ref), channel_id=1, source_target_pairs={{0,2},{2,0},{1,3},{3,1},{4,6},{6,4},{5,7},{7,5},{8,10},{10,8},{9,1... | collective-permute-start | bytes 12296 | tf_op jit(solution)/shard_map/ppermute | solution.py:207
  77.1 0.0 collective-permute-done.1.other_ref
  77.1 0.0 copy-done
  77.1 0.0 copy-done.1
  77.1 0.0 copy-start.2
  77.1 0.6 copy-done.2
  77.7 2.0 %update.1 = (f32[16,512]{1,0:T(8,128)}, f32[16,512]{1,0:T(8,128)}) custom-call(f32[64,16,128]{2,1,0:T(8,128)} %copy-done, f32[8,128]{1,0:T(8,128)} %copy-done.1, f32[8,128]{1,0:T(8,128)} %copy-done.2, f32[16,512]{1,0:T(8,128)} %rhs_ref.3, f32[1]{0:T(128)S(6)} %copy.10.scale_ref, f32[1]{0:T(128)S(6)} %copy.11.noise_ref), custom_call_target="tpu_custom_call" | custom-call | tf_op jit(solution)/shard_map/update/pallas_call | solution.py:209
  (1 shorter events, 0.0 us)
Async XLA Ops:
  33.5 4.2 %collective-permute-start = (f32[64,16,128]{2,1,0:T(8,128)S(1)}, f32[64,16,128]{2,1,0:T(8,128)S(1)}, u32[]{:S(2)}, u32[]{:S(2)}) collective-permute-start(f32[64,16,128]{2,1,0:T(8,128)S(1)} %slice.8), channel_id=1, source_target_pairs={{0,2},{2,0},{1,3},{3,1},{4,6},{6,4},{5,7},{7,5},{8,10},{10,8},{9,1... | collective-permute-start | bytes 1572872 | tf_op jit(solution)/shard_map/ppermute | solution.py:190
  73.2 3.8 %copy-start = (f32[64,16,128]{2,1,0:T(8,128)}, f32[64,16,128]{2,1,0:T(8,128)S(1)}, u32[]{:S(2)}) copy-start(f32[64,16,128]{2,1,0:T(8,128)S(1)} %all_to_all.11.got_ref) | copy-start | bytes 1572868
  73.3 3.8 %copy-start.1 = (f32[8,128]{1,0:T(8,128)}, f32[8,128]{1,0:T(8,128)S(1)}, u32[]{:S(2)}) copy-start(f32[8,128]{1,0:T(8,128)S(1)} %slice_reduce_fusion.own_ref) | copy-start | bytes 12292
  73.3 3.8 %collective-permute-start.1 = (f32[8,128]{1,0:T(8,128)S(1)}, f32[8,128]{1,0:T(8,128)S(1)}, u32[]{:S(2)}, u32[]{:S(2)}) collective-permute-start(f32[8,128]{1,0:T(8,128)S(1)} %slice_reduce_fusion.own_ref), channel_id=1, source_target_pairs={{0,2},{2,0},{1,3},{3,1},{4,6},{6,4},{5,7},{7,5},{8,10},{10,8},{9,1... | collective-permute-start | bytes 12296 | tf_op jit(solution)/shard_map/ppermute | solution.py:207
  77.1 0.6 copy-start.2

commit v2 on v1

--- a/solution.py
+++ b/solution.py
@@ -25,7 +25,7 @@
         jnp.dot(enc_ref[...], w1_ref[...], preferred_element_type=F32), 0.0
     ).astype(BF16)
     features = lax.dot_general(
-        w2_ref[...], hidden, (((0,), (1,)), ((), ())), preferred_element_type=F32
+        w2_ref[...], hidden, (((1,), (1,)), ((), ())), preferred_element_type=F32
     )
     n = features.shape[0]
     diagonal = lax.broadcasted_iota(jnp.int32, (n, n), 0) == lax.broadcasted_iota(
@@ -184,8 +184,9 @@
         pack_kernel,
         out_shape=jax.ShapeDtypeStruct((PEERS, 32, 128), F32),
         scratch_shapes=[pltpu.VMEM((P_SETS, 16, 128), F32)],
+        compiler_params=pltpu.CompilerParams(vmem_limit_bytes=8 << 20),
         name="features",
-    )(encodings, first_weight, second_weight, inv_scale.reshape(1, -1), rhs)
+    )(encodings, first_weight, second_weight.T, inv_scale.reshape(1, -1), rhs)
     own = lax.all_to_all(sent, ("xh", "g"), 0, 0, tiled=True)
     other = lax.ppermute(own[:, 16:], "c", [(0, 1), (1, 0)])
     rows, columns = CHIPS * 64, 2 * CHIPS * 64
@@ -210,6 +211,7 @@
         finish_kernel,
         out_shape=(jax.ShapeDtypeStruct(rhs.shape, F32),) * 2,
         in_specs=[vmem, vmem, vmem, vmem, smem, smem],
+        compiler_params=pltpu.CompilerParams(vmem_limit_bytes=8 << 20),
         name="update",
     )(got, sums, far, rhs, outputscale, noise)
 

time: 80 us -> 78.8 us (0.985)
  Pallas kernels: 23.9 us -> 20.5 us
  local copies, waits for them, and re-layouts: 2.14 us -> 4.47 us
    pallas_call x1, Pallas kernels: 3.07 us -> 0.69 us  [on_device(): pl.pallas_call(pack_kernel, out_shape=jax.ShapeDtypeStruct((PEERS, 32, 12...]
    unnamed x7 -> x12, local copies, waits for them, and re-layouts: 2.11 us -> 4.43 us
    pallas_call x1, Pallas kernels: 1.96 us -> 0.91 us  [on_device(): pl.pallas_call(finish_kernel, out_shape=(jax.ShapeDtypeStruct(rhs.shape,...]
where the time goes in v2:
time: 78.8 us; the launch traced here: 78.3 us
  blocking collectives  44.7 us (57%)
  Pallas kernels  20.5 us (26%)
  starting transfers between devices  5.1 us (6%)
  local copies, waits for them, and re-layouts  4.47 us (6%)
  between operations  1.98 us (3%)
  waiting for transfers between devices  1.54 us (2%)
    all_to_all x1, blocking collectives, on_device(): own = lax.all_to_all(sent, ('xh', 'g'), 0, 0, tiled=True)  28 us
    pallas_call x1, Pallas kernels, on_device(): pl.pallas_call(product_kernel, out_shape=jax.ShapeDtypeStruct((PEERS, 16,...  18.9 us
    all_to_all x1, blocking collectives, on_device(): got = lax.all_to_all(partial, ('xh', 'g'), 0, 0, tiled=True)  16.6 us
    unnamed x12, local copies, waits for them, and re-layouts  4.43 us
    ppermute x1, starting transfers between devices, on_device(): other = lax.ppermute(own[:, 16:], 'c', [(0, 1), (1, 0)])  2.66 us
    ppermute x1, starting transfers between devices, on_device(): far = lax.ppermute(sums, 'c', [(0, 1), (1, 0)])  2.44 us
  transfers between devices with their start and end apart: 2, of which 1 were waited for; matrix products, arithmetic and copies ran while one was open for 0% of the time, Pallas kernels for 0%

profile of v2, /device:TPU:1, one launch (start us, length us, event | category | flops | bytes accessed | tf_op | source)
XLA Modules:
  0.0 78.3 jit_solution(13480725124149673661)
XLA Ops:
  0.6 0.0 copy-start.5
  0.6 0.6 copy-done.5
  1.3 0.0 copy-start
  1.3 1.2 %copy-done = bf16[1024,512]{1,0:T(8,128)(2,1)S(1)} copy-done((bf16[1024,512]{1,0:T(8,128)(2,1)S(1)}, bf16[1024,512]{1,0:T(8,128)(2,1)}, u32[]{:S(2)}) %copy-start) | copy-done | bytes 1048600
  2.5 0.0 copy-start.1
  2.5 1.0 %copy-done.1 = bf16[256,1024]{1,0:T(8,128)(2,1)S(1)} copy-done((bf16[256,1024]{1,0:T(8,128)(2,1)S(1)}, bf16[256,1024]{1,0:T(8,128)(2,1)}, u32[]{:S(2)}) %copy-start.1) | copy-done | bytes 524312
  3.6 0.0 copy-start.2
  3.6 0.8 copy-done.2
  4.3 0.0 copy-start.4
  4.3 0.8 copy-done.4
  5.1 0.7 features.1
  5.8 28.0 %all_to_all.10.own_ref = f32[64,32,128]{2,1,0:T(8,128)S(1)} all-to-all(f32[64,32,128]{2,1,0:T(8,128)S(1)} %features.1), channel_id=1, replica_groups=mesh['g'=32,'c'=2,'xh'=2] {'xh','g'}, dimensions={0} | all-to-all | bytes 2097152 | tf_op jit(solution)/shard_map/all_to_all | solution.py:190
  33.9 2.7 %collective-permute-start = (f32[64,16,128]{2,1,0:T(8,128)S(1)}, f32[64,16,128]{2,1,0:T(8,128)S(1)}, u32[]{:S(2)}, u32[]{:S(2)}) collective-permute-start(f32[64,16,128]{2,1,0:T(8,128)S(1)} %slice.8), channel_id=1, source_target_pairs={{0,2},{2,0},{1,3},{3,1},{4,6},{6,4},{5,7},{7,5},{8,10},{10,8},{9,1... | collective-permute-start | bytes 1572872 | tf_op jit(solution)/shard_map/ppermute | solution.py:191
  36.5 1.5 %collective-permute-done.other_ref = f32[64,16,128]{2,1,0:T(8,128)S(1)} collective-permute-done((f32[64,16,128]{2,1,0:T(8,128)S(1)}, f32[64,16,128]{2,1,0:T(8,128)S(1)}, u32[]{:S(2)}, u32[]{:S(2)}) %collective-permute-start) | collective-permute-done | bytes 524320 | tf_op jit(solution)/shard_map/ppermute | solution.py:191
  38.1 18.9 %kernel_product.1 = f32[64,16,128]{2,1,0:T(8,128)S(1)} custom-call(f32[64,32,128]{2,1,0:T(8,128)S(1)} %all_to_all.10.own_ref, f32[64,16,128]{2,1,0:T(8,128)S(1)} %collective-permute-done.other_ref), custom_call_target="tpu_custom_call" | custom-call | tf_op jit(solution)/shard_map/kernel_product/pallas_call | solution.py:193
  57.0 16.6 %all_to_all.11.got_ref = f32[64,16,128]{2,1,0:T(8,128)S(1)} all-to-all(f32[64,16,128]{2,1,0:T(8,128)S(1)} %kernel_product.1), channel_id=1, replica_groups=mesh['g'=32,'c'=2,'xh'=2] {'xh','g'}, dimensions={0} | all-to-all | bytes 1048576 | tf_op jit(solution)/shard_map/all_to_all | solution.py:206
  73.6 0.0 copy-start.3
  73.6 0.1 slice_reduce_fusion.own_ref
  73.7 2.4 %collective-permute-start.1 = (f32[8,128]{1,0:T(8,128)S(1)}, f32[8,128]{1,0:T(8,128)S(1)}, u32[]{:S(2)}, u32[]{:S(2)}) collective-permute-start(f32[8,128]{1,0:T(8,128)S(1)} %slice_reduce_fusion.own_ref), channel_id=1, source_target_pairs={{0,2},{2,0},{1,3},{3,1},{4,6},{6,4},{5,7},{7,5},{8,10},{10,8},{9,1... | collective-permute-start | bytes 12296 | tf_op jit(solution)/shard_map/ppermute | solution.py:208
  77.4 0.0 collective-permute-done.1.other_ref
  77.4 0.0 copy-done.3
  77.4 0.9 %update.1 = (f32[16,512]{1,0:T(8,128)}, f32[16,512]{1,0:T(8,128)}) custom-call(f32[64,16,128]{2,1,0:T(8,128)S(1)} %all_to_all.11.got_ref, f32[8,128]{1,0:T(8,128)S(1)} %slice_reduce_fusion.own_ref, f32[8,128]{1,0:T(8,128)S(1)} %collective-permute-done.1.other_ref, f32[16,512]{1,0:T(8,128)S(1)} %copy-done.3, f32[1]{0:T(128)S(6)} %copy.9.scale_ref, ...), custom_call_target="tpu_custom_call" | custom-call | tf_op jit(solution)/shard_map/update/pallas_call | solution.py:210
  (1 shorter events, 0.0 us)
Async XLA Ops:
  0.6 0.7 copy-start.5
  1.3 1.2 %copy-start = (bf16[1024,512]{1,0:T(8,128)(2,1)S(1)}, bf16[1024,512]{1,0:T(8,128)(2,1)}, u32[]{:S(2)}) copy-start(bf16[1024,512]{1,0:T(8,128)(2,1)} %w1_ref.1) | copy-start | bytes 3145732
  2.5 1.0 %copy-start.1 = (bf16[256,1024]{1,0:T(8,128)(2,1)S(1)}, bf16[256,1024]{1,0:T(8,128)(2,1)}, u32[]{:S(2)}) copy-start(bf16[256,1024]{1,0:T(8,128)(2,1)} %enc_ref.1) | copy-start | bytes 1572868
  3.6 0.8 copy-start.2
  4.3 0.8 copy-start.4
  33.9 4.2 %collective-permute-start = (f32[64,16,128]{2,1,0:T(8,128)S(1)}, f32[64,16,128]{2,1,0:T(8,128)S(1)}, u32[]{:S(2)}, u32[]{:S(2)}) collective-permute-start(f32[64,16,128]{2,1,0:T(8,128)S(1)} %slice.8), channel_id=1, source_target_pairs={{0,2},{2,0},{1,3},{3,1},{4,6},{6,4},{5,7},{7,5},{8,10},{10,8},{9,1... | collective-permute-start | bytes 1572872 | tf_op jit(solution)/shard_map/ppermute | solution.py:191
  73.6 3.8 %copy-start.3 = (f32[16,512]{1,0:T(8,128)S(1)}, f32[16,512]{1,0:T(8,128)}, u32[]{:S(2)}) copy-start(f32[16,512]{1,0:T(8,128)} %rhs_ref.3) | copy-start | bytes 98308
  73.7 3.7 %collective-permute-start.1 = (f32[8,128]{1,0:T(8,128)S(1)}, f32[8,128]{1,0:T(8,128)S(1)}, u32[]{:S(2)}, u32[]{:S(2)}) collective-permute-start(f32[8,128]{1,0:T(8,128)S(1)} %slice_reduce_fusion.own_ref), channel_id=1, source_target_pairs={{0,2},{2,0},{1,3},{3,1},{4,6},{6,4},{5,7},{7,5},{8,10},{10,8},{9,1... | collective-permute-start | bytes 12296 | tf_op jit(solution)/shard_map/ppermute | solution.py:208

commit v3 on v2

--- a/solution.py
+++ b/solution.py
@@ -13,6 +13,9 @@
 P_SETS = 8
 WIDTH = 32
 DEPTH = 256
+STEPS = 4
+STRIP = 2048
+ROWS = 128
 
 
 def halves(x):
@@ -20,10 +23,49 @@
     return high, (x - high.astype(F32)).astype(BF16)
 
 
-def pack_kernel(enc_ref, w1_ref, w2_ref, inv_ref, rhs_ref, out_ref, set_ref):
-    hidden = jnp.maximum(
-        jnp.dot(enc_ref[...], w1_ref[...], preferred_element_type=F32), 0.0
-    ).astype(BF16)
+def pack_kernel(
+    enc_hbm, w1_hbm, w2_hbm, inv_hbm, scale_hbm, noise_hbm, rhs_hbm,
+    out_ref, pair_ref,
+    enc_ref, w1_ref, w2_ref, inv_ref, scale_ref, noise_ref, rhs_ref, set_ref, big_sem, sem,
+):
+    small = [
+        pltpu.make_async_copy(src, dst, sem.at[n])
+        for n, (src, dst) in enumerate(
+            (
+                (w2_hbm, w2_ref),
+                (inv_hbm, inv_ref),
+                (rhs_hbm, rhs_ref),
+                (scale_hbm, scale_ref),
+                (noise_hbm, noise_ref),
+            )
+        )
+    ]
+    depth = enc_hbm.shape[1] // STEPS
+    big = []
+    for n in range(STEPS):
+        at = pl.ds(n * depth, depth)
+        big.append(
+            (
+                pltpu.make_async_copy(enc_hbm.at[:, at], enc_ref.at[:, at], big_sem.at[2 * n]),
+                pltpu.make_async_copy(w1_hbm.at[at], w1_ref.at[at], big_sem.at[2 * n + 1]),
+            )
+        )
+    for pair in big:
+        for copy in pair:
+            copy.start()
+    for copy in small:
+        copy.start()
+    hidden = jnp.zeros((enc_hbm.shape[0], w1_hbm.shape[1]), F32)
+    for n in range(STEPS):
+        at = slice(n * depth, (n + 1) * depth)
+        for copy in big[n]:
+            copy.wait()
+        hidden = hidden + jnp.dot(enc_ref[:, at], w1_ref[at], preferred_element_type=F32)
+    hidden = jnp.maximum(hidden, 0.0).astype(BF16)
+    for copy in small:
+        copy.wait()
+    pair_ref[:4] = jnp.broadcast_to(scale_ref[...], (4, 128))
+    pair_ref[4:] = jnp.broadcast_to(noise_ref[...], (4, 128))
     features = lax.dot_general(
         w2_ref[...], hidden, (((1,), (1,)), ((), ())), preferred_element_type=F32
     )
@@ -93,53 +135,44 @@
     return jnp.concatenate(parts + [tail, blank], axis=0)
 
 
-def product_kernel(own_ref, other_ref, out_ref, left_ref, right_ref, vec_ref, rows_ref, acc_ref):
+def product_kernel(own_ref, other_ref, out_ref, left_ref, right_ref, vec_ref, rows_ref):
     tiles = CHIPS // 2
 
-    def prepare(k, _):
+    for k in range(tiles):
         features, columns = points_of(own_ref, k, 0)
-        at = pl.ds(pl.multiple_of(k * 128, 128), 128)
+        at = slice(k * 128, (k + 1) * 128)
         left_ref[at, :] = operand(features, True).T
         rows_ref[k] = columns
         for n, (ref, lo) in enumerate(((own_ref, 16), (other_ref, 0))):
             features, columns = points_of(ref, k, lo)
-            at = pl.ds(pl.multiple_of((n * tiles + k) * 128, 128), 128)
+            at = slice((n * tiles + k) * 128, (n * tiles + k + 1) * 128)
             right_ref[:, at] = operand(features, False)
             v1, v2 = halves(columns)
             vec_ref[at, :] = jnp.concatenate([v1, v2], axis=0).T
-        return 0
-
-    lax.fori_loop(0, tiles, prepare, 0)
-    acc_ref[...] = jnp.zeros_like(acc_ref)
-
-    def multiply(j, _):
-        at = pl.ds(pl.multiple_of(j * 256, 256), 256)
-        right = right_ref[:, at]
-        vec = vec_ref[at, :]
-        for r in range(left_ref.shape[0] // 256):
-            rows = slice(256 * r, 256 * (r + 1))
-            exponent = jnp.dot(left_ref[rows, :], right, preferred_element_type=F32)
-            tile = jnp.exp2(exponent).astype(BF16)
-            acc_ref[rows, :] += jnp.dot(tile, vec, preferred_element_type=F32)
-        return 0
-
-    lax.fori_loop(0, right_ref.shape[1] // 256, multiply, 0)
-
     product = jnp.zeros((32, 128), F32)
     square = jnp.zeros((32, 128), F32)
-    for k in range(tiles):
-        both = acc_ref[128 * k : 128 * (k + 1), :].T
-        image = both[:32] + both[32:]
-        rows = rows_ref[k]
-        product = product + rows * image
-        square = square + rows * rows
-        for xh in range(2):
-            top, low = image[16 * xh : 16 * xh + 8], image[16 * xh + 8 : 16 * xh + 16]
-            for chip in range(2):
-                at = slice(64 * chip, 64 * (chip + 1))
-                out_ref[CHIPS * xh + 2 * k + chip, :8] = jnp.concatenate(
-                    [top[:, at], low[:, at]], axis=1
-                )
+    for r in range(left_ref.shape[0] // ROWS):
+        left = left_ref[ROWS * r : ROWS * (r + 1), :]
+        total = jnp.zeros((ROWS, 64), F32)
+        for j in range(right_ref.shape[1] // STRIP):
+            at = slice(STRIP * j, STRIP * (j + 1))
+            exponent = jnp.dot(left, right_ref[:, at], preferred_element_type=F32)
+            tile = jnp.exp2(exponent).astype(BF16)
+            total = total + jnp.dot(tile, vec_ref[at, :], preferred_element_type=F32)
+        for k in range(ROWS // 128 * r, ROWS // 128 * (r + 1)):
+            lo = 128 * k - ROWS * r
+            both = total[lo : lo + 128].T
+            image = both[:32] + both[32:]
+            rows = rows_ref[k]
+            product = product + rows * image
+            square = square + rows * rows
+            for xh in range(2):
+                top, low = image[16 * xh : 16 * xh + 8], image[16 * xh + 8 : 16 * xh + 16]
+                for chip in range(2):
+                    at = slice(64 * chip, 64 * (chip + 1))
+                    out_ref[CHIPS * xh + 2 * k + chip, :8] = jnp.concatenate(
+                        [top[:, at], low[:, at]], axis=1
+                    )
     product = jnp.sum(product, axis=1, keepdims=True)
     square = jnp.sum(square, axis=1, keepdims=True) * (P_SETS / PEERS)
     lane = lax.broadcasted_iota(jnp.int32, (8, 128), 1)
@@ -152,8 +185,8 @@
         out_ref[CHIPS * xh : CHIPS * (xh + 1), 8:] = jnp.broadcast_to(sums, (CHIPS, 8, 128))
 
 
-def finish_kernel(got_ref, own_ref, other_ref, rhs_ref, scale_ref, noise_ref, sol_ref, res_ref):
-    scale, noise = scale_ref[0], noise_ref[0]
+def finish_kernel(got_ref, own_ref, other_ref, rhs_ref, pair_ref, sol_ref, res_ref):
+    scale, noise = pair_ref[0:1, 0:1], pair_ref[4:5, 0:1]
     sums = own_ref[...] + other_ref[...]
     product = jnp.concatenate([sums[:, 0:1], sums[:, 1:2]], axis=0)
     square = jnp.concatenate([sums[:, 2:3], sums[:, 3:4]], axis=0)
@@ -180,13 +213,36 @@
 
 
 def on_device(encodings, first_weight, second_weight, inv_scale, outputscale, noise, rhs):
-    sent = pl.pallas_call(
+    hbm, vmem = pl.BlockSpec(memory_space=pltpu.HBM), pl.BlockSpec(memory_space=pltpu.VMEM)
+    sent, pair = pl.pallas_call(
         pack_kernel,
-        out_shape=jax.ShapeDtypeStruct((PEERS, 32, 128), F32),
-        scratch_shapes=[pltpu.VMEM((P_SETS, 16, 128), F32)],
-        compiler_params=pltpu.CompilerParams(vmem_limit_bytes=8 << 20),
+        out_shape=(
+            jax.ShapeDtypeStruct((PEERS, 32, 128), F32),
+            jax.ShapeDtypeStruct((8, 128), F32),
+        ),
+        in_specs=[hbm] * 7,
+        scratch_shapes=[
+            pltpu.VMEM(encodings.shape, BF16),
+            pltpu.VMEM(first_weight.shape, BF16),
+            pltpu.VMEM(second_weight.shape[::-1], BF16),
+            pltpu.VMEM((1, inv_scale.size), F32),
+            pltpu.VMEM((1, 1), F32),
+            pltpu.VMEM((1, 1), F32),
+            pltpu.VMEM(rhs.shape, F32),
+            pltpu.VMEM((P_SETS, 16, 128), F32),
+            pltpu.SemaphoreType.DMA((2 * STEPS,)),
+            pltpu.SemaphoreType.DMA((5,)),
+        ],
         name="features",
-    )(encodings, first_weight, second_weight.T, inv_scale.reshape(1, -1), rhs)
+    )(
+        encodings,
+        first_weight,
+        second_weight.T,
+        inv_scale.reshape(1, -1),
+        outputscale.reshape(1, 1),
+        noise.reshape(1, 1),
+        rhs,
+    )
     own = lax.all_to_all(sent, ("xh", "g"), 0, 0, tiled=True)
     other = lax.ppermute(own[:, 16:], "c", [(0, 1), (1, 0)])
     rows, columns = CHIPS * 64, 2 * CHIPS * 64
@@ -198,7 +254,6 @@
             pltpu.VMEM((DEPTH, columns), BF16),
             pltpu.VMEM((columns, 64), BF16),
             pltpu.VMEM((CHIPS // 2, 32, 128), F32),
-            pltpu.VMEM((rows, 64), F32),
         ],
         compiler_params=pltpu.CompilerParams(vmem_limit_bytes=32 << 20),
         name="kernel_product",
@@ -206,14 +261,13 @@
     got = lax.all_to_all(partial, ("xh", "g"), 0, 0, tiled=True)
     sums = jnp.sum(got[:, 8:], axis=0)
     far = lax.ppermute(sums, "c", [(0, 1), (1, 0)])
-    vmem, smem = pl.BlockSpec(memory_space=pltpu.VMEM), pl.BlockSpec(memory_space=pltpu.SMEM)
     return pl.pallas_call(
         finish_kernel,
         out_shape=(jax.ShapeDtypeStruct(rhs.shape, F32),) * 2,
-        in_specs=[vmem, vmem, vmem, vmem, smem, smem],
+        in_specs=[vmem] * 5,
         compiler_params=pltpu.CompilerParams(vmem_limit_bytes=8 << 20),
         name="update",
-    )(got, sums, far, rhs, outputscale, noise)
+    )(got, sums, far, rhs, pair)
 
 
 def solution(mesh):

time: 78.8 us -> 68.8 us (0.87)
  Pallas kernels: 20.5 us -> 14.2 us
  local copies, waits for them, and re-layouts: 4.47 us -> 0.04 us
  waiting for transfers between devices: 1.54 us -> 2.36 us
    pallas_call x1, Pallas kernels: 18.9 us -> 10.1 us  [on_device(): pl.pallas_call(product_kernel, out_shape=jax.ShapeDtypeStruct((PEERS, 16,...]
    unnamed x12 -> x4, local copies, waits for them, and re-layouts: 4.43 us -> 0.01 us
    pallas_call x1, Pallas kernels: 0.69 us -> 3.14 us  [on_device(): pl.pallas_call(pack_kernel, out_shape=(jax.ShapeDtypeStruct((PEERS, 32, 1...]
    ppermute x1, waiting for transfers between devices: 0.01 us -> 0.82 us  [on_device(): far = lax.ppermute(sums, 'c', [(0, 1), (1, 0)])]
  transfers between devices with their start and end apart: 2 -> 2, of which waited for: 1 -> 2; matrix products, arithmetic and copies ran while one was open for 0% -> 0% of each run, Pallas kernels for 0% -> 0%
where the time goes in v3:
time: 68.8 us; the launch traced here: 68.5 us
  blocking collectives  44.9 us (65%)
  Pallas kernels  14.2 us (21%)
  starting transfers between devices  5.1 us (7%)
  waiting for transfers between devices  2.36 us (3%)
  between operations  1.95 us (3%)
    all_to_all x1, blocking collectives, on_device(): own = lax.all_to_all(sent, ('xh', 'g'), 0, 0, tiled=True)  28.3 us
    all_to_all x1, blocking collectives, on_device(): got = lax.all_to_all(partial, ('xh', 'g'), 0, 0, tiled=True)  16.6 us
    pallas_call x1, Pallas kernels, on_device(): pl.pallas_call(product_kernel, out_shape=jax.ShapeDtypeStruct((PEERS, 16,...  10.1 us
    pallas_call x1, Pallas kernels, on_device(): pl.pallas_call(pack_kernel, out_shape=(jax.ShapeDtypeStruct((PEERS, 32, 1...  3.14 us
    ppermute x1, starting transfers between devices, on_device(): other = lax.ppermute(own[:, 16:], 'c', [(0, 1), (1, 0)])  2.66 us
    ppermute x1, starting transfers between devices, on_device(): far = lax.ppermute(sums, 'c', [(0, 1), (1, 0)])  2.44 us
    ppermute x1, waiting for transfers between devices, on_device(): other = lax.ppermute(own[:, 16:], 'c', [(0, 1), (1, 0)])  1.54 us
  transfers between devices with their start and end apart: 2, of which 2 were waited for; matrix products, arithmetic and copies ran while one was open for 0% of the time, Pallas kernels for 0%

profile of v3, /device:TPU:1, one launch (start us, length us, event | category | flops | bytes accessed | tf_op | source)
XLA Modules:
  0.0 68.5 jit_solution(18303297052059829464)
XLA Ops:
  1.9 3.1 %features.1 = (f32[64,32,128]{2,1,0:T(8,128)}, f32[8,128]{1,0:T(8,128)}) custom-call(bf16[256,1024]{1,0:T(8,128)(2,1)} %enc_hbm.1, bf16[1024,512]{1,0:T(8,128)(2,1)} %w1_hbm.1, bf16[32,512]{1,0:T(8,128)(2,1)} %bitcast.6, f32[1,32]{1,0:T(1,128)} %bitcast.7, f32[1,1]{1,0:T(1,128)} %bitcast.4.scale_hbm, f32[1,1]{1,0:T(1,128)} %bitcast.5.noise_hbm, ...), custom_call_target="tpu_custom_call" | custom-call | tf_op jit(solution)/shard_map/features/pallas_call | solution.py:217
  5.1 28.3 %all_to_all.10.own_ref = f32[64,32,128]{2,1,0:T(8,128)S(1)} all-to-all(f32[64,32,128]{2,1,0:T(8,128)} %get-tuple-element.4), channel_id=1, replica_groups=mesh['g'=32,'c'=2,'xh'=2] {'xh','g'}, dimensions={0} | all-to-all | bytes 2097152 | tf_op jit(solution)/shard_map/all_to_all | solution.py:246
  33.4 2.7 %collective-permute-start = (f32[64,16,128]{2,1,0:T(8,128)S(1)}, f32[64,16,128]{2,1,0:T(8,128)S(1)}, u32[]{:S(2)}, u32[]{:S(2)}) collective-permute-start(f32[64,16,128]{2,1,0:T(8,128)S(1)} %slice.8), channel_id=1, source_target_pairs={{0,2},{2,0},{1,3},{3,1},{4,6},{6,4},{5,7},{7,5},{8,10},{10,8},{9,1... | collective-permute-start | bytes 1572872 | tf_op jit(solution)/shard_map/ppermute | solution.py:247
  36.0 1.5 %collective-permute-done.other_ref = f32[64,16,128]{2,1,0:T(8,128)S(1)} collective-permute-done((f32[64,16,128]{2,1,0:T(8,128)S(1)}, f32[64,16,128]{2,1,0:T(8,128)S(1)}, u32[]{:S(2)}, u32[]{:S(2)}) %collective-permute-start) | collective-permute-done | bytes 524320 | tf_op jit(solution)/shard_map/ppermute | solution.py:247
  37.6 10.1 %kernel_product.1 = f32[64,16,128]{2,1,0:T(8,128)S(1)} custom-call(f32[64,32,128]{2,1,0:T(8,128)S(1)} %all_to_all.10.own_ref, f32[64,16,128]{2,1,0:T(8,128)S(1)} %collective-permute-done.other_ref), custom_call_target="tpu_custom_call" | custom-call | tf_op jit(solution)/shard_map/kernel_product/pallas_call | solution.py:249
  47.7 16.6 %all_to_all.11.got_ref = f32[64,16,128]{2,1,0:T(8,128)S(1)} all-to-all(f32[64,16,128]{2,1,0:T(8,128)S(1)} %kernel_product.1), channel_id=1, replica_groups=mesh['g'=32,'c'=2,'xh'=2] {'xh','g'}, dimensions={0} | all-to-all | bytes 1048576 | tf_op jit(solution)/shard_map/all_to_all | solution.py:261
  64.3 0.0 copy-start
  64.3 0.0 copy-start.1
  64.3 0.1 slice_reduce_fusion.own_ref
  64.4 2.4 %collective-permute-start.1 = (f32[8,128]{1,0:T(8,128)S(1)}, f32[8,128]{1,0:T(8,128)S(1)}, u32[]{:S(2)}, u32[]{:S(2)}) collective-permute-start(f32[8,128]{1,0:T(8,128)S(1)} %slice_reduce_fusion.own_ref), channel_id=1, source_target_pairs={{0,2},{2,0},{1,3},{3,1},{4,6},{6,4},{5,7},{7,5},{8,10},{10,8},{9,1... | collective-permute-start | bytes 12296 | tf_op jit(solution)/shard_map/ppermute | solution.py:263
  66.8 0.8 %collective-permute-done.1.other_ref = f32[8,128]{1,0:T(8,128)S(1)} collective-permute-done((f32[8,128]{1,0:T(8,128)S(1)}, f32[8,128]{1,0:T(8,128)S(1)}, u32[]{:S(2)}, u32[]{:S(2)}) %collective-permute-start.1) | collective-permute-done | bytes 4128 | tf_op jit(solution)/shard_map/ppermute | solution.py:263
  67.6 0.0 copy-done
  67.6 0.0 copy-done.1
  67.6 0.9 %update.1 = (f32[16,512]{1,0:T(8,128)}, f32[16,512]{1,0:T(8,128)}) custom-call(f32[64,16,128]{2,1,0:T(8,128)S(1)} %all_to_all.11.got_ref, f32[8,128]{1,0:T(8,128)S(1)} %slice_reduce_fusion.own_ref, f32[8,128]{1,0:T(8,128)S(1)} %collective-permute-done.1.other_ref, f32[16,512]{1,0:T(8,128)S(1)} %copy-done, f32[8,128]{1,0:T(8,128)S(1)} %copy-done.1), custom_call_target="tpu_custom_call" | custom-call | tf_op jit(solution)/shard_map/update/pallas_call | solution.py:264
  (1 shorter events, 0.0 us)
Async XLA Ops:
  33.4 4.2 %collective-permute-start = (f32[64,16,128]{2,1,0:T(8,128)S(1)}, f32[64,16,128]{2,1,0:T(8,128)S(1)}, u32[]{:S(2)}, u32[]{:S(2)}) collective-permute-start(f32[64,16,128]{2,1,0:T(8,128)S(1)} %slice.8), channel_id=1, source_target_pairs={{0,2},{2,0},{1,3},{3,1},{4,6},{6,4},{5,7},{7,5},{8,10},{10,8},{9,1... | collective-permute-start | bytes 1572872 | tf_op jit(solution)/shard_map/ppermute | solution.py:247
  64.3 3.3 %copy-start = (f32[16,512]{1,0:T(8,128)S(1)}, f32[16,512]{1,0:T(8,128)}, u32[]{:S(2)}) copy-start(f32[16,512]{1,0:T(8,128)} %rhs_ref.1) | copy-start | bytes 98308
  64.3 3.3 %copy-start.1 = (f32[8,128]{1,0:T(8,128)S(1)}, f32[8,128]{1,0:T(8,128)}, u32[]{:S(2)}) copy-start(f32[8,128]{1,0:T(8,128)} %get-tuple-element.5.pair_ref) | copy-start | bytes 12292
  64.4 3.3 %collective-permute-start.1 = (f32[8,128]{1,0:T(8,128)S(1)}, f32[8,128]{1,0:T(8,128)S(1)}, u32[]{:S(2)}, u32[]{:S(2)}) collective-permute-start(f32[8,128]{1,0:T(8,128)S(1)} %slice_reduce_fusion.own_ref), channel_id=1, source_target_pairs={{0,2},{2,0},{1,3},{3,1},{4,6},{6,4},{5,7},{7,5},{8,10},{10,8},{9,1... | collective-permute-start | bytes 12296 | tf_op jit(solution)/shard_map/ppermute | solution.py:263

commit v4 on v3

--- a/solution.py
+++ b/solution.py
@@ -24,9 +24,8 @@
 
 
 def pack_kernel(
-    enc_hbm, w1_hbm, w2_hbm, inv_hbm, scale_hbm, noise_hbm, rhs_hbm,
-    out_ref, pair_ref,
-    enc_ref, w1_ref, w2_ref, inv_ref, scale_ref, noise_ref, rhs_ref, set_ref, big_sem, sem,
+    enc_hbm, w1_hbm, w2_hbm, inv_hbm, rhs_hbm, out_ref,
+    enc_ref, w1_ref, w2_ref, inv_ref, rhs_ref, set_ref, big_sem, sem,
 ):
     small = [
         pltpu.make_async_copy(src, dst, sem.at[n])
@@ -35,8 +34,6 @@
                 (w2_hbm, w2_ref),
                 (inv_hbm, inv_ref),
                 (rhs_hbm, rhs_ref),
-                (scale_hbm, scale_ref),
-                (noise_hbm, noise_ref),
             )
         )
     ]
@@ -64,8 +61,6 @@
     hidden = jnp.maximum(hidden, 0.0).astype(BF16)
     for copy in small:
         copy.wait()
-    pair_ref[:4] = jnp.broadcast_to(scale_ref[...], (4, 128))
-    pair_ref[4:] = jnp.broadcast_to(noise_ref[...], (4, 128))
     features = lax.dot_general(
         w2_ref[...], hidden, (((1,), (1,)), ((), ())), preferred_element_type=F32
     )
@@ -185,8 +180,8 @@
         out_ref[CHIPS * xh : CHIPS * (xh + 1), 8:] = jnp.broadcast_to(sums, (CHIPS, 8, 128))
 
 
-def finish_kernel(got_ref, own_ref, other_ref, rhs_ref, pair_ref, sol_ref, res_ref):
-    scale, noise = pair_ref[0:1, 0:1], pair_ref[4:5, 0:1]
+def finish_kernel(got_ref, own_ref, other_ref, rhs_ref, scale_ref, noise_ref, sol_ref, res_ref):
+    scale, noise = scale_ref[...], noise_ref[...]
     sums = own_ref[...] + other_ref[...]
     product = jnp.concatenate([sums[:, 0:1], sums[:, 1:2]], axis=0)
     square = jnp.concatenate([sums[:, 2:3], sums[:, 3:4]], axis=0)
@@ -214,24 +209,19 @@
 
 def on_device(encodings, first_weight, second_weight, inv_scale, outputscale, noise, rhs):
     hbm, vmem = pl.BlockSpec(memory_space=pltpu.HBM), pl.BlockSpec(memory_space=pltpu.VMEM)
-    sent, pair = pl.pallas_call(
+    sent = pl.pallas_call(
         pack_kernel,
-        out_shape=(
-            jax.ShapeDtypeStruct((PEERS, 32, 128), F32),
-            jax.ShapeDtypeStruct((8, 128), F32),
-        ),
-        in_specs=[hbm] * 7,
+        out_shape=jax.ShapeDtypeStruct((PEERS, 32, 128), F32),
+        in_specs=[hbm] * 5,
         scratch_shapes=[
             pltpu.VMEM(encodings.shape, BF16),
             pltpu.VMEM(first_weight.shape, BF16),
             pltpu.VMEM(second_weight.shape[::-1], BF16),
             pltpu.VMEM((1, inv_scale.size), F32),
-            pltpu.VMEM((1, 1), F32),
-            pltpu.VMEM((1, 1), F32),
             pltpu.VMEM(rhs.shape, F32),
             pltpu.VMEM((P_SETS, 16, 128), F32),
             pltpu.SemaphoreType.DMA((2 * STEPS,)),
-            pltpu.SemaphoreType.DMA((5,)),
+            pltpu.SemaphoreType.DMA((3,)),
         ],
         name="features",
     )(
@@ -239,8 +229,6 @@
         first_weight,
         second_weight.T,
         inv_scale.reshape(1, -1),
-        outputscale.reshape(1, 1),
-        noise.reshape(1, 1),
         rhs,
     )
     own = lax.all_to_all(sent, ("xh", "g"), 0, 0, tiled=True)
@@ -264,10 +252,10 @@
     return pl.pallas_call(
         finish_kernel,
         out_shape=(jax.ShapeDtypeStruct(rhs.shape, F32),) * 2,
-        in_specs=[vmem] * 5,
+        in_specs=[vmem] * 6,
         compiler_params=pltpu.CompilerParams(vmem_limit_bytes=8 << 20),
         name="update",
-    )(got, sums, far, rhs, pair)
+    )(got, sums, far, rhs, outputscale.reshape(1, 1), noise.reshape(1, 1))
 
 
 def solution(mesh):

time: 68.8 us -> 68 us (0.988)
  waiting for transfers between devices: 2.36 us -> 1.54 us
    ppermute x1, waiting for transfers between devices: 0.82 us -> 0.01 us  [on_device(): far = lax.ppermute(sums, 'c', [(0, 1), (1, 0)])]
  transfers between devices with their start and end apart: 2 -> 2, of which waited for: 2 -> 1; matrix products, arithmetic and copies ran while one was open for 0% -> 0% of each run, Pallas kernels for 0% -> 0%
where the time goes in v4:
time: 68 us; the launch traced here: 67.7 us
  blocking collectives  44.9 us (66%)
  Pallas kernels  14.1 us (21%)
  starting transfers between devices  5.1 us (7%)
  between operations  1.97 us (3%)
  waiting for transfers between devices  1.54 us (2%)
    all_to_all x1, blocking collectives, on_device(): own = lax.all_to_all(sent, ('xh', 'g'), 0, 0, tiled=True)  28.3 us
    all_to_all x1, blocking collectives, on_device(): got = lax.all_to_all(partial, ('xh', 'g'), 0, 0, tiled=True)  16.6 us
    pallas_call x1, Pallas kernels, on_device(): pl.pallas_call(product_kernel, out_shape=jax.ShapeDtypeStruct((PEERS, 16,...  10.1 us
    pallas_call x1, Pallas kernels, on_device(): pl.pallas_call(pack_kernel, out_shape=jax.ShapeDtypeStruct((PEERS, 32, 12...  3.11 us
    ppermute x1, starting transfers between devices, on_device(): other = lax.ppermute(own[:, 16:], 'c', [(0, 1), (1, 0)])  2.65 us
    ppermute x1, starting transfers between devices, on_device(): far = lax.ppermute(sums, 'c', [(0, 1), (1, 0)])  2.44 us
    ppermute x1, waiting for transfers between devices, on_device(): other = lax.ppermute(own[:, 16:], 'c', [(0, 1), (1, 0)])  1.54 us
  transfers between devices with their start and end apart: 2, of which 1 were waited for; matrix products, arithmetic and copies ran while one was open for 0% of the time, Pallas kernels for 0%

profile of v4, /device:TPU:1, one launch (start us, length us, event | category | flops | bytes accessed | tf_op | source)
XLA Modules:
  0.0 67.7 jit_solution(17554547095750241487)
XLA Ops:
  0.6 3.1 %features.1 = f32[64,32,128]{2,1,0:T(8,128)} custom-call(bf16[256,1024]{1,0:T(8,128)(2,1)} %enc_hbm.1, bf16[1024,512]{1,0:T(8,128)(2,1)} %w1_hbm.1, bf16[32,512]{1,0:T(8,128)(2,1)} %bitcast.6, f32[1,32]{1,0:T(1,128)} %bitcast.7, f32[16,512]{1,0:T(8,128)} %rhs_ref.1), custom_call_target="tpu_custom_call" | custom-call | tf_op jit(solution)/shard_map/features/pallas_call | solution.py:212
  3.7 28.3 %all_to_all.10.own_ref = f32[64,32,128]{2,1,0:T(8,128)S(1)} all-to-all(f32[64,32,128]{2,1,0:T(8,128)} %features.1), channel_id=1, replica_groups=mesh['g'=32,'c'=2,'xh'=2] {'xh','g'}, dimensions={0} | all-to-all | bytes 2097152 | tf_op jit(solution)/shard_map/all_to_all | solution.py:234
  32.0 2.7 %collective-permute-start = (f32[64,16,128]{2,1,0:T(8,128)S(1)}, f32[64,16,128]{2,1,0:T(8,128)S(1)}, u32[]{:S(2)}, u32[]{:S(2)}) collective-permute-start(f32[64,16,128]{2,1,0:T(8,128)S(1)} %slice.8), channel_id=1, source_target_pairs={{0,2},{2,0},{1,3},{3,1},{4,6},{6,4},{5,7},{7,5},{8,10},{10,8},{9,1... | collective-permute-start | bytes 1572872 | tf_op jit(solution)/shard_map/ppermute | solution.py:235
  34.7 1.5 %collective-permute-done.other_ref = f32[64,16,128]{2,1,0:T(8,128)S(1)} collective-permute-done((f32[64,16,128]{2,1,0:T(8,128)S(1)}, f32[64,16,128]{2,1,0:T(8,128)S(1)}, u32[]{:S(2)}, u32[]{:S(2)}) %collective-permute-start) | collective-permute-done | bytes 524320 | tf_op jit(solution)/shard_map/ppermute | solution.py:235
  36.2 10.1 %kernel_product.1 = f32[64,16,128]{2,1,0:T(8,128)S(1)} custom-call(f32[64,32,128]{2,1,0:T(8,128)S(1)} %all_to_all.10.own_ref, f32[64,16,128]{2,1,0:T(8,128)S(1)} %collective-permute-done.other_ref), custom_call_target="tpu_custom_call" | custom-call | tf_op jit(solution)/shard_map/kernel_product/pallas_call | solution.py:237
  46.4 16.6 %all_to_all.11.got_ref = f32[64,16,128]{2,1,0:T(8,128)S(1)} all-to-all(f32[64,16,128]{2,1,0:T(8,128)S(1)} %kernel_product.1), channel_id=1, replica_groups=mesh['g'=32,'c'=2,'xh'=2] {'xh','g'}, dimensions={0} | all-to-all | bytes 1048576 | tf_op jit(solution)/shard_map/all_to_all | solution.py:249
  63.0 0.0 copy-start
  63.0 0.1 slice_reduce_fusion.own_ref
  63.0 2.4 %collective-permute-start.1 = (f32[8,128]{1,0:T(8,128)S(1)}, f32[8,128]{1,0:T(8,128)S(1)}, u32[]{:S(2)}, u32[]{:S(2)}) collective-permute-start(f32[8,128]{1,0:T(8,128)S(1)} %slice_reduce_fusion.own_ref), channel_id=1, source_target_pairs={{0,2},{2,0},{1,3},{3,1},{4,6},{6,4},{5,7},{7,5},{8,10},{10,8},{9,1... | collective-permute-start | bytes 12296 | tf_op jit(solution)/shard_map/ppermute | solution.py:251
  66.8 0.0 collective-permute-done.1.other_ref
  66.8 0.0 copy-done
  66.8 0.9 %update.1 = (f32[16,512]{1,0:T(8,128)}, f32[16,512]{1,0:T(8,128)}) custom-call(f32[64,16,128]{2,1,0:T(8,128)S(1)} %all_to_all.11.got_ref, f32[8,128]{1,0:T(8,128)S(1)} %slice_reduce_fusion.own_ref, f32[8,128]{1,0:T(8,128)S(1)} %collective-permute-done.1.other_ref, f32[16,512]{1,0:T(8,128)S(1)} %copy-done, f32[1,1]{1,0:T(1,128)} %bitcast.4.scale_ref, ...), custom_call_target="tpu_custom_call" | custom-call | tf_op jit(solution)/shard_map/update/pallas_call | solution.py:252
  (1 shorter events, 0.0 us)
Async XLA Ops:
  32.0 4.2 %collective-permute-start = (f32[64,16,128]{2,1,0:T(8,128)S(1)}, f32[64,16,128]{2,1,0:T(8,128)S(1)}, u32[]{:S(2)}, u32[]{:S(2)}) collective-permute-start(f32[64,16,128]{2,1,0:T(8,128)S(1)} %slice.8), channel_id=1, source_target_pairs={{0,2},{2,0},{1,3},{3,1},{4,6},{6,4},{5,7},{7,5},{8,10},{10,8},{9,1... | collective-permute-start | bytes 1572872 | tf_op jit(solution)/shard_map/ppermute | solution.py:235
  63.0 3.8 %copy-start = (f32[16,512]{1,0:T(8,128)S(1)}, f32[16,512]{1,0:T(8,128)}, u32[]{:S(2)}) copy-start(f32[16,512]{1,0:T(8,128)} %rhs_ref.1) | copy-start | bytes 98308
  63.0 3.7 %collective-permute-start.1 = (f32[8,128]{1,0:T(8,128)S(1)}, f32[8,128]{1,0:T(8,128)S(1)}, u32[]{:S(2)}, u32[]{:S(2)}) collective-permute-start(f32[8,128]{1,0:T(8,128)S(1)} %slice_reduce_fusion.own_ref), channel_id=1, source_target_pairs={{0,2},{2,0},{1,3},{3,1},{4,6},{6,4},{5,7},{7,5},{8,10},{10,8},{9,1... | collective-permute-start | bytes 12296 | tf_op jit(solution)/shard_map/ppermute | solution.py:251

commit v5 on v4

v5 whole, which is shorter than its diff:
```python
import jax
import jax.numpy as jnp
from jax import lax
from jax.experimental import pallas as pl
from jax.experimental.pallas import tpu as pltpu
from jax.sharding import Mesh
from jax.sharding import PartitionSpec as P

F32, BF16 = jnp.float32, jnp.bfloat16
ROOT_LOG2E = 1.2011224087864498
CHIPS = 32
PEERS = 64
GROUPS = 8
WIDTH = 32
DEPTH = 256
STEPS = 4
ROWS = 256
PAIRS = [(a, b, t) for a in range(GROUPS) for b in range(a + 1, GROUPS) for t in range(2)]
TILES = CHIPS // 2
HALF = TILES * 128 // 2


def halves(x):
    high = x.astype(BF16)
    return high, (x - high.astype(F32)).astype(BF16)


def pack_kernel(
    enc_hbm, w1_hbm, w2_hbm, inv_hbm, rhs_hbm, out_ref,
    enc_ref, w1_ref, w2_ref, inv_ref, rhs_ref, set_ref, part_ref, big_sem, sem,
):
    small = [
        pltpu.make_async_copy(src, dst, sem.at[n])
        for n, (src, dst) in enumerate(
            ((w2_hbm, w2_ref), (inv_hbm, inv_ref), (rhs_hbm, rhs_ref))
        )
    ]
    depth = enc_hbm.shape[1] // STEPS
    big = []
    for n in range(STEPS):
        at = pl.ds(n * depth, depth)
        big.append(
            (
                pltpu.make_async_copy(enc_hbm.at[:, at], enc_ref.at[:, at], big_sem.at[2 * n]),
                pltpu.make_async_copy(w1_hbm.at[at], w1_ref.at[at], big_sem.at[2 * n + 1]),
            )
        )
    for pair in big:
        for copy in pair:
            copy.start()
    for copy in small:
        copy.start()
    hidden = jnp.zeros((enc_hbm.shape[0], w1_hbm.shape[1]), F32)
    for n in range(STEPS):
        at = slice(n * depth, (n + 1) * depth)
        for copy in big[n]:
            copy.wait()
        hidden = hidden + jnp.dot(enc_ref[:, at], w1_ref[at], preferred_element_type=F32)
    hidden = jnp.maximum(hidden, 0.0).astype(BF16)
    for copy in small:
        copy.wait()
    features = lax.dot_general(
        w2_ref[...], hidden, (((1,), (1,)), ((), ())), preferred_element_type=F32
    )
    n = features.shape[0]
    diagonal = lax.broadcasted_iota(jnp.int32, (n, n), 0) == lax.broadcasted_iota(
        jnp.int32, (n, n), 1
    )
    inv = jnp.sum(
        jnp.where(diagonal, jnp.broadcast_to(inv_ref[...], (n, n)), 0.0), axis=1, keepdims=True
    )
    features = features * inv * ROOT_LOG2E
    late = rhs_ref.shape[1] // 2
    for a in range(GROUPS):
        lo = WIDTH * a
        at, after = slice(lo, lo + WIDTH), slice(late + lo, late + lo + WIDTH)
        set_ref[a] = jnp.concatenate(
            [features[:16, at], features[16:, at], rhs_ref[:, at], rhs_ref[:, after]], axis=1
        )
        for t in range(2):
            lo = WIDTH * a + 16 * t
            at, after = slice(lo, lo + 16), slice(late + lo, late + lo + 16)
            part_ref[2 * a + t] = jnp.concatenate(
                [features[8 * m : 8 * m + 8, at] for m in range(4)]
                + [rhs_ref[8 * m : 8 * m + 8, s] for m in range(2) for s in (at, after)],
                axis=1,
            )
    for k, (a, b, t) in enumerate(PAIRS):
        out_ref[k, :16] = set_ref[a]
        out_ref[k, 16:] = part_ref[2 * b + t]
    for a in range(GROUPS):
        out_ref[len(PAIRS) + a, :8] = jnp.zeros((8, 128), F32)
        out_ref[len(PAIRS) + a, 8:] = set_ref[a]


def points_of(ref, k, lo):
    a0, a1 = ref[2 * k, lo : lo + 16], ref[2 * k + 1, lo : lo + 16]
    b0, b1 = ref[CHIPS + 2 * k, lo : lo + 16], ref[CHIPS + 2 * k + 1, lo : lo + 16]
    four = (a0, b0, a1, b1)
    features = jnp.concatenate(
        [
            jnp.concatenate([x[:, :32] for x in four], axis=1),
            jnp.concatenate([x[:, 32:64] for x in four], axis=1),
        ],
        axis=0,
    )
    columns = jnp.concatenate(
        [
            jnp.concatenate([a0[:, 64:], a1[:, 64:]], axis=1),
            jnp.concatenate([b0[:, 64:], b1[:, 64:]], axis=1),
        ],
        axis=0,
    )
    return features, columns


def half_points_of(ref, k, lo):
    units = [[ref[CHIPS * xh + 4 * k + j, lo : lo + 8] for xh in range(2)] for j in range(4)]
    features = jnp.concatenate(
        [
            jnp.concatenate([u[:, 16 * m : 16 * m + 16] for pair in units for u in pair], axis=1)
            for m in range(4)
        ],
        axis=0,
    )
    columns = jnp.concatenate(
        [
            jnp.concatenate([pair[xh][:, s : s + 32] for pair in units], axis=1)
            for xh in range(2)
            for s in (64, 96)
        ],
        axis=0,
    )
    return features, columns


def operand(features, left):
    y1, y2 = halves(features)
    kept = y1.astype(F32) + y2.astype(F32)
    norm = -0.5 * jnp.sum(kept * kept, axis=0, keepdims=True)
    n1 = norm.astype(BF16).astype(F32)
    n2 = (norm - n1).astype(BF16).astype(F32)
    n3 = norm - n1 - n2
    row = lax.broadcasted_iota(jnp.int32, (16, features.shape[1]), 0)
    own, other = (3, 0) if left else (0, 3)
    tail = jnp.where(
        row == own,
        n1,
        jnp.where(
            row == own + 1,
            n2,
            jnp.where(
                row == own + 2, n3, jnp.where((row >= other) & (row < other + 3), 1.0, 0.0)
            ),
        ),
    ).astype(BF16)
    blank = jnp.zeros((DEPTH - 144, features.shape[1]), BF16)
    parts = [y1, y1, y2, y2] if left else [y1, y2, y1, y2]
    return jnp.concatenate(parts + [tail, blank], axis=0)


def product_kernel(
    own_ref, other_ref, out_ref, low_ref, far_ref,
    left_ref, right_ref, vec_ref, rows_ref, flat_ref, col_ref,
):
    on_pair = lax.axis_index("xh") * CHIPS + lax.axis_index("g") < len(PAIRS)
    lane = lax.broadcasted_iota(jnp.int32, (8, 128), 1)

    def set_rows(lo, flat):
        for k in range(TILES):
            features, columns = points_of(own_ref, k, lo)
            at = slice(k * 128, (k + 1) * 128)
            left_ref[at, :] = operand(features, True).T
            rows_ref[k] = columns
            if flat:
                flat_ref[:, at] = jnp.concatenate(halves(columns), axis=0)

    def set_columns(n, points):
        features, columns = points
        at = slice(n * 128, (n + 1) * 128)
        right_ref[:, at] = operand(features, False)
        vec_ref[at, :] = jnp.concatenate(halves(columns), axis=0).T

    def multiply(width, both_ways):
        product = jnp.zeros((32, 128), F32)
        square = jnp.zeros((32, 128), F32)
        for r in range(left_ref.shape[0] // ROWS):
            strip = slice(ROWS * r, ROWS * (r + 1))
            exponent = jnp.dot(
                left_ref[strip, :], right_ref[:, :width], preferred_element_type=F32
            )
            tile = jnp.exp2(exponent).astype(BF16)
            total = jnp.dot(tile, vec_ref[:width, :], preferred_element_type=F32)
            if both_ways:
                back = jnp.dot(flat_ref[:, strip], tile, preferred_element_type=F32)
                col_ref[...] = back if r == 0 else col_ref[...] + back
            for k in range(ROWS // 128 * r, ROWS // 128 * (r + 1)):
                lo = 128 * k - ROWS * r
                pair = total[lo : lo + 128].T
                image = pair[:32] + pair[32:]
                rows = rows_ref[k]
                product = product + rows * image
                if not both_ways:
                    square = square + rows * rows
                for xh in range(2):
                    top, low = image[16 * xh : 16 * xh + 8], image[16 * xh + 8 : 16 * xh + 16]
                    for chip in range(2):
                        at = slice(64 * chip, 64 * (chip + 1))
                        out_ref[CHIPS * xh + 2 * k + chip] = jnp.concatenate(
                            [top[:, at], low[:, at]], axis=1
                        )
        product = jnp.sum(product, axis=1, keepdims=True) * (2.0 if both_ways else 1.0)
        square = jnp.sum(square, axis=1, keepdims=True)
        sums = []
        for xh in range(2):
            here = jnp.zeros((8, 128), F32)
            for n, x in enumerate((product, square)):
                for a in range(2):
                    lo = 16 * xh + 8 * a
                    here = jnp.where(lane == 64 + 2 * n + a, x[lo : lo + 8], here)
            sums.append(here)
        return sums

    @pl.when(on_pair)
    def _():
        set_rows(0, True)
        for n in range(TILES // 2):
            set_columns(n, half_points_of(own_ref, n, 16))
        for n in range(TILES // 2):
            set_columns(TILES // 2 + n, half_points_of(other_ref, n, 8))
        sums = multiply(2 * HALF, True)
        for n in range(TILES):
            at = slice(n * 128, (n + 1) * 128)
            image = col_ref[:32, at] + col_ref[32:, at]
            k = n % (TILES // 2)
            for xh in range(2):
                for j in range(4):
                    at = slice(32 * j, 32 * j + 32)
                    part = jnp.concatenate(
                        [image[16 * xh : 16 * xh + 8, at], image[16 * xh + 8 : 16 * xh + 16, at]]
                        + [sums[xh][:, 64:]],
                        axis=1,
                    )
                    if n < TILES // 2:
                        low_ref[CHIPS * xh + 4 * k + j] = part
                    else:
                        far_ref[CHIPS * xh + 4 * k + j] = part

    @pl.when(jnp.logical_not(on_pair))
    def _():
        set_rows(8, False)
        for n in range(TILES):
            set_columns(n, points_of(own_ref, n, 8))
        for n in range(TILES):
            set_columns(TILES + n, points_of(other_ref, n, 0))
        sums = multiply(4 * HALF, False)
        for xh in range(2):
            at = slice(CHIPS * xh, CHIPS * (xh + 1))
            low_ref[at] = jnp.broadcast_to(sums[xh], (CHIPS, 8, 128))
            far_ref[at] = jnp.broadcast_to(sums[xh], (CHIPS, 8, 128))


def join_kernel(whole_ref, low_ref, near_ref, out_ref):
    out_ref[:, :8] = whole_ref[...]
    out_ref[:, 8:] = low_ref[...] + near_ref[...]


def finish_kernel(got_ref, rhs_ref, pair_ref, sol_ref, res_ref):
    scale, noise = pair_ref[0:1, 0:1], pair_ref[4:5, 0:1]
    whole = [None] * GROUPS
    part = [None] * (2 * GROUPS)
    sums = got_ref[len(PAIRS), 8:]

    def plus(x, y):
        return y if x is None else x + y

    for k, (a, b, t) in enumerate(PAIRS):
        low = got_ref[k, 8:]
        whole[a] = plus(whole[a], got_ref[k, :8])
        part[2 * b + t] = plus(part[2 * b + t], low)
        sums = sums + low
    for a in range(GROUPS):
        whole[a] = plus(whole[a], got_ref[len(PAIRS) + a, :8])
        if a:
            sums = sums + got_ref[len(PAIRS) + a, 8:]
    product = jnp.concatenate([sums[:, 64:65], sums[:, 65:66]], axis=0)
    square = jnp.concatenate([sums[:, 66:67], sums[:, 67:68]], axis=0)
    step = square / (scale * product + noise * square)
    image = jnp.concatenate(
        [
            jnp.concatenate(
                [
                    x[:, 64 * m + 32 * h : 64 * m + 32 * h + 32]
                    for h in range(2)
                    for x in whole
                ],
                axis=1,
            )
            for m in range(2)
        ],
        axis=0,
    )
    blank = jnp.zeros((8, 16), F32)
    image = image + jnp.concatenate(
        [
            jnp.concatenate(
                [
                    blank if x is None else x[:, 32 * m + 16 * h : 32 * m + 16 * h + 16]
                    for h in range(2)
                    for x in part
                ],
                axis=1,
            )
            for m in range(2)
        ],
        axis=0,
    )
    direction = rhs_ref[...]
    sol_ref[...] = step * direction
    res_ref[...] = direction - step * (scale * image + noise * direction)


def on_device(encodings, first_weight, second_weight, inv_scale, outputscale, noise, rhs):
    hbm, vmem = pl.BlockSpec(memory_space=pltpu.HBM), pl.BlockSpec(memory_space=pltpu.VMEM)
    swap = [(0, 1), (1, 0)]
    sent = pl.pallas_call(
        pack_kernel,
        out_shape=jax.ShapeDtypeStruct((PEERS, 24, 128), F32),
        in_specs=[hbm] * 5,
        scratch_shapes=[
            pltpu.VMEM(encodings.shape, BF16),
            pltpu.VMEM(first_weight.shape, BF16),
            pltpu.VMEM(second_weight.shape[::-1], BF16),
            pltpu.VMEM((1, inv_scale.size), F32),
            pltpu.VMEM(rhs.shape, F32),
            pltpu.VMEM((GROUPS, 16, 128), F32),
            pltpu.VMEM((2 * GROUPS, 8, 128), F32),
            pltpu.SemaphoreType.DMA((2 * STEPS,)),
            pltpu.SemaphoreType.DMA((3,)),
        ],
        name="features",
    )(encodings, first_weight, second_weight.T, inv_scale.reshape(1, -1), rhs)
    own = lax.all_to_all(sent, ("xh", "g"), 0, 0, tiled=True)
    other = lax.ppermute(own[:, 8:], "c", swap)
    whole, low, far = pl.pallas_call(
        product_kernel,
        out_shape=(jax.ShapeDtypeStruct((PEERS, 8, 128), F32),) * 3,
        scratch_shapes=[
            pltpu.VMEM((2 * HALF, DEPTH), BF16),
            pltpu.VMEM((DEPTH, 4 * HALF), BF16),
            pltpu.VMEM((4 * HALF, 64), BF16),
            pltpu.VMEM((TILES, 32, 128), F32),
            pltpu.VMEM((64, 2 * HALF), BF16),
            pltpu.VMEM((64, 2 * HALF), F32),
        ],
        compiler_params=pltpu.CompilerParams(vmem_limit_bytes=32 << 20),
        name="kernel_product",
    )(own, other)
    near = lax.ppermute(far, "c", swap)
    partial = pl.pallas_call(
        join_kernel,
        out_shape=jax.ShapeDtypeStruct((PEERS, 16, 128), F32),
        in_specs=[vmem] * 3,
        compiler_params=pltpu.CompilerParams(vmem_limit_bytes=8 << 20),
        name="join",
    )(whole, low, near)
    got = lax.all_to_all(partial, ("xh", "g"), 0, 0, tiled=True)
    row = lax.broadcasted_iota(jnp.int32, (8, 128), 0)
    pair = jnp.where(row < 4, outputscale[0], noise[0])
    return pl.pallas_call(
        finish_kernel,
        out_shape=(jax.ShapeDtypeStruct(rhs.shape, F32),) * 2,
        in_specs=[vmem] * 3,
        compiler_params=pltpu.CompilerParams(vmem_limit_bytes=8 << 20),
        name="update",
    )(got, rhs, pair)


def solution(mesh):
    split = Mesh(mesh.devices.reshape(CHIPS, 2, 2), ("g", "c", "xh"))
    vectors = P("xh", ("g", "c"))
    return jax.shard_map(
        on_device,
        mesh=split,
        in_specs=(P(("g", "c", "xh"), None), P(), P(), P(), P(), P(), vectors),
        out_specs=(vectors, vectors),
        check_vma=False,
    )
```

time: 68 us -> 65.3 us (0.960)
  the two profiles are of different devices: /device:TPU:1 before, /device:TPU:0 now
where the time goes in v5:
time: 65.3 us; the launch traced here: 64.9 us
  blocking collectives  26.9 us (41%)
  waiting for transfers between devices  15.1 us (23%)
  Pallas kernels  12.3 us (19%)
  starting transfers between devices  8.55 us (13%)
  between operations  1.98 us (3%)
    all_to_all x1, blocking collectives, on_device(): own = lax.all_to_all(sent, ('xh', 'g'), 0, 0, tiled=True)  26.9 us
    all_to_all x1, waiting for transfers between devices, on_device(): got = lax.all_to_all(partial, ('xh', 'g'), 0, 0, tiled=True)  11.8 us
    all_to_all x1, starting transfers between devices, on_device(): got = lax.all_to_all(partial, ('xh', 'g'), 0, 0, tiled=True)  8.24 us
    pallas_call x1, Pallas kernels, on_device(): pl.pallas_call(product_kernel, out_shape=(jax.ShapeDtypeStruct((PEERS, 8,...  7.45 us
    pallas_call x1, Pallas kernels, on_device(): pl.pallas_call(pack_kernel, out_shape=jax.ShapeDtypeStruct((PEERS, 24, 12...  3.01 us
    ppermute x1, waiting for transfers between devices, on_device(): other = lax.ppermute(own[:, 8:], 'c', swap)  1.9 us
    ppermute x1, waiting for transfers between devices, on_device(): near = lax.ppermute(far, 'c', swap)  1.39 us
  transfers between devices with their start and end apart: 3, of which 3 were waited for; matrix products, arithmetic and copies ran while one was open for 0% of the time, Pallas kernels for 0%

profile of v5, /device:TPU:0, one launch (start us, length us, event | category | flops | bytes accessed | tf_op | source)
XLA Modules:
  0.0 64.9 jit_solution(14996620776504887778)
XLA Ops:
  0.6 3.0 %features.1 = f32[64,24,128]{2,1,0:T(8,128)} custom-call(bf16[256,1024]{1,0:T(8,128)(2,1)} %enc_hbm.1, bf16[1024,512]{1,0:T(8,128)(2,1)} %w1_hbm.1, bf16[32,512]{1,0:T(8,128)(2,1)} %bitcast.6, f32[1,32]{1,0:T(1,128)} %bitcast.7, f32[16,512]{1,0:T(8,128)} %rhs_ref.1), custom_call_target="tpu_custom_call" | custom-call | tf_op jit(solution)/shard_map/features/pallas_call | solution.py:326
  3.6 26.9 %all_to_all.10.own_ref = f32[64,24,128]{2,1,0:T(8,128)S(1)} all-to-all(f32[64,24,128]{2,1,0:T(8,128)} %features.1), channel_id=1, replica_groups=mesh['g'=32,'c'=2,'xh'=2] {'xh','g'}, dimensions={0} | all-to-all | bytes 1572864 | tf_op jit(solution)/shard_map/all_to_all | solution.py:343
  30.5 0.1 collective-permute-start
  30.6 1.9 %collective-permute-done.other_ref = f32[64,16,128]{2,1,0:T(8,128)S(1)} collective-permute-done((f32[64,16,128]{2,1,0:T(8,128)S(1)}, f32[64,16,128]{2,1,0:T(8,128)S(1)}, u32[]{:S(2)}, u32[]{:S(2)}) %collective-permute-start) | collective-permute-done | bytes 524320 | tf_op jit(solution)/shard_map/ppermute | solution.py:344
  32.5 7.5 %kernel_product.1 = (f32[64,8,128]{2,1,0:T(8,128)S(1)}, f32[64,8,128]{2,1,0:T(8,128)S(1)}, f32[64,8,128]{2,1,0:T(8,128)S(1)}) custom-call(f32[64,24,128]{2,1,0:T(8,128)S(1)} %all_to_all.10.own_ref, f32[64,16,128]{2,1,0:T(8,128)S(1)} %collective-permute-done.other_ref), custom_call_target="tpu_custom_call" | custom-call | tf_op jit(solution)/shard_map/kernel_product/pallas_call | solution.py:345
  40.0 0.2 collective-permute-start.1
  40.2 1.4 %collective-permute-done.1.near_ref = f32[64,8,128]{2,1,0:T(8,128)S(1)} collective-permute-done((f32[64,8,128]{2,1,0:T(8,128)S(1)}, f32[64,8,128]{2,1,0:T(8,128)S(1)}, u32[]{:S(2)}, u32[]{:S(2)}) %collective-permute-start.1) | collective-permute-done | bytes 262176 | tf_op jit(solution)/shard_map/ppermute | solution.py:359
  41.6 0.8 %join.1 = f32[64,16,128]{2,1,0:T(8,128)} custom-call(f32[64,8,128]{2,1,0:T(8,128)S(1)} %get-tuple-element.5.whole_ref, f32[64,8,128]{2,1,0:T(8,128)S(1)} %get-tuple-element.6.low_ref, f32[64,8,128]{2,1,0:T(8,128)S(1)} %collective-permute-done.1.near_ref), custom_call_target="tpu_custom_call" | custom-call | tf_op jit(solution)/shard_map/join/pallas_call | solution.py:360
  42.5 0.0 copy-start
  42.5 8.2 %all-to-all-start.1 = ((f32[64,16,128]{2,1,0:T(8,128)}), f32[64,16,128]{2,1,0:T(8,128)S(1)}, u32[]{:S(2)}, u32[]{:S(2)}) async-start(f32[64,16,128]{2,1,0:T(8,128)} %join.1), calls=%async_computation.1 | async-start | bytes 1048576 | tf_op jit(solution)/shard_map/all_to_all | solution.py:367
  52.0 11.8 %all-to-all-done.1.got_ref = f32[64,16,128]{2,1,0:T(8,128)S(1)} async-done(((f32[64,16,128]{2,1,0:T(8,128)}), f32[64,16,128]{2,1,0:T(8,128)S(1)}, u32[]{:S(2)}, u32[]{:S(2)}) %all-to-all-start.1) | async-done | bytes 524320 | tf_op jit(solution)/shard_map/all_to_all | solution.py:367
  63.9 0.1 iota.7.pair_ref
  63.9 0.0 copy-done
  63.9 1.0 %update.1 = (f32[16,512]{1,0:T(8,128)}, f32[16,512]{1,0:T(8,128)}) custom-call(f32[64,16,128]{2,1,0:T(8,128)S(1)} %all-to-all-done.1.got_ref, f32[16,512]{1,0:T(8,128)S(1)} %copy-done, f32[8,128]{1,0:T(8,128)S(1)} %iota.7.pair_ref), custom_call_target="tpu_custom_call" | custom-call | tf_op jit(solution)/shard_map/update/pallas_call | solution.py:370
  (2 shorter events, 0.0 us)
Async XLA Ops:
  30.5 2.0 %collective-permute-start = (f32[64,16,128]{2,1,0:T(8,128)S(1)}, f32[64,16,128]{2,1,0:T(8,128)S(1)}, u32[]{:S(2)}, u32[]{:S(2)}) collective-permute-start(f32[64,16,128]{2,1,0:T(8,128)S(1)} %slice.4), channel_id=1, source_target_pairs={{0,2},{2,0},{1,3},{3,1},{4,6},{6,4},{5,7},{7,5},{8,10},{10,8},{9,1... | collective-permute-start | bytes 1572872 | tf_op jit(solution)/shard_map/ppermute | solution.py:344
  40.0 1.6 %collective-permute-start.1 = (f32[64,8,128]{2,1,0:T(8,128)S(1)}, f32[64,8,128]{2,1,0:T(8,128)S(1)}, u32[]{:S(2)}, u32[]{:S(2)}) collective-permute-start(f32[64,8,128]{2,1,0:T(8,128)S(1)} %get-tuple-element.7), channel_id=1, source_target_pairs={{0,2},{2,0},{1,3},{3,1},{4,6},{6,4},{5,7},{7,5},{8,10},{10,8},{9,1... | collective-permute-start | bytes 786440 | tf_op jit(solution)/shard_map/ppermute | solution.py:359
  42.5 21.5 %copy-start = (f32[16,512]{1,0:T(8,128)S(1)}, f32[16,512]{1,0:T(8,128)}, u32[]{:S(2)}) copy-start(f32[16,512]{1,0:T(8,128)} %rhs_ref.1) | copy-start | bytes 98308
  42.5 21.4 %all-to-all-start.1 = ((f32[64,16,128]{2,1,0:T(8,128)}), f32[64,16,128]{2,1,0:T(8,128)S(1)}, u32[]{:S(2)}, u32[]{:S(2)}) async-start(f32[64,16,128]{2,1,0:T(8,128)} %join.1), calls=%async_computation.1 | async-start | bytes 1048576 | tf_op jit(solution)/shard_map/all_to_all | solution.py:367

commit v6 on v5

--- a/solution.py
+++ b/solution.py
@@ -160,113 +160,147 @@
 
 
 def product_kernel(
-    own_ref, other_ref, out_ref, low_ref, far_ref,
-    left_ref, right_ref, vec_ref, rows_ref, flat_ref, col_ref,
+    own_ref, other_ref, whole_ref, low_ref, far_ref,
+    left_ref, right_ref, vec_ref, rows_ref, flat_ref, back_ref,
 ):
     on_pair = lax.axis_index("xh") * CHIPS + lax.axis_index("g") < len(PAIRS)
+    core = lax.axis_index("c")
     lane = lax.broadcasted_iota(jnp.int32, (8, 128), 1)
 
-    def set_rows(lo, flat):
-        for k in range(TILES):
-            features, columns = points_of(own_ref, k, lo)
-            at = slice(k * 128, (k + 1) * 128)
-            left_ref[at, :] = operand(features, True).T
-            rows_ref[k] = columns
-            if flat:
-                flat_ref[:, at] = jnp.concatenate(halves(columns), axis=0)
-
-    def set_columns(n, points):
+    def set_rows(k, points):
         features, columns = points
-        at = slice(n * 128, (n + 1) * 128)
+        at = slice(k * 128, (k + 1) * 128)
+        left_ref[at, :] = operand(features, True).T
+        rows_ref[k] = columns
+        flat_ref[:, at] = jnp.concatenate(halves(columns), axis=0)
+
+    def set_columns(at, points):
+        features, columns = points
         right_ref[:, at] = operand(features, False)
         vec_ref[at, :] = jnp.concatenate(halves(columns), axis=0).T
 
-    def multiply(width, both_ways):
-        product = jnp.zeros((32, 128), F32)
-        square = jnp.zeros((32, 128), F32)
-        for r in range(left_ref.shape[0] // ROWS):
-            strip = slice(ROWS * r, ROWS * (r + 1))
-            exponent = jnp.dot(
-                left_ref[strip, :], right_ref[:, :width], preferred_element_type=F32
-            )
-            tile = jnp.exp2(exponent).astype(BF16)
-            total = jnp.dot(tile, vec_ref[:width, :], preferred_element_type=F32)
-            if both_ways:
-                back = jnp.dot(flat_ref[:, strip], tile, preferred_element_type=F32)
-                col_ref[...] = back if r == 0 else col_ref[...] + back
-            for k in range(ROWS // 128 * r, ROWS // 128 * (r + 1)):
-                lo = 128 * k - ROWS * r
-                pair = total[lo : lo + 128].T
-                image = pair[:32] + pair[32:]
-                rows = rows_ref[k]
-                product = product + rows * image
-                if not both_ways:
-                    square = square + rows * rows
-                for xh in range(2):
-                    top, low = image[16 * xh : 16 * xh + 8], image[16 * xh + 8 : 16 * xh + 16]
-                    for chip in range(2):
-                        at = slice(64 * chip, 64 * (chip + 1))
-                        out_ref[CHIPS * xh + 2 * k + chip] = jnp.concatenate(
-                            [top[:, at], low[:, at]], axis=1
-                        )
-        product = jnp.sum(product, axis=1, keepdims=True) * (2.0 if both_ways else 1.0)
-        square = jnp.sum(square, axis=1, keepdims=True)
-        sums = []
+    def block(strip, at, back_from):
+        exponent = jnp.dot(left_ref[strip, :], right_ref[:, at], preferred_element_type=F32)
+        tile = jnp.exp2(exponent).astype(BF16)
+        total = jnp.dot(tile, vec_ref[at, :], preferred_element_type=F32)
+        if back_from < at.stop:
+            back = jnp.dot(
+                flat_ref[:, strip], tile[:, back_from - at.start :], preferred_element_type=F32
+            )
+            back_ref[:, back_from : at.stop] = back_ref[:, back_from : at.stop] + back
+        return total
+
+    def give_rows(k, image):
         for xh in range(2):
-            here = jnp.zeros((8, 128), F32)
-            for n, x in enumerate((product, square)):
-                for a in range(2):
-                    lo = 16 * xh + 8 * a
-                    here = jnp.where(lane == 64 + 2 * n + a, x[lo : lo + 8], here)
-            sums.append(here)
-        return sums
+            top, low = image[16 * xh : 16 * xh + 8], image[16 * xh + 8 : 16 * xh + 16]
+            for chip in range(2):
+                at = slice(64 * chip, 64 * (chip + 1))
+                whole_ref[CHIPS * xh + 2 * k + chip] = jnp.concatenate(
+                    [top[:, at], low[:, at]], axis=1
+                )
+
+    def sums_of(product, square):
+        here = jnp.zeros((8, 128), F32)
+        for n, x in enumerate((product, square)):
+            x = jnp.sum(x, axis=1, keepdims=True)
+            for m in range(4):
+                here = jnp.where(lane == 64 + 4 * (m // 2) + 2 * n + m % 2, x[8 * m : 8 * m + 8], here)
+        return here
+
+    back_ref[...] = jnp.zeros_like(back_ref)
 
     @pl.when(on_pair)
     def _():
-        set_rows(0, True)
-        for n in range(TILES // 2):
-            set_columns(n, half_points_of(own_ref, n, 16))
-        for n in range(TILES // 2):
-            set_columns(TILES // 2 + n, half_points_of(other_ref, n, 8))
-        sums = multiply(2 * HALF, True)
+        for k in range(TILES):
+            set_rows(k, points_of(own_ref, k, 0))
+        for n in range(TILES):
+            ref, k, lo = (own_ref, n, 16) if n < TILES // 2 else (other_ref, n - TILES // 2, 8)
+            set_columns(slice(128 * n, 128 * n + 128), half_points_of(ref, k, lo))
+        product = jnp.zeros((32, 128), F32)
+        for r in range(2 * HALF // ROWS):
+            total = block(slice(ROWS * r, ROWS * (r + 1)), slice(0, 2 * HALF), 0)
+            for n in range(ROWS // 128):
+                k = ROWS // 128 * r + n
+                both = total[128 * n : 128 * (n + 1)].T
+                image = both[:32] + both[32:]
+                product = product + 2.0 * (rows_ref[k] * image)
+                give_rows(k, image)
+        far_ref[PEERS] = sums_of(product, jnp.zeros((32, 128), F32))
+        blank = jnp.zeros((8, 64), F32)
         for n in range(TILES):
             at = slice(n * 128, (n + 1) * 128)
-            image = col_ref[:32, at] + col_ref[32:, at]
+            image = back_ref[:32, at] + back_ref[32:, at]
             k = n % (TILES // 2)
+            ref = low_ref if n < TILES // 2 else far_ref
             for xh in range(2):
                 for j in range(4):
                     at = slice(32 * j, 32 * j + 32)
-                    part = jnp.concatenate(
-                        [image[16 * xh : 16 * xh + 8, at], image[16 * xh + 8 : 16 * xh + 16, at]]
-                        + [sums[xh][:, 64:]],
+                    ref[CHIPS * xh + 4 * k + j] = jnp.concatenate(
+                        [
+                            image[16 * xh : 16 * xh + 8, at],
+                            image[16 * xh + 8 : 16 * xh + 16, at],
+                            blank,
+                        ],
                         axis=1,
                     )
-                    if n < TILES // 2:
-                        low_ref[CHIPS * xh + 4 * k + j] = part
-                    else:
-                        far_ref[CHIPS * xh + 4 * k + j] = part
 
     @pl.when(jnp.logical_not(on_pair))
     def _():
-        set_rows(8, False)
-        for n in range(TILES):
-            set_columns(n, points_of(own_ref, n, 8))
-        for n in range(TILES):
-            set_columns(TILES + n, points_of(other_ref, n, 0))
-        sums = multiply(4 * HALF, False)
-        for xh in range(2):
-            at = slice(CHIPS * xh, CHIPS * (xh + 1))
-            low_ref[at] = jnp.broadcast_to(sums[xh], (CHIPS, 8, 128))
-            far_ref[at] = jnp.broadcast_to(sums[xh], (CHIPS, 8, 128))
-
-
-def join_kernel(whole_ref, low_ref, near_ref, out_ref):
-    out_ref[:, :8] = whole_ref[...]
-    out_ref[:, 8:] = low_ref[...] + near_ref[...]
-
-
-def finish_kernel(got_ref, rhs_ref, pair_ref, sol_ref, res_ref):
-    scale, noise = pair_ref[0:1, 0:1], pair_ref[4:5, 0:1]
+        for k in range(TILES):
+            points = points_of(own_ref, k, 8)
+            set_rows(k, points)
+            set_columns(slice(128 * k, 128 * k + 128), points)
+        for k in range(TILES):
+            half = (k // (TILES // 2) + core) % 2
+            at = 2 * HALF + half * HALF + k % (TILES // 2) * 128
+            set_columns(pl.ds(pl.multiple_of(at, 128), 128), points_of(other_ref, k, 0))
+        product = jnp.zeros((32, 128), F32)
+        square = jnp.zeros((32, 128), F32)
+        for r in range(2 * HALF // ROWS):
+            strip = slice(ROWS * r, ROWS * (r + 1))
+            near = block(strip, slice(strip.start, 2 * HALF), strip.stop)
+            start = 2 * HALF + strip.start // HALF * HALF
+            total = jnp.concatenate(
+                [near, block(strip, slice(start, start + HALF), start)], axis=1
+            )
+            for n in range(ROWS // 128):
+                k = ROWS // 128 * r + n
+                at = slice(128 * k, 128 * (k + 1))
+                four = total[128 * n : 128 * (n + 1)].T
+                image = four[:32] + four[32:64] + (back_ref[:32, at] + back_ref[32:, at])
+                cross = four[64:96] + four[96:]
+                rows = rows_ref[k]
+                product = product + rows * (image + 2.0 * cross)
+                square = square + rows * rows
+                give_rows(k, image + cross)
+        far_ref[PEERS] = sums_of(product, square)
+        low_ref[...] = jnp.zeros_like(low_ref)
+        for k in range(TILES):
+            half = (k // (TILES // 2) + core) % 2
+            at = pl.multiple_of(2 * HALF + half * HALF + k % (TILES // 2) * 128, 128)
+            both = back_ref[:, pl.ds(at, 128)]
+            image = both[:32] + both[32:]
+            for xh in range(2):
+                top, low = image[16 * xh : 16 * xh + 8], image[16 * xh + 8 : 16 * xh + 16]
+                for chip in range(2):
+                    at = slice(64 * chip, 64 * (chip + 1))
+                    far_ref[CHIPS * xh + 2 * k + chip] = jnp.concatenate(
+                        [top[:, at], low[:, at]], axis=1
+                    )
+
+
+def join_kernel(whole_ref, low_ref, far_ref, near_ref, pair_ref, out_ref):
+    on_pair = lax.axis_index("xh") * CHIPS + lax.axis_index("g") < len(PAIRS)
+    lane = lax.broadcasted_iota(jnp.int32, (8, 128), 1)
+    near = near_ref[:PEERS]
+    sums = jnp.where(lane < 72, far_ref[PEERS] + near_ref[PEERS], pair_ref[...])
+    out_ref[:, :8] = whole_ref[...] + jnp.where(on_pair, 0.0, near)
+    out_ref[:, 8:] = low_ref[...] + jnp.where(on_pair, near, 0.0) + sums
+
+
+def finish_kernel(got_ref, rhs_ref, sol_ref, res_ref):
+    pair = got_ref[0, 8:]
+    scale, noise = pair[0:1, 72:73], pair[0:1, 100:101]
     whole = [None] * GROUPS
     part = [None] * (2 * GROUPS)
     sums = got_ref[len(PAIRS), 8:]
@@ -283,8 +317,9 @@
         whole[a] = plus(whole[a], got_ref[len(PAIRS) + a, :8])
         if a:
             sums = sums + got_ref[len(PAIRS) + a, 8:]
-    product = jnp.concatenate([sums[:, 64:65], sums[:, 65:66]], axis=0)
-    square = jnp.concatenate([sums[:, 66:67], sums[:, 67:68]], axis=0)
+    mine = jnp.where(lax.axis_index("xh") == 0, sums[:, 64:68], sums[:, 68:72])
+    product = jnp.concatenate([mine[:, 0:1], mine[:, 1:2]], axis=0)
+    square = jnp.concatenate([mine[:, 2:3], mine[:, 3:4]], axis=0)
     step = square / (scale * product + noise * square)
     image = jnp.concatenate(
         [
@@ -344,36 +379,36 @@
     other = lax.ppermute(own[:, 8:], "c", swap)
     whole, low, far = pl.pallas_call(
         product_kernel,
-        out_shape=(jax.ShapeDtypeStruct((PEERS, 8, 128), F32),) * 3,
+        out_shape=tuple(jax.ShapeDtypeStruct((n, 8, 128), F32) for n in (PEERS, PEERS, PEERS + 1)),
         scratch_shapes=[
             pltpu.VMEM((2 * HALF, DEPTH), BF16),
             pltpu.VMEM((DEPTH, 4 * HALF), BF16),
             pltpu.VMEM((4 * HALF, 64), BF16),
             pltpu.VMEM((TILES, 32, 128), F32),
             pltpu.VMEM((64, 2 * HALF), BF16),
-            pltpu.VMEM((64, 2 * HALF), F32),
+            pltpu.VMEM((64, 4 * HALF), F32),
         ],
         compiler_params=pltpu.CompilerParams(vmem_limit_bytes=32 << 20),
         name="kernel_product",
     )(own, other)
     near = lax.ppermute(far, "c", swap)
+    lane = lax.broadcasted_iota(jnp.int32, (8, 128), 1)
+    pair = jnp.where(lane < 72, 0.0, jnp.where(lane < 100, outputscale[0], noise[0]))
     partial = pl.pallas_call(
         join_kernel,
         out_shape=jax.ShapeDtypeStruct((PEERS, 16, 128), F32),
-        in_specs=[vmem] * 3,
+        in_specs=[vmem] * 5,
         compiler_params=pltpu.CompilerParams(vmem_limit_bytes=8 << 20),
         name="join",
-    )(whole, low, near)
+    )(whole, low, far, near, pair)
     got = lax.all_to_all(partial, ("xh", "g"), 0, 0, tiled=True)
-    row = lax.broadcasted_iota(jnp.int32, (8, 128), 0)
-    pair = jnp.where(row < 4, outputscale[0], noise[0])
     return pl.pallas_call(
         finish_kernel,
         out_shape=(jax.ShapeDtypeStruct(rhs.shape, F32),) * 2,
-        in_specs=[vmem] * 3,
+        in_specs=[vmem] * 2,
         compiler_params=pltpu.CompilerParams(vmem_limit_bytes=8 << 20),
         name="update",
-    )(got, rhs, pair)
+    )(got, rhs)
 
 
 def solution(mesh):

time: 65.3 us -> 61.9 us (0.948)
  blocking collectives: 26.9 us -> 45.5 us
  waiting for transfers between devices: 15.1 us -> 1.98 us
  starting transfers between devices: 8.55 us -> 0.3 us
    all_to_all x0 -> x1, blocking collectives: none -> 18.6 us  [on_device(): got = lax.all_to_all(partial, ('xh', 'g'), 0, 0, tiled=True)]
    all_to_all x1 -> x0, waiting for transfers between devices: 11.8 us -> none  [on_device(): got = lax.all_to_all(partial, ('xh', 'g'), 0, 0, tiled=True)]
    all_to_all x1 -> x0, starting transfers between devices: 8.24 us -> none  [on_device(): got = lax.all_to_all(partial, ('xh', 'g'), 0, 0, tiled=True)]
    ppermute x1, waiting for transfers between devices: 1.9 us -> 0.59 us  [on_device(): other = lax.ppermute(own[:, 8:], 'c', swap)]
    pallas_call x1, Pallas kernels: 0.83 us -> 0.06 us  [on_device(): pl.pallas_call(join_kernel, out_shape=jax.ShapeDtypeStruct((PEERS, 16, 12...]
  transfers between devices with their start and end apart: 3 -> 2, of which waited for: 3 -> 2; matrix products, arithmetic and copies ran while one was open for 0% -> 0% of each run, Pallas kernels for 0% -> 0%
where the time goes in v6:
time: 61.9 us; the launch traced here: 61.5 us
  blocking collectives  45.5 us (74%)
  Pallas kernels  11.7 us (19%)
  waiting for transfers between devices  1.98 us (3%)
  between operations  1.98 us (3%)
    all_to_all x1, blocking collectives, on_device(): own = lax.all_to_all(sent, ('xh', 'g'), 0, 0, tiled=True)  26.9 us
    all_to_all x1, blocking collectives, on_device(): got = lax.all_to_all(partial, ('xh', 'g'), 0, 0, tiled=True)  18.6 us
    pallas_call x1, Pallas kernels, on_device(): pl.pallas_call(product_kernel, out_shape=tuple((jax.ShapeDtypeStruct((n,...  7.56 us
    pallas_call x1, Pallas kernels, on_device(): pl.pallas_call(pack_kernel, out_shape=jax.ShapeDtypeStruct((PEERS, 24, 12...  3 us
    ppermute x1, waiting for transfers between devices, on_device(): near = lax.ppermute(far, 'c', swap)  1.39 us
  transfers between devices with their start and end apart: 2, of which 2 were waited for; matrix products, arithmetic and copies ran while one was open for 0% of the time, Pallas kernels for 0%

profile of v6, /device:TPU:0, one launch (start us, length us, event | category | flops | bytes accessed | tf_op | source)
XLA Modules:
  0.0 61.5 jit_solution(4846389883712387460)
XLA Ops:
  0.6 3.0 %features.1 = f32[64,24,128]{2,1,0:T(8,128)} custom-call(bf16[256,1024]{1,0:T(8,128)(2,1)} %enc_hbm.1, bf16[1024,512]{1,0:T(8,128)(2,1)} %w1_hbm.1, bf16[32,512]{1,0:T(8,128)(2,1)} %bitcast.6, f32[1,32]{1,0:T(1,128)} %bitcast.7, f32[16,512]{1,0:T(8,128)} %rhs_ref.1), custom_call_target="tpu_custom_call" | custom-call | tf_op jit(solution)/shard_map/features/pallas_call | solution.py:361
  3.6 26.9 %all_to_all.10.own_ref = f32[64,24,128]{2,1,0:T(8,128)S(1)} all-to-all(f32[64,24,128]{2,1,0:T(8,128)} %features.1), channel_id=1, replica_groups=mesh['g'=32,'c'=2,'xh'=2] {'xh','g'}, dimensions={0} | all-to-all | bytes 1572864 | tf_op jit(solution)/shard_map/all_to_all | solution.py:378
  30.5 0.1 collective-permute-start
  31.9 0.6 collective-permute-done.other_ref
  32.5 7.6 %kernel_product.1 = (f32[64,8,128]{2,1,0:T(8,128)S(1)}, f32[64,8,128]{2,1,0:T(8,128)S(1)}, f32[65,8,128]{2,1,0:T(8,128)S(1)}) custom-call(f32[64,24,128]{2,1,0:T(8,128)S(1)} %all_to_all.10.own_ref, f32[64,16,128]{2,1,0:T(8,128)S(1)} %collective-permute-done.other_ref), custom_call_target="tpu_custom_call" | custom-call | tf_op jit(solution)/shard_map/kernel_product/pallas_call | solution.py:380
  40.1 0.2 collective-permute-start.1
  40.3 1.4 %collective-permute-done.1.near_ref = f32[65,8,128]{2,1,0:T(8,128)S(1)} collective-permute-done((f32[65,8,128]{2,1,0:T(8,128)S(1)}, f32[65,8,128]{2,1,0:T(8,128)S(1)}, u32[]{:S(2)}, u32[]{:S(2)}) %collective-permute-start.1) | collective-permute-done | bytes 266272 | tf_op jit(solution)/shard_map/ppermute | solution.py:394
  41.7 0.1 join.1
  41.8 0.0 copy-start
  41.8 18.6 %all_to_all.11.got_ref = f32[64,16,128]{2,1,0:T(8,128)S(1)} all-to-all(f32[64,16,128]{2,1,0:T(8,128)S(1)} %join.1), channel_id=1, replica_groups=mesh['g'=32,'c'=2,'xh'=2] {'xh','g'}, dimensions={0} | all-to-all | bytes 1048576 | tf_op jit(solution)/shard_map/all_to_all | solution.py:404
  60.4 0.0 copy-done
  60.4 1.1 %update.1 = (f32[16,512]{1,0:T(8,128)}, f32[16,512]{1,0:T(8,128)}) custom-call(f32[64,16,128]{2,1,0:T(8,128)S(1)} %all_to_all.11.got_ref, f32[16,512]{1,0:T(8,128)S(1)} %copy-done), custom_call_target="tpu_custom_call" | custom-call | tf_op jit(solution)/shard_map/update/pallas_call | solution.py:405
  (4 shorter events, 0.1 us)
Async XLA Ops:
  30.5 2.0 %collective-permute-start = (f32[64,16,128]{2,1,0:T(8,128)S(1)}, f32[64,16,128]{2,1,0:T(8,128)S(1)}, u32[]{:S(2)}, u32[]{:S(2)}) collective-permute-start(f32[64,16,128]{2,1,0:T(8,128)S(1)} %slice.4), channel_id=1, source_target_pairs={{0,2},{2,0},{1,3},{3,1},{4,6},{6,4},{5,7},{7,5},{8,10},{10,8},{9,1... | collective-permute-start | bytes 1572872 | tf_op jit(solution)/shard_map/ppermute | solution.py:379
  40.1 1.6 %collective-permute-start.1 = (f32[65,8,128]{2,1,0:T(8,128)S(1)}, f32[65,8,128]{2,1,0:T(8,128)S(1)}, u32[]{:S(2)}, u32[]{:S(2)}) collective-permute-start(f32[65,8,128]{2,1,0:T(8,128)S(1)} %get-tuple-element.7.far_ref), channel_id=1, source_target_pairs={{0,2},{2,0},{1,3},{3,1},{4,6},{6,4},{5,7},{7,5},{8,10},{10,8},{9,1... | collective-permute-start | bytes 798728 | tf_op jit(solution)/shard_map/ppermute | solution.py:394
  41.8 18.6 %copy-start = (f32[16,512]{1,0:T(8,128)S(1)}, f32[16,512]{1,0:T(8,128)}, u32[]{:S(2)}) copy-start(f32[16,512]{1,0:T(8,128)} %rhs_ref.1) | copy-start | bytes 98308

commit v7 on v5

--- a/solution.py
+++ b/solution.py
@@ -159,114 +159,169 @@
     return jnp.concatenate(parts + [tail, blank], axis=0)
 
 
-def product_kernel(
-    own_ref, other_ref, out_ref, low_ref, far_ref,
-    left_ref, right_ref, vec_ref, rows_ref, flat_ref, col_ref,
+def on_pair():
+    return lax.axis_index("xh") * CHIPS + lax.axis_index("g") < len(PAIRS)
+
+
+def set_columns(right_ref, vec_ref, at, points):
+    features, columns = points
+    right_ref[:, at] = operand(features, False)
+    vec_ref[at, :] = jnp.concatenate(halves(columns), axis=0).T
+
+
+def block(left_ref, flat_ref, right_ref, vec_ref, back_ref, strip, at, back_from, first):
+    exponent = jnp.dot(left_ref[strip, :], right_ref[:, at], preferred_element_type=F32)
+    tile = jnp.exp2(exponent).astype(BF16)
+    total = jnp.dot(tile, vec_ref[at, :], preferred_element_type=F32)
+    if back_from < at.stop:
+        to = slice(back_from, at.stop)
+        back = jnp.dot(
+            flat_ref[:, strip], tile[:, back_from - at.start :], preferred_element_type=F32
+        )
+        back_ref[:, to] = back if first else back_ref[:, to] + back
+    return total
+
+
+def near_kernel(
+    own_ref, left_ref, rows_ref, flat_ref, image_ref, back_ref, right_ref, vec_ref
 ):
-    on_pair = lax.axis_index("xh") * CHIPS + lax.axis_index("g") < len(PAIRS)
+    pair = on_pair()
+
+    def set_rows(k, points):
+        features, columns = points
+        at = slice(k * 128, (k + 1) * 128)
+        left_ref[at, :] = operand(features, True).T
+        rows_ref[k] = columns
+        flat_ref[:, at] = jnp.concatenate(halves(columns), axis=0)
+
+    def multiply(ranges):
+        for r in range(2 * HALF // ROWS):
+            strip = slice(ROWS * r, ROWS * (r + 1))
+            at, back_from = ranges(strip)
+            total = block(
+                left_ref, flat_ref, right_ref, vec_ref, back_ref, strip, at, back_from, r == 0
+            )
+            for n in range(ROWS // 128):
+                both = total[128 * n : 128 * (n + 1)].T
+                image_ref[ROWS // 128 * r + n] = both[:32] + both[32:]
+
+    @pl.when(pair)
+    def _():
+        for k in range(TILES):
+            set_rows(k, points_of(own_ref, k, 0))
+        for n in range(TILES // 2):
+            at = slice(128 * n, 128 * n + 128)
+            set_columns(right_ref, vec_ref, at, half_points_of(own_ref, n, 16))
+        multiply(lambda strip: (slice(0, HALF), 0))
+
+    @pl.when(jnp.logical_not(pair))
+    def _():
+        for k in range(TILES):
+            points = points_of(own_ref, k, 8)
+            set_rows(k, points)
+            set_columns(right_ref, vec_ref, slice(128 * k, 128 * k + 128), points)
+        multiply(lambda strip: (slice(strip.start, 2 * HALF), strip.stop))
+        for k in range(ROWS // 128, TILES):
+            at = slice(128 * k, 128 * (k + 1))
+            image_ref[k] = image_ref[k] + (back_ref[:32, at] + back_ref[32:, at])
+
+
+def far_kernel(
+    other_ref, left_ref, rows_ref, flat_ref, image_ref, back_in_ref,
+    whole_ref, low_ref, far_ref, right_ref, vec_ref, back_ref,
+):
+    pair = on_pair()
+    core = lax.axis_index("c")
     lane = lax.broadcasted_iota(jnp.int32, (8, 128), 1)
 
-    def set_rows(lo, flat):
-        for k in range(TILES):
-            features, columns = points_of(own_ref, k, lo)
-            at = slice(k * 128, (k + 1) * 128)
-            left_ref[at, :] = operand(features, True).T
-            rows_ref[k] = columns
-            if flat:
-                flat_ref[:, at] = jnp.concatenate(halves(columns), axis=0)
-
-    def set_columns(n, points):
-        features, columns = points
-        at = slice(n * 128, (n + 1) * 128)
-        right_ref[:, at] = operand(features, False)
-        vec_ref[at, :] = jnp.concatenate(halves(columns), axis=0).T
-
-    def multiply(width, both_ways):
+    def multiply(columns_of, both_times, square_times):
         product = jnp.zeros((32, 128), F32)
         square = jnp.zeros((32, 128), F32)
-        for r in range(left_ref.shape[0] // ROWS):
+        for r in range(2 * HALF // ROWS):
             strip = slice(ROWS * r, ROWS * (r + 1))
-            exponent = jnp.dot(
-                left_ref[strip, :], right_ref[:, :width], preferred_element_type=F32
-            )
-            tile = jnp.exp2(exponent).astype(BF16)
-            total = jnp.dot(tile, vec_ref[:width, :], preferred_element_type=F32)
-            if both_ways:
-                back = jnp.dot(flat_ref[:, strip], tile, preferred_element_type=F32)
-                col_ref[...] = back if r == 0 else col_ref[...] + back
-            for k in range(ROWS // 128 * r, ROWS // 128 * (r + 1)):
-                lo = 128 * k - ROWS * r
-                pair = total[lo : lo + 128].T
-                image = pair[:32] + pair[32:]
+            at, first = columns_of(strip)
+            total = block(
+                left_ref, flat_ref, right_ref, vec_ref, back_ref, strip, at, at.start, first
+            )
+            for n in range(ROWS // 128):
+                k = ROWS // 128 * r + n
+                both = total[128 * n : 128 * (n + 1)].T
+                cross = both[:32] + both[32:]
                 rows = rows_ref[k]
-                product = product + rows * image
-                if not both_ways:
+                product = product + rows * (both_times * image_ref[k] + 2.0 * cross)
+                if square_times:
                     square = square + rows * rows
+                give_whole(whole_ref, k, image_ref[k] + cross)
+        here = jnp.zeros((8, 128), F32)
+        for n, x in enumerate((product, square)):
+            x = jnp.sum(x, axis=1, keepdims=True)
+            for m in range(4):
+                to = 64 + 4 * (m // 2) + 2 * n + m % 2
+                here = jnp.where(lane == to, x[8 * m : 8 * m + 8], here)
+        far_ref[PEERS] = here
+
+    def give_whole(ref, k, image):
+        for xh in range(2):
+            top, low = image[16 * xh : 16 * xh + 8], image[16 * xh + 8 : 16 * xh + 16]
+            for chip in range(2):
+                at = slice(64 * chip, 64 * (chip + 1))
+                ref[CHIPS * xh + 2 * k + chip] = jnp.concatenate([top[:, at], low[:, at]], axis=1)
+
+    @pl.when(pair)
+    def _():
+        for n in range(TILES // 2):
+            at = slice(128 * n, 128 * n + 128)
+            set_columns(right_ref, vec_ref, at, half_points_of(other_ref, n, 8))
+        multiply(lambda strip: (slice(0, HALF), strip.start == 0), 2.0, 0)
+        blank = jnp.zeros((8, 64), F32)
+        for given, ref in ((back_in_ref, low_ref), (back_ref, far_ref)):
+            for k in range(TILES // 2):
+                at = slice(k * 128, (k + 1) * 128)
+                image = given[:32, at] + given[32:, at]
                 for xh in range(2):
                     top, low = image[16 * xh : 16 * xh + 8], image[16 * xh + 8 : 16 * xh + 16]
-                    for chip in range(2):
-                        at = slice(64 * chip, 64 * (chip + 1))
-                        out_ref[CHIPS * xh + 2 * k + chip] = jnp.concatenate(
-                            [top[:, at], low[:, at]], axis=1
+                    for j in range(4):
+                        at = slice(32 * j, 32 * j + 32)
+                        ref[CHIPS * xh + 4 * k + j] = jnp.concatenate(
+                            [top[:, at], low[:, at], blank], axis=1
                         )
-        product = jnp.sum(product, axis=1, keepdims=True) * (2.0 if both_ways else 1.0)
-        square = jnp.sum(square, axis=1, keepdims=True)
-        sums = []
-        for xh in range(2):
-            here = jnp.zeros((8, 128), F32)
-            for n, x in enumerate((product, square)):
-                for a in range(2):
-                    lo = 16 * xh + 8 * a
-                    here = jnp.where(lane == 64 + 2 * n + a, x[lo : lo + 8], here)
-            sums.append(here)
-        return sums
-
-    @pl.when(on_pair)
+
+    @pl.when(jnp.logical_not(pair))
     def _():
-        set_rows(0, True)
-        for n in range(TILES // 2):
-            set_columns(n, half_points_of(own_ref, n, 16))
-        for n in range(TILES // 2):
-            set_columns(TILES // 2 + n, half_points_of(other_ref, n, 8))
-        sums = multiply(2 * HALF, True)
-        for n in range(TILES):
-            at = slice(n * 128, (n + 1) * 128)
-            image = col_ref[:32, at] + col_ref[32:, at]
-            k = n % (TILES // 2)
-            for xh in range(2):
-                for j in range(4):
-                    at = slice(32 * j, 32 * j + 32)
-                    part = jnp.concatenate(
-                        [image[16 * xh : 16 * xh + 8, at], image[16 * xh + 8 : 16 * xh + 16, at]]
-                        + [sums[xh][:, 64:]],
-                        axis=1,
-                    )
-                    if n < TILES // 2:
-                        low_ref[CHIPS * xh + 4 * k + j] = part
-                    else:
-                        far_ref[CHIPS * xh + 4 * k + j] = part
-
-    @pl.when(jnp.logical_not(on_pair))
-    def _():
-        set_rows(8, False)
-        for n in range(TILES):
-            set_columns(n, points_of(own_ref, n, 8))
-        for n in range(TILES):
-            set_columns(TILES + n, points_of(other_ref, n, 0))
-        sums = multiply(4 * HALF, False)
-        for xh in range(2):
-            at = slice(CHIPS * xh, CHIPS * (xh + 1))
-            low_ref[at] = jnp.broadcast_to(sums[xh], (CHIPS, 8, 128))
-            far_ref[at] = jnp.broadcast_to(sums[xh], (CHIPS, 8, 128))
-
-
-def join_kernel(whole_ref, low_ref, near_ref, out_ref):
-    out_ref[:, :8] = whole_ref[...]
-    out_ref[:, 8:] = low_ref[...] + near_ref[...]
-
-
-def finish_kernel(got_ref, rhs_ref, pair_ref, sol_ref, res_ref):
-    scale, noise = pair_ref[0:1, 0:1], pair_ref[4:5, 0:1]
+        def place(k):
+            half = (k // (TILES // 2) + core) % 2
+            return pl.ds(pl.multiple_of(half * HALF + k % (TILES // 2) * 128, 128), 128)
+
+        for k in range(TILES):
+            set_columns(right_ref, vec_ref, place(k), points_of(other_ref, k, 0))
+
+        def columns_of(strip):
+            start = strip.start // HALF * HALF
+            return slice(start, start + HALF), strip.start == start
+
+        multiply(columns_of, 1.0, 1)
+        low_ref[...] = jnp.zeros_like(low_ref)
+        for k in range(TILES):
+            both = back_ref[:, place(k)]
+            give_whole(far_ref, k, both[:32] + both[32:])
+
+
+def join_kernel(whole_ref, low_ref, far_ref, near_ref, scale_ref, noise_ref, out_ref):
+    pair = on_pair()
+    lane = lax.broadcasted_iota(jnp.int32, (8, 128), 1)
+    near = near_ref[:PEERS]
+    sums = jnp.where(
+        lane < 72,
+        far_ref[PEERS] + near_ref[PEERS],
+        jnp.where(lane < 100, scale_ref[0], noise_ref[0]),
+    )
+    out_ref[:, :8] = whole_ref[...] + jnp.where(pair, 0.0, near)
+    out_ref[:, 8:] = low_ref[...] + jnp.where(pair, near, 0.0) + sums
+
+
+def finish_kernel(got_ref, rhs_ref, sol_ref, res_ref):
+    pair = got_ref[0, 8:]
+    scale, noise = pair[0:1, 72:73], pair[0:1, 100:101]
     whole = [None] * GROUPS
     part = [None] * (2 * GROUPS)
     sums = got_ref[len(PAIRS), 8:]
@@ -283,8 +338,9 @@
         whole[a] = plus(whole[a], got_ref[len(PAIRS) + a, :8])
         if a:
             sums = sums + got_ref[len(PAIRS) + a, 8:]
-    product = jnp.concatenate([sums[:, 64:65], sums[:, 65:66]], axis=0)
-    square = jnp.concatenate([sums[:, 66:67], sums[:, 67:68]], axis=0)
+    mine = jnp.where(lax.axis_index("xh") == 0, sums[:, 64:68], sums[:, 68:72])
+    product = jnp.concatenate([mine[:, 0:1], mine[:, 1:2]], axis=0)
+    square = jnp.concatenate([mine[:, 2:3], mine[:, 3:4]], axis=0)
     step = square / (scale * product + noise * square)
     image = jnp.concatenate(
         [
@@ -342,38 +398,53 @@
     )(encodings, first_weight, second_weight.T, inv_scale.reshape(1, -1), rhs)
     own = lax.all_to_all(sent, ("xh", "g"), 0, 0, tiled=True)
     other = lax.ppermute(own[:, 8:], "c", swap)
+    cost = pl.CostEstimate(flops=4 << 30, bytes_accessed=1 << 20, transcendentals=1 << 21)
+    *rows, back = pl.pallas_call(
+        near_kernel,
+        out_shape=(
+            jax.ShapeDtypeStruct((2 * HALF, DEPTH), BF16),
+            jax.ShapeDtypeStruct((TILES, 32, 128), F32),
+            jax.ShapeDtypeStruct((64, 2 * HALF), BF16),
+            jax.ShapeDtypeStruct((TILES, 32, 128), F32),
+            jax.ShapeDtypeStruct((64, 2 * HALF), F32),
+        ),
+        scratch_shapes=[
+            pltpu.VMEM((DEPTH, 2 * HALF), BF16),
+            pltpu.VMEM((2 * HALF, 64), BF16),
+        ],
+        compiler_params=pltpu.CompilerParams(vmem_limit_bytes=24 << 20),
+        cost_estimate=cost,
+        name="own_columns",
+    )(own)
     whole, low, far = pl.pallas_call(
-        product_kernel,
-        out_shape=(jax.ShapeDtypeStruct((PEERS, 8, 128), F32),) * 3,
+        far_kernel,
+        out_shape=tuple(jax.ShapeDtypeStruct((n, 8, 128), F32) for n in (PEERS, PEERS, PEERS + 1)),
         scratch_shapes=[
-            pltpu.VMEM((2 * HALF, DEPTH), BF16),
-            pltpu.VMEM((DEPTH, 4 * HALF), BF16),
-            pltpu.VMEM((4 * HALF, 64), BF16),
-            pltpu.VMEM((TILES, 32, 128), F32),
-            pltpu.VMEM((64, 2 * HALF), BF16),
+            pltpu.VMEM((DEPTH, 2 * HALF), BF16),
+            pltpu.VMEM((2 * HALF, 64), BF16),
             pltpu.VMEM((64, 2 * HALF), F32),
         ],
-        compiler_params=pltpu.CompilerParams(vmem_limit_bytes=32 << 20),
-        name="kernel_product",
-    )(own, other)
+        compiler_params=pltpu.CompilerParams(vmem_limit_bytes=24 << 20),
+        cost_estimate=cost,
+        name="other_columns",
+    )(other, *rows, back)
     near = lax.ppermute(far, "c", swap)
+    smem = pl.BlockSpec(memory_space=pltpu.SMEM)
     partial = pl.pallas_call(
         join_kernel,
         out_shape=jax.ShapeDtypeStruct((PEERS, 16, 128), F32),
-        in_specs=[vmem] * 3,
+        in_specs=[vmem] * 4 + [smem] * 2,
         compiler_params=pltpu.CompilerParams(vmem_limit_bytes=8 << 20),
         name="join",
-    )(whole, low, near)
+    )(whole, low, far, near, outputscale, noise)
     got = lax.all_to_all(partial, ("xh", "g"), 0, 0, tiled=True)
-    row = lax.broadcasted_iota(jnp.int32, (8, 128), 0)
-    pair = jnp.where(row < 4, outputscale[0], noise[0])
     return pl.pallas_call(
         finish_kernel,
         out_shape=(jax.ShapeDtypeStruct(rhs.shape, F32),) * 2,
-        in_specs=[vmem] * 3,
+        in_specs=[vmem] * 2,
         compiler_params=pltpu.CompilerParams(vmem_limit_bytes=8 << 20),
         name="update",
-    )(got, rhs, pair)
+    )(got, rhs)
 
 
 def solution(mesh):

time: 65.3 us -> 60.8 us (0.931)
  the two profiles are of different devices: /device:TPU:0 before, /device:TPU:1 now
where the time goes in v7:
time: 60.8 us; the launch traced here: 59.9 us
  blocking collectives  42.7 us (70%)
  Pallas kernels  12.1 us (20%)
  starting transfers between devices  2.87 us (5%)
  between operations  1.97 us (3%)
    all_to_all x1, blocking collectives, on_device(): own = lax.all_to_all(sent, ('xh', 'g'), 0, 0, tiled=True)  25.6 us
    all_to_all x1, blocking collectives, on_device(): got = lax.all_to_all(partial, ('xh', 'g'), 0, 0, tiled=True)  17.1 us
    pallas_call x1, Pallas kernels, on_device(): pl.pallas_call(far_kernel, out_shape=tuple((jax.ShapeDtypeStruct((n, 8, 1...  4.05 us
    pallas_call x1, Pallas kernels, on_device(): pl.pallas_call(near_kernel, out_shape=(jax.ShapeDtypeStruct((2 * HALF, DE...  3.85 us
    pallas_call x1, Pallas kernels, on_device(): pl.pallas_call(pack_kernel, out_shape=jax.ShapeDtypeStruct((PEERS, 24, 12...  3 us
    ppermute x1, starting transfers between devices, on_device(): other = lax.ppermute(own[:, 8:], 'c', swap)  2.77 us
  transfers between devices with their start and end apart: 2, of which 1 were waited for; matrix products, arithmetic and copies ran while one was open for 0% of the time, Pallas kernels for 6%

profile of v7, /device:TPU:1, one launch (start us, length us, event | category | flops | bytes accessed | tf_op | source)
XLA Modules:
  0.0 59.9 jit_solution(11108434387318298858)
XLA Ops:
  0.6 3.0 %features.1 = f32[64,24,128]{2,1,0:T(8,128)} custom-call(bf16[256,1024]{1,0:T(8,128)(2,1)} %enc_hbm.1, bf16[1024,512]{1,0:T(8,128)(2,1)} %w1_hbm.1, bf16[32,512]{1,0:T(8,128)(2,1)} %bitcast.2, f32[1,32]{1,0:T(1,128)} %bitcast.3, f32[16,512]{1,0:T(8,128)} %rhs_ref.1), custom_call_target="tpu_custom_call" | custom-call | tf_op jit(solution)/shard_map/features/pallas_call | solution.py:382
  3.6 25.6 %all_to_all.10.own_ref = f32[64,24,128]{2,1,0:T(8,128)S(1)} all-to-all(f32[64,24,128]{2,1,0:T(8,128)} %features.1), channel_id=1, replica_groups=mesh['g'=32,'c'=2,'xh'=2] {'xh','g'}, dimensions={0} | all-to-all | bytes 1572864 | tf_op jit(solution)/shard_map/all_to_all | solution.py:399
  29.3 2.8 %collective-permute-start = (f32[64,16,128]{2,1,0:T(8,128)S(1)}, f32[64,16,128]{2,1,0:T(8,128)S(1)}, u32[]{:S(2)}, u32[]{:S(2)}) collective-permute-start(f32[64,16,128]{2,1,0:T(8,128)S(1)} %slice.4), channel_id=1, source_target_pairs={{0,2},{2,0},{1,3},{3,1},{4,6},{6,4},{5,7},{7,5},{8,10},{10,8},{9,1... | collective-permute-start | bytes 1572872 | tf_op jit(solution)/shard_map/ppermute | solution.py:400
  32.0 3.9 %own_columns.1 = (bf16[2048,256]{1,0:T(8,128)(2,1)S(1)}, f32[16,32,128]{2,1,0:T(8,128)S(1)}, bf16[64,2048]{1,0:T(8,128)(2,1)S(1)}, f32[16,32,128]{2,1,0:T(8,128)S(1)}, f32[64,2048]{1,0:T(8,128)S(1)}) custom-call(f32[64,24,128]{2,1,0:T(8,128)S(1)} %all_to_all.10.own_ref), custom_call_target="tpu_custom_call" | custom-call | flops 4294967296 | bytes 1048576 | tf_op jit(solution)/shard_map/own_columns/pallas_call | solution.py:402
  35.9 0.0 collective-permute-done.other_ref
  35.9 4.0 %other_columns.1 = (f32[64,8,128]{2,1,0:T(8,128)S(1)}, f32[64,8,128]{2,1,0:T(8,128)S(1)}, f32[65,8,128]{2,1,0:T(8,128)S(1)}) custom-call(f32[64,16,128]{2,1,0:T(8,128)S(1)} %collective-permute-done.other_ref, bf16[2048,256]{1,0:T(8,128)(2,1)S(1)} %get-tuple-element.10.left_ref, f32[16,32,128]{2,1,0:T(8,128)S(1)} %get-tuple-element.11.rows_ref, ...), custom_call_target="tpu_custom_call" | custom-call | flops 4294967296 | bytes 1048576 | tf_op jit(solution)/shard_map/other_columns/pallas_call | solution.py:419
  40.0 0.1 collective-permute-start.1
  41.4 0.2 collective-permute-done.1.near_ref
  41.6 0.1 join.1
  41.6 0.0 copy-start
  41.7 17.1 %all_to_all.11.got_ref = f32[64,16,128]{2,1,0:T(8,128)S(1)} all-to-all(f32[64,16,128]{2,1,0:T(8,128)S(1)} %join.1), channel_id=1, replica_groups=mesh['g'=32,'c'=2,'xh'=2] {'xh','g'}, dimensions={0} | all-to-all | bytes 1048576 | tf_op jit(solution)/shard_map/all_to_all | solution.py:440
  58.8 0.0 copy-done
  58.8 1.1 %update.1 = (f32[16,512]{1,0:T(8,128)}, f32[16,512]{1,0:T(8,128)}) custom-call(f32[64,16,128]{2,1,0:T(8,128)S(1)} %all_to_all.11.got_ref, f32[16,512]{1,0:T(8,128)S(1)} %copy-done), custom_call_target="tpu_custom_call" | custom-call | tf_op jit(solution)/shard_map/update/pallas_call | solution.py:441
  (1 shorter events, 0.0 us)
Async XLA Ops:
  29.3 6.6 %collective-permute-start = (f32[64,16,128]{2,1,0:T(8,128)S(1)}, f32[64,16,128]{2,1,0:T(8,128)S(1)}, u32[]{:S(2)}, u32[]{:S(2)}) collective-permute-start(f32[64,16,128]{2,1,0:T(8,128)S(1)} %slice.4), channel_id=1, source_target_pairs={{0,2},{2,0},{1,3},{3,1},{4,6},{6,4},{5,7},{7,5},{8,10},{10,8},{9,1... | collective-permute-start | bytes 1572872 | tf_op jit(solution)/shard_map/ppermute | solution.py:400
  40.0 1.6 %collective-permute-start.1 = (f32[65,8,128]{2,1,0:T(8,128)S(1)}, f32[65,8,128]{2,1,0:T(8,128)S(1)}, u32[]{:S(2)}, u32[]{:S(2)}) collective-permute-start(f32[65,8,128]{2,1,0:T(8,128)S(1)} %get-tuple-element.17.far_ref), channel_id=1, source_target_pairs={{0,2},{2,0},{1,3},{3,1},{4,6},{6,4},{5,7},{7,5},{8,10},{10,8},{9,1... | collective-permute-start | bytes 798728 | tf_op jit(solution)/shard_map/ppermute | solution.py:431
  41.6 17.1 %copy-start = (f32[16,512]{1,0:T(8,128)S(1)}, f32[16,512]{1,0:T(8,128)}, u32[]{:S(2)}) copy-start(f32[16,512]{1,0:T(8,128)} %rhs_ref.1) | copy-start | bytes 98308

commit v8 on v7

--- a/solution.py
+++ b/solution.py
@@ -15,6 +15,8 @@
 DEPTH = 256
 STEPS = 4
 ROWS = 256
+PAIR_ROWS = 512
+AHEAD = 0
 PAIRS = [(a, b, t) for a in range(GROUPS) for b in range(a + 1, GROUPS) for t in range(2)]
 TILES = CHIPS // 2
 HALF = TILES * 128 // 2
@@ -194,25 +196,30 @@
         rows_ref[k] = columns
         flat_ref[:, at] = jnp.concatenate(halves(columns), axis=0)
 
-    def multiply(ranges):
-        for r in range(2 * HALF // ROWS):
-            strip = slice(ROWS * r, ROWS * (r + 1))
+    def multiply(rows, prepare, ranges):
+        for r in range(2 * HALF // rows):
+            strip = slice(rows * r, rows * (r + 1))
+            ahead = strip.stop + AHEAD
+            for k in range((strip.start + AHEAD if r else 0) // 128, min(ahead, 2 * HALF) // 128):
+                prepare(k)
             at, back_from = ranges(strip)
             total = block(
                 left_ref, flat_ref, right_ref, vec_ref, back_ref, strip, at, back_from, r == 0
             )
-            for n in range(ROWS // 128):
+            for n in range(rows // 128):
                 both = total[128 * n : 128 * (n + 1)].T
-                image_ref[ROWS // 128 * r + n] = both[:32] + both[32:]
+                image_ref[rows // 128 * r + n] = both[:32] + both[32:]
 
     @pl.when(pair)
     def _():
-        for k in range(TILES):
-            set_rows(k, points_of(own_ref, k, 0))
         for n in range(TILES // 2):
             at = slice(128 * n, 128 * n + 128)
             set_columns(right_ref, vec_ref, at, half_points_of(own_ref, n, 16))
-        multiply(lambda strip: (slice(0, HALF), 0))
+        multiply(
+            PAIR_ROWS,
+            lambda k: set_rows(k, points_of(own_ref, k, 0)),
+            lambda strip: (slice(0, HALF), 0),
+        )
 
     @pl.when(jnp.logical_not(pair))
     def _():
@@ -220,7 +227,9 @@
             points = points_of(own_ref, k, 8)
             set_rows(k, points)
             set_columns(right_ref, vec_ref, slice(128 * k, 128 * k + 128), points)
-        multiply(lambda strip: (slice(strip.start, 2 * HALF), strip.stop))
+        multiply(
+            ROWS, lambda k: None, lambda strip: (slice(strip.start, 2 * HALF), strip.stop)
+        )
         for k in range(ROWS // 128, TILES):
             at = slice(128 * k, 128 * (k + 1))
             image_ref[k] = image_ref[k] + (back_ref[:32, at] + back_ref[32:, at])
@@ -234,17 +243,19 @@
     core = lax.axis_index("c")
     lane = lax.broadcasted_iota(jnp.int32, (8, 128), 1)
 
-    def multiply(columns_of, both_times, square_times):
+    def multiply(step, columns_of, both_times, square_times, beside=None):
         product = jnp.zeros((32, 128), F32)
         square = jnp.zeros((32, 128), F32)
-        for r in range(2 * HALF // ROWS):
-            strip = slice(ROWS * r, ROWS * (r + 1))
+        for r in range(2 * HALF // step):
+            strip = slice(step * r, step * (r + 1))
             at, first = columns_of(strip)
+            if beside is not None:
+                beside(r, 2 * HALF // step)
             total = block(
                 left_ref, flat_ref, right_ref, vec_ref, back_ref, strip, at, at.start, first
             )
-            for n in range(ROWS // 128):
-                k = ROWS // 128 * r + n
+            for n in range(step // 128):
+                k = step // 128 * r + n
                 both = total[128 * n : 128 * (n + 1)].T
                 cross = both[:32] + both[32:]
                 rows = rows_ref[k]
@@ -272,19 +283,26 @@
         for n in range(TILES // 2):
             at = slice(128 * n, 128 * n + 128)
             set_columns(right_ref, vec_ref, at, half_points_of(other_ref, n, 8))
-        multiply(lambda strip: (slice(0, HALF), strip.start == 0), 2.0, 0)
         blank = jnp.zeros((8, 64), F32)
-        for given, ref in ((back_in_ref, low_ref), (back_ref, far_ref)):
-            for k in range(TILES // 2):
-                at = slice(k * 128, (k + 1) * 128)
-                image = given[:32, at] + given[32:, at]
-                for xh in range(2):
-                    top, low = image[16 * xh : 16 * xh + 8], image[16 * xh + 8 : 16 * xh + 16]
-                    for j in range(4):
-                        at = slice(32 * j, 32 * j + 32)
-                        ref[CHIPS * xh + 4 * k + j] = jnp.concatenate(
-                            [top[:, at], low[:, at], blank], axis=1
-                        )
+
+        def give_part(given, ref, k):
+            at = slice(k * 128, (k + 1) * 128)
+            image = given[:32, at] + given[32:, at]
+            for xh in range(2):
+                top, low = image[16 * xh : 16 * xh + 8], image[16 * xh + 8 : 16 * xh + 16]
+                for j in range(4):
+                    at = slice(32 * j, 32 * j + 32)
+                    ref[CHIPS * xh + 4 * k + j] = jnp.concatenate(
+                        [top[:, at], low[:, at], blank], axis=1
+                    )
+
+        def beside(r, steps):
+            for k in range(r * (TILES // 2) // steps, (r + 1) * (TILES // 2) // steps):
+                give_part(back_in_ref, low_ref, k)
+
+        multiply(PAIR_ROWS, lambda strip: (slice(0, HALF), strip.start == 0), 2.0, 0, beside)
+        for k in range(TILES // 2):
+            give_part(back_ref, far_ref, k)
 
     @pl.when(jnp.logical_not(pair))
     def _():
@@ -299,7 +317,7 @@
             start = strip.start // HALF * HALF
             return slice(start, start + HALF), strip.start == start
 
-        multiply(columns_of, 1.0, 1)
+        multiply(ROWS, columns_of, 1.0, 1)
         low_ref[...] = jnp.zeros_like(low_ref)
         for k in range(TILES):
             both = back_ref[:, place(k)]
@@ -381,7 +399,7 @@
     swap = [(0, 1), (1, 0)]
     sent = pl.pallas_call(
         pack_kernel,
-        out_shape=jax.ShapeDtypeStruct((PEERS, 24, 128), F32),
+        out_shape=pltpu.VMEM((PEERS, 24, 128), F32),
         in_specs=[hbm] * 5,
         scratch_shapes=[
             pltpu.VMEM(encodings.shape, BF16),

time: 60.8 us -> 59.6 us (0.980)
  Pallas kernels: 12.1 us -> 10.7 us
    pallas_call x1, Pallas kernels: 3 us -> 2.11 us  [on_device(): pl.pallas_call(pack_kernel, out_shape=pltpu.VMEM((PEERS, 24, 128), F32),...]
where the time goes in v8:
time: 59.6 us; the launch traced here: 58.7 us
  blocking collectives  42.9 us (72%)
  Pallas kernels  10.7 us (18%)
  starting transfers between devices  2.89 us (5%)
  between operations  1.98 us (3%)
    all_to_all x1, blocking collectives, on_device(): own = lax.all_to_all(sent, ('xh', 'g'), 0, 0, tiled=True)  25.4 us
    all_to_all x1, blocking collectives, on_device(): got = lax.all_to_all(partial, ('xh', 'g'), 0, 0, tiled=True)  17.5 us
    pallas_call x1, Pallas kernels, on_device(): pl.pallas_call(far_kernel, out_shape=tuple((jax.ShapeDtypeStruct((n, 8, 1...  3.78 us
    pallas_call x1, Pallas kernels, on_device(): pl.pallas_call(near_kernel, out_shape=(jax.ShapeDtypeStruct((2 * HALF, DE...  3.63 us
    ppermute x1, starting transfers between devices, on_device(): other = lax.ppermute(own[:, 8:], 'c', swap)  2.79 us
    pallas_call x1, Pallas kernels, on_device(): pl.pallas_call(pack_kernel, out_shape=pltpu.VMEM((PEERS, 24, 128), F32),...  2.11 us
  transfers between devices with their start and end apart: 2, of which 1 were waited for; matrix products, arithmetic and copies ran while one was open for 0% of the time, Pallas kernels for 6%

profile of v8, /device:TPU:1, one launch (start us, length us, event | category | flops | bytes accessed | tf_op | source)
XLA Modules:
  0.0 58.7 jit_solution(12601895742161175737)
XLA Ops:
  0.6 2.1 %features.1 = f32[64,24,128]{2,1,0:T(8,128)S(1)} custom-call(bf16[256,1024]{1,0:T(8,128)(2,1)} %enc_hbm.1, bf16[1024,512]{1,0:T(8,128)(2,1)} %w1_hbm.1, bf16[32,512]{1,0:T(8,128)(2,1)} %bitcast.2, f32[1,32]{1,0:T(1,128)} %bitcast.3, f32[16,512]{1,0:T(8,128)} %rhs_ref.1), custom_call_target="tpu_custom_call" | custom-call | tf_op jit(solution)/shard_map/features/pallas_call | solution.py:400
  2.8 25.4 %all_to_all.10.own_ref = f32[64,24,128]{2,1,0:T(8,128)S(1)} all-to-all(f32[64,24,128]{2,1,0:T(8,128)S(1)} %features.1), channel_id=1, replica_groups=mesh['g'=32,'c'=2,'xh'=2] {'xh','g'}, dimensions={0} | all-to-all | bytes 1572864 | tf_op jit(solution)/shard_map/all_to_all | solution.py:417
  28.2 2.8 %collective-permute-start = (f32[64,16,128]{2,1,0:T(8,128)S(1)}, f32[64,16,128]{2,1,0:T(8,128)S(1)}, u32[]{:S(2)}, u32[]{:S(2)}) collective-permute-start(f32[64,16,128]{2,1,0:T(8,128)S(1)} %slice.4), channel_id=1, source_target_pairs={{0,2},{2,0},{1,3},{3,1},{4,6},{6,4},{5,7},{7,5},{8,10},{10,8},{9,1... | collective-permute-start | bytes 1572872 | tf_op jit(solution)/shard_map/ppermute | solution.py:418
  30.9 3.6 %own_columns.1 = (bf16[2048,256]{1,0:T(8,128)(2,1)S(1)}, f32[16,32,128]{2,1,0:T(8,128)S(1)}, bf16[64,2048]{1,0:T(8,128)(2,1)S(1)}, f32[16,32,128]{2,1,0:T(8,128)S(1)}, f32[64,2048]{1,0:T(8,128)S(1)}) custom-call(f32[64,24,128]{2,1,0:T(8,128)S(1)} %all_to_all.10.own_ref), custom_call_target="tpu_custom_call" | custom-call | flops 4294967296 | bytes 1048576 | tf_op jit(solution)/shard_map/own_columns/pallas_call | solution.py:420
  34.6 0.0 collective-permute-done.other_ref
  34.6 3.8 %other_columns.1 = (f32[64,8,128]{2,1,0:T(8,128)S(1)}, f32[64,8,128]{2,1,0:T(8,128)S(1)}, f32[65,8,128]{2,1,0:T(8,128)S(1)}) custom-call(f32[64,16,128]{2,1,0:T(8,128)S(1)} %collective-permute-done.other_ref, bf16[2048,256]{1,0:T(8,128)(2,1)S(1)} %get-tuple-element.10.left_ref, f32[16,32,128]{2,1,0:T(8,128)S(1)} %get-tuple-element.11.rows_ref, ...), custom_call_target="tpu_custom_call" | custom-call | flops 4294967296 | bytes 1048576 | tf_op jit(solution)/shard_map/other_columns/pallas_call | solution.py:437
  38.4 0.1 collective-permute-start.1
  39.8 0.2 collective-permute-done.1.near_ref
  40.0 0.1 join.1
  40.1 0.0 copy-start
  40.1 17.5 %all_to_all.11.got_ref = f32[64,16,128]{2,1,0:T(8,128)S(1)} all-to-all(f32[64,16,128]{2,1,0:T(8,128)S(1)} %join.1), channel_id=1, replica_groups=mesh['g'=32,'c'=2,'xh'=2] {'xh','g'}, dimensions={0} | all-to-all | bytes 1048576 | tf_op jit(solution)/shard_map/all_to_all | solution.py:458
  57.6 0.0 copy-done
  57.6 1.1 %update.1 = (f32[16,512]{1,0:T(8,128)}, f32[16,512]{1,0:T(8,128)}) custom-call(f32[64,16,128]{2,1,0:T(8,128)S(1)} %all_to_all.11.got_ref, f32[16,512]{1,0:T(8,128)S(1)} %copy-done), custom_call_target="tpu_custom_call" | custom-call | tf_op jit(solution)/shard_map/update/pallas_call | solution.py:459
  (1 shorter events, 0.0 us)
Async XLA Ops:
  28.2 6.4 %collective-permute-start = (f32[64,16,128]{2,1,0:T(8,128)S(1)}, f32[64,16,128]{2,1,0:T(8,128)S(1)}, u32[]{:S(2)}, u32[]{:S(2)}) collective-permute-start(f32[64,16,128]{2,1,0:T(8,128)S(1)} %slice.4), channel_id=1, source_target_pairs={{0,2},{2,0},{1,3},{3,1},{4,6},{6,4},{5,7},{7,5},{8,10},{10,8},{9,1... | collective-permute-start | bytes 1572872 | tf_op jit(solution)/shard_map/ppermute | solution.py:418
  38.4 1.6 %collective-permute-start.1 = (f32[65,8,128]{2,1,0:T(8,128)S(1)}, f32[65,8,128]{2,1,0:T(8,128)S(1)}, u32[]{:S(2)}, u32[]{:S(2)}) collective-permute-start(f32[65,8,128]{2,1,0:T(8,128)S(1)} %get-tuple-element.17.far_ref), channel_id=1, source_target_pairs={{0,2},{2,0},{1,3},{3,1},{4,6},{6,4},{5,7},{7,5},{8,10},{10,8},{9,1... | collective-permute-start | bytes 798728 | tf_op jit(solution)/shard_map/ppermute | solution.py:449
  40.1 17.5 %copy-start = (f32[16,512]{1,0:T(8,128)S(1)}, f32[16,512]{1,0:T(8,128)}, u32[]{:S(2)}) copy-start(f32[16,512]{1,0:T(8,128)} %rhs_ref.1) | copy-start | bytes 98308

commit v9 on v8

--- a/solution.py
+++ b/solution.py
@@ -13,6 +13,7 @@
 GROUPS = 8
 WIDTH = 32
 DEPTH = 256
+SHALLOW = 144
 STEPS = 4
 ROWS = 256
 PAIR_ROWS = 512
@@ -136,7 +137,7 @@
     return features, columns
 
 
-def operand(features, left):
+def operand(features, left, depth):
     y1, y2 = halves(features)
     kept = y1.astype(F32) + y2.astype(F32)
     norm = -0.5 * jnp.sum(kept * kept, axis=0, keepdims=True)
@@ -156,23 +157,26 @@
             ),
         ),
     ).astype(BF16)
-    blank = jnp.zeros((DEPTH - 144, features.shape[1]), BF16)
-    parts = [y1, y1, y2, y2] if left else [y1, y2, y1, y2]
-    return jnp.concatenate(parts + [tail, blank], axis=0)
+    parts = ([y1, y1, y2, y2] if left else [y1, y2, y1, y2]) + [tail]
+    if depth > SHALLOW:
+        parts.append(jnp.zeros((depth - SHALLOW, features.shape[1]), BF16))
+    return jnp.concatenate(parts, axis=0)
 
 
 def on_pair():
     return lax.axis_index("xh") * CHIPS + lax.axis_index("g") < len(PAIRS)
 
 
-def set_columns(right_ref, vec_ref, at, points):
+def set_columns(right_ref, vec_ref, at, points, depth):
     features, columns = points
-    right_ref[:, at] = operand(features, False)
+    right_ref[:depth, at] = operand(features, False, depth)
     vec_ref[at, :] = jnp.concatenate(halves(columns), axis=0).T
 
 
-def block(left_ref, flat_ref, right_ref, vec_ref, back_ref, strip, at, back_from, first):
-    exponent = jnp.dot(left_ref[strip, :], right_ref[:, at], preferred_element_type=F32)
+def block(depth, left_ref, flat_ref, right_ref, vec_ref, back_ref, strip, at, back_from, first):
+    exponent = jnp.dot(
+        left_ref[strip, :depth], right_ref[:depth, at], preferred_element_type=F32
+    )
     tile = jnp.exp2(exponent).astype(BF16)
     total = jnp.dot(tile, vec_ref[at, :], preferred_element_type=F32)
     if back_from < at.stop:
@@ -189,14 +193,14 @@
 ):
     pair = on_pair()
 
-    def set_rows(k, points):
+    def set_rows(k, points, depth):
         features, columns = points
         at = slice(k * 128, (k + 1) * 128)
-        left_ref[at, :] = operand(features, True).T
+        left_ref[at, :depth] = operand(features, True, depth).T
         rows_ref[k] = columns
         flat_ref[:, at] = jnp.concatenate(halves(columns), axis=0)
 
-    def multiply(rows, prepare, ranges):
+    def multiply(depth, rows, prepare, ranges):
         for r in range(2 * HALF // rows):
             strip = slice(rows * r, rows * (r + 1))
             ahead = strip.stop + AHEAD
@@ -204,7 +208,8 @@
                 prepare(k)
             at, back_from = ranges(strip)
             total = block(
-                left_ref, flat_ref, right_ref, vec_ref, back_ref, strip, at, back_from, r == 0
+                depth, left_ref, flat_ref, right_ref, vec_ref, back_ref,
+                strip, at, back_from, r == 0,
             )
             for n in range(rows // 128):
                 both = total[128 * n : 128 * (n + 1)].T
@@ -214,10 +219,11 @@
     def _():
         for n in range(TILES // 2):
             at = slice(128 * n, 128 * n + 128)
-            set_columns(right_ref, vec_ref, at, half_points_of(own_ref, n, 16))
+            set_columns(right_ref, vec_ref, at, half_points_of(own_ref, n, 16), DEPTH)
         multiply(
+            DEPTH,
             PAIR_ROWS,
-            lambda k: set_rows(k, points_of(own_ref, k, 0)),
+            lambda k: set_rows(k, points_of(own_ref, k, 0), DEPTH),
             lambda strip: (slice(0, HALF), 0),
         )
 
@@ -225,10 +231,10 @@
     def _():
         for k in range(TILES):
             points = points_of(own_ref, k, 8)
-            set_rows(k, points)
-            set_columns(right_ref, vec_ref, slice(128 * k, 128 * k + 128), points)
+            set_rows(k, points, SHALLOW)
+            set_columns(right_ref, vec_ref, slice(128 * k, 128 * k + 128), points, SHALLOW)
         multiply(
-            ROWS, lambda k: None, lambda strip: (slice(strip.start, 2 * HALF), strip.stop)
+            SHALLOW, ROWS, lambda k: None, lambda strip: (slice(strip.start, 2 * HALF), strip.stop)
         )
         for k in range(ROWS // 128, TILES):
             at = slice(128 * k, 128 * (k + 1))
@@ -243,7 +249,7 @@
     core = lax.axis_index("c")
     lane = lax.broadcasted_iota(jnp.int32, (8, 128), 1)
 
-    def multiply(step, columns_of, both_times, square_times, beside=None):
+    def multiply(depth, step, columns_of, both_times, square_times, beside=None):
         product = jnp.zeros((32, 128), F32)
         square = jnp.zeros((32, 128), F32)
         for r in range(2 * HALF // step):
@@ -252,7 +258,8 @@
             if beside is not None:
                 beside(r, 2 * HALF // step)
             total = block(
-                left_ref, flat_ref, right_ref, vec_ref, back_ref, strip, at, at.start, first
+                depth, left_ref, flat_ref, right_ref, vec_ref, back_ref,
+                strip, at, at.start, first,
             )
             for n in range(step // 128):
                 k = step // 128 * r + n
@@ -282,7 +289,7 @@
     def _():
         for n in range(TILES // 2):
             at = slice(128 * n, 128 * n + 128)
-            set_columns(right_ref, vec_ref, at, half_points_of(other_ref, n, 8))
+            set_columns(right_ref, vec_ref, at, half_points_of(other_ref, n, 8), DEPTH)
         blank = jnp.zeros((8, 64), F32)
 
         def give_part(given, ref, k):
@@ -300,7 +307,7 @@
             for k in range(r * (TILES // 2) // steps, (r + 1) * (TILES // 2) // steps):
                 give_part(back_in_ref, low_ref, k)
 
-        multiply(PAIR_ROWS, lambda strip: (slice(0, HALF), strip.start == 0), 2.0, 0, beside)
+        multiply(DEPTH, PAIR_ROWS, lambda strip: (slice(0, HALF), strip.start == 0), 2.0, 0, beside)
         for k in range(TILES // 2):
             give_part(back_ref, far_ref, k)
 
@@ -311,13 +318,13 @@
             return pl.ds(pl.multiple_of(half * HALF + k % (TILES // 2) * 128, 128), 128)
 
         for k in range(TILES):
-            set_columns(right_ref, vec_ref, place(k), points_of(other_ref, k, 0))
+            set_columns(right_ref, vec_ref, place(k), points_of(other_ref, k, 0), SHALLOW)
 
         def columns_of(strip):
             start = strip.start // HALF * HALF
             return slice(start, start + HALF), strip.start == start
 
-        multiply(ROWS, columns_of, 1.0, 1)
+        multiply(SHALLOW, ROWS, columns_of, 1.0, 1)
         low_ref[...] = jnp.zeros_like(low_ref)
         for k in range(TILES):
             both = back_ref[:, place(k)]

time: 59.6 us -> 59.1 us (level)
  no operation moved by 1% of the time
where the time goes in v9:
time: 59.1 us; the launch traced here: 58.2 us
  blocking collectives  42.4 us (72%)
  Pallas kernels  10.7 us (18%)
  starting transfers between devices  2.89 us (5%)
  between operations  1.98 us (3%)
    all_to_all x1, blocking collectives, on_device(): own = lax.all_to_all(sent, ('xh', 'g'), 0, 0, tiled=True)  25.4 us
    all_to_all x1, blocking collectives, on_device(): got = lax.all_to_all(partial, ('xh', 'g'), 0, 0, tiled=True)  17 us
    pallas_call x1, Pallas kernels, on_device(): pl.pallas_call(far_kernel, out_shape=tuple((jax.ShapeDtypeStruct((n, 8, 1...  3.78 us
    pallas_call x1, Pallas kernels, on_device(): pl.pallas_call(near_kernel, out_shape=(jax.ShapeDtypeStruct((2 * HALF, DE...  3.63 us
    ppermute x1, starting transfers between devices, on_device(): other = lax.ppermute(own[:, 8:], 'c', swap)  2.79 us
    pallas_call x1, Pallas kernels, on_device(): pl.pallas_call(pack_kernel, out_shape=pltpu.VMEM((PEERS, 24, 128), F32),...  2.11 us
  transfers between devices with their start and end apart: 2, of which 1 were waited for; matrix products, arithmetic and copies ran while one was open for 0% of the time, Pallas kernels for 6%

profile of v9, /device:TPU:1, one launch (start us, length us, event | category | flops | bytes accessed | tf_op | source)
XLA Modules:
  0.0 58.2 jit_solution(14919431194828960082)
XLA Ops:
  0.6 2.1 %features.1 = f32[64,24,128]{2,1,0:T(8,128)S(1)} custom-call(bf16[256,1024]{1,0:T(8,128)(2,1)} %enc_hbm.1, bf16[1024,512]{1,0:T(8,128)(2,1)} %w1_hbm.1, bf16[32,512]{1,0:T(8,128)(2,1)} %bitcast.2, f32[1,32]{1,0:T(1,128)} %bitcast.3, f32[16,512]{1,0:T(8,128)} %rhs_ref.1), custom_call_target="tpu_custom_call" | custom-call | tf_op jit(solution)/shard_map/features/pallas_call | solution.py:407
  2.8 25.4 %all_to_all.10.own_ref = f32[64,24,128]{2,1,0:T(8,128)S(1)} all-to-all(f32[64,24,128]{2,1,0:T(8,128)S(1)} %features.1), channel_id=1, replica_groups=mesh['g'=32,'c'=2,'xh'=2] {'xh','g'}, dimensions={0} | all-to-all | bytes 1572864 | tf_op jit(solution)/shard_map/all_to_all | solution.py:424
  28.2 2.8 %collective-permute-start = (f32[64,16,128]{2,1,0:T(8,128)S(1)}, f32[64,16,128]{2,1,0:T(8,128)S(1)}, u32[]{:S(2)}, u32[]{:S(2)}) collective-permute-start(f32[64,16,128]{2,1,0:T(8,128)S(1)} %slice.4), channel_id=1, source_target_pairs={{0,2},{2,0},{1,3},{3,1},{4,6},{6,4},{5,7},{7,5},{8,10},{10,8},{9,1... | collective-permute-start | bytes 1572872 | tf_op jit(solution)/shard_map/ppermute | solution.py:425
  30.9 3.6 %own_columns.1 = (bf16[2048,256]{1,0:T(8,128)(2,1)S(1)}, f32[16,32,128]{2,1,0:T(8,128)S(1)}, bf16[64,2048]{1,0:T(8,128)(2,1)S(1)}, f32[16,32,128]{2,1,0:T(8,128)S(1)}, f32[64,2048]{1,0:T(8,128)S(1)}) custom-call(f32[64,24,128]{2,1,0:T(8,128)S(1)} %all_to_all.10.own_ref), custom_call_target="tpu_custom_call" | custom-call | flops 4294967296 | bytes 1048576 | tf_op jit(solution)/shard_map/own_columns/pallas_call | solution.py:427
  34.6 0.0 collective-permute-done.other_ref
  34.6 3.8 %other_columns.1 = (f32[64,8,128]{2,1,0:T(8,128)S(1)}, f32[64,8,128]{2,1,0:T(8,128)S(1)}, f32[65,8,128]{2,1,0:T(8,128)S(1)}) custom-call(f32[64,16,128]{2,1,0:T(8,128)S(1)} %collective-permute-done.other_ref, bf16[2048,256]{1,0:T(8,128)(2,1)S(1)} %get-tuple-element.10.left_ref, f32[16,32,128]{2,1,0:T(8,128)S(1)} %get-tuple-element.11.rows_ref, ...), custom_call_target="tpu_custom_call" | custom-call | flops 4294967296 | bytes 1048576 | tf_op jit(solution)/shard_map/other_columns/pallas_call | solution.py:444
  38.4 0.1 collective-permute-start.1
  39.8 0.2 collective-permute-done.1.near_ref
  40.0 0.1 join.1
  40.1 0.0 copy-start
  40.1 17.0 %all_to_all.11.got_ref = f32[64,16,128]{2,1,0:T(8,128)S(1)} all-to-all(f32[64,16,128]{2,1,0:T(8,128)S(1)} %join.1), channel_id=1, replica_groups=mesh['g'=32,'c'=2,'xh'=2] {'xh','g'}, dimensions={0} | all-to-all | bytes 1048576 | tf_op jit(solution)/shard_map/all_to_all | solution.py:465
  57.1 0.0 copy-done
  57.1 1.1 %update.1 = (f32[16,512]{1,0:T(8,128)}, f32[16,512]{1,0:T(8,128)}) custom-call(f32[64,16,128]{2,1,0:T(8,128)S(1)} %all_to_all.11.got_ref, f32[16,512]{1,0:T(8,128)S(1)} %copy-done), custom_call_target="tpu_custom_call" | custom-call | tf_op jit(solution)/shard_map/update/pallas_call | solution.py:466
  (1 shorter events, 0.0 us)
Async XLA Ops:
  28.2 6.4 %collective-permute-start = (f32[64,16,128]{2,1,0:T(8,128)S(1)}, f32[64,16,128]{2,1,0:T(8,128)S(1)}, u32[]{:S(2)}, u32[]{:S(2)}) collective-permute-start(f32[64,16,128]{2,1,0:T(8,128)S(1)} %slice.4), channel_id=1, source_target_pairs={{0,2},{2,0},{1,3},{3,1},{4,6},{6,4},{5,7},{7,5},{8,10},{10,8},{9,1... | collective-permute-start | bytes 1572872 | tf_op jit(solution)/shard_map/ppermute | solution.py:425
  38.4 1.6 %collective-permute-start.1 = (f32[65,8,128]{2,1,0:T(8,128)S(1)}, f32[65,8,128]{2,1,0:T(8,128)S(1)}, u32[]{:S(2)}, u32[]{:S(2)}) collective-permute-start(f32[65,8,128]{2,1,0:T(8,128)S(1)} %get-tuple-element.17.far_ref), channel_id=1, source_target_pairs={{0,2},{2,0},{1,3},{3,1},{4,6},{6,4},{5,7},{7,5},{8,10},{10,8},{9,1... | collective-permute-start | bytes 798728 | tf_op jit(solution)/shard_map/ppermute | solution.py:456
  40.1 17.0 %copy-start = (f32[16,512]{1,0:T(8,128)S(1)}, f32[16,512]{1,0:T(8,128)}, u32[]{:S(2)}) copy-start(f32[16,512]{1,0:T(8,128)} %rhs_ref.1) | copy-start | bytes 98308

commit v10 on v9

--- a/solution.py
+++ b/solution.py
@@ -170,7 +170,11 @@
 def set_columns(right_ref, vec_ref, at, points, depth):
     features, columns = points
     right_ref[:depth, at] = operand(features, False, depth)
-    vec_ref[at, :] = jnp.concatenate(halves(columns), axis=0).T
+    parts = jnp.concatenate(halves(columns), axis=0)
+    if vec_ref.shape[0] == 64:
+        vec_ref[:, at] = parts
+    else:
+        vec_ref[at, :] = parts.T
 
 
 def block(depth, left_ref, flat_ref, right_ref, vec_ref, back_ref, strip, at, back_from, first):
@@ -178,7 +182,12 @@
         left_ref[strip, :depth], right_ref[:depth, at], preferred_element_type=F32
     )
     tile = jnp.exp2(exponent).astype(BF16)
-    total = jnp.dot(tile, vec_ref[at, :], preferred_element_type=F32)
+    if vec_ref.shape[0] == 64:
+        total = lax.dot_general(
+            vec_ref[:, at], tile, (((1,), (1,)), ((), ())), preferred_element_type=F32
+        )
+    else:
+        total = jnp.dot(tile, vec_ref[at, :], preferred_element_type=F32).T
     if back_from < at.stop:
         to = slice(back_from, at.stop)
         back = jnp.dot(
@@ -189,7 +198,7 @@
 
 
 def near_kernel(
-    own_ref, left_ref, rows_ref, flat_ref, image_ref, back_ref, right_ref, vec_ref
+    own_ref, left_ref, rows_ref, flat_ref, image_ref, back_ref, right_ref, vec_ref, line_ref
 ):
     pair = on_pair()
 
@@ -200,7 +209,7 @@
         rows_ref[k] = columns
         flat_ref[:, at] = jnp.concatenate(halves(columns), axis=0)
 
-    def multiply(depth, rows, prepare, ranges):
+    def multiply(vec_ref, depth, rows, prepare, ranges):
         for r in range(2 * HALF // rows):
             strip = slice(rows * r, rows * (r + 1))
             ahead = strip.stop + AHEAD
@@ -212,17 +221,18 @@
                 strip, at, back_from, r == 0,
             )
             for n in range(rows // 128):
-                both = total[128 * n : 128 * (n + 1)].T
+                both = total[:, 128 * n : 128 * (n + 1)]
                 image_ref[rows // 128 * r + n] = both[:32] + both[32:]
 
     @pl.when(pair)
     def _():
         for n in range(TILES // 2):
             at = slice(128 * n, 128 * n + 128)
-            set_columns(right_ref, vec_ref, at, half_points_of(own_ref, n, 16), DEPTH)
+            set_columns(right_ref, line_ref, at, half_points_of(own_ref, n, 16), DEPTH)
         multiply(
+            line_ref,
             DEPTH,
-            PAIR_ROWS,
+            ROWS,
             lambda k: set_rows(k, points_of(own_ref, k, 0), DEPTH),
             lambda strip: (slice(0, HALF), 0),
         )
@@ -234,7 +244,7 @@
             set_rows(k, points, SHALLOW)
             set_columns(right_ref, vec_ref, slice(128 * k, 128 * k + 128), points, SHALLOW)
         multiply(
-            SHALLOW, ROWS, lambda k: None, lambda strip: (slice(strip.start, 2 * HALF), strip.stop)
+            vec_ref, SHALLOW, ROWS, lambda k: None, lambda strip: (slice(strip.start, 2 * HALF), strip.stop)
         )
         for k in range(ROWS // 128, TILES):
             at = slice(128 * k, 128 * (k + 1))
@@ -243,13 +253,13 @@
 
 def far_kernel(
     other_ref, left_ref, rows_ref, flat_ref, image_ref, back_in_ref,
-    whole_ref, low_ref, far_ref, right_ref, vec_ref, back_ref,
+    whole_ref, low_ref, far_ref, right_ref, vec_ref, line_ref, back_ref,
 ):
     pair = on_pair()
     core = lax.axis_index("c")
     lane = lax.broadcasted_iota(jnp.int32, (8, 128), 1)
 
-    def multiply(depth, step, columns_of, both_times, square_times, beside=None):
+    def multiply(vec_ref, depth, step, columns_of, both_times, square_times, beside=None):
         product = jnp.zeros((32, 128), F32)
         square = jnp.zeros((32, 128), F32)
         for r in range(2 * HALF // step):
@@ -263,7 +273,7 @@
             )
             for n in range(step // 128):
                 k = step // 128 * r + n
-                both = total[128 * n : 128 * (n + 1)].T
+                both = total[:, 128 * n : 128 * (n + 1)]
                 cross = both[:32] + both[32:]
                 rows = rows_ref[k]
                 product = product + rows * (both_times * image_ref[k] + 2.0 * cross)
@@ -289,7 +299,7 @@
     def _():
         for n in range(TILES // 2):
             at = slice(128 * n, 128 * n + 128)
-            set_columns(right_ref, vec_ref, at, half_points_of(other_ref, n, 8), DEPTH)
+            set_columns(right_ref, line_ref, at, half_points_of(other_ref, n, 8), DEPTH)
         blank = jnp.zeros((8, 64), F32)
 
         def give_part(given, ref, k):
@@ -307,7 +317,7 @@
             for k in range(r * (TILES // 2) // steps, (r + 1) * (TILES // 2) // steps):
                 give_part(back_in_ref, low_ref, k)
 
-        multiply(DEPTH, PAIR_ROWS, lambda strip: (slice(0, HALF), strip.start == 0), 2.0, 0, beside)
+        multiply(line_ref, DEPTH, PAIR_ROWS, lambda strip: (slice(0, HALF), strip.start == 0), 2.0, 0, beside)
         for k in range(TILES // 2):
             give_part(back_ref, far_ref, k)
 
@@ -324,7 +334,7 @@
             start = strip.start // HALF * HALF
             return slice(start, start + HALF), strip.start == start
 
-        multiply(SHALLOW, ROWS, columns_of, 1.0, 1)
+        multiply(vec_ref, SHALLOW, ROWS, columns_of, 1.0, 1)
         low_ref[...] = jnp.zeros_like(low_ref)
         for k in range(TILES):
             both = back_ref[:, place(k)]
@@ -436,6 +446,7 @@
         scratch_shapes=[
             pltpu.VMEM((DEPTH, 2 * HALF), BF16),
             pltpu.VMEM((2 * HALF, 64), BF16),
+            pltpu.VMEM((64, HALF), BF16),
         ],
         compiler_params=pltpu.CompilerParams(vmem_limit_bytes=24 << 20),
         cost_estimate=cost,
@@ -447,6 +458,7 @@
         scratch_shapes=[
             pltpu.VMEM((DEPTH, 2 * HALF), BF16),
             pltpu.VMEM((2 * HALF, 64), BF16),
+            pltpu.VMEM((64, HALF), BF16),
             pltpu.VMEM((64, 2 * HALF), F32),
         ],
         compiler_params=pltpu.CompilerParams(vmem_limit_bytes=24 << 20),

time: 59.1 us -> 59.1 us (level)
  no operation moved by 1% of the time
where the time goes in v10:
time: 59.1 us; the launch traced here: 58.3 us
  blocking collectives  42.6 us (72%)
  Pallas kernels  10.5 us (18%)
  starting transfers between devices  2.88 us (5%)
  between operations  1.98 us (3%)
    all_to_all x1, blocking collectives, on_device(): own = lax.all_to_all(sent, ('xh', 'g'), 0, 0, tiled=True)  25.4 us
    all_to_all x1, blocking collectives, on_device(): got = lax.all_to_all(partial, ('xh', 'g'), 0, 0, tiled=True)  17.3 us
    pallas_call x1, Pallas kernels, on_device(): pl.pallas_call(far_kernel, out_shape=tuple((jax.ShapeDtypeStruct((n, 8, 1...  3.66 us
    pallas_call x1, Pallas kernels, on_device(): pl.pallas_call(near_kernel, out_shape=(jax.ShapeDtypeStruct((2 * HALF, DE...  3.54 us
    ppermute x1, starting transfers between devices, on_device(): other = lax.ppermute(own[:, 8:], 'c', swap)  2.79 us
    pallas_call x1, Pallas kernels, on_device(): pl.pallas_call(pack_kernel, out_shape=pltpu.VMEM((PEERS, 24, 128), F32),...  2.11 us
  transfers between devices with their start and end apart: 2, of which 1 were waited for; matrix products, arithmetic and copies ran while one was open for 0% of the time, Pallas kernels for 6%

profile of v10, /device:TPU:1, one launch (start us, length us, event | category | flops | bytes accessed | tf_op | source)
XLA Modules:
  0.0 58.3 jit_solution(6918235722667196665)
XLA Ops:
  0.6 2.1 %features.1 = f32[64,24,128]{2,1,0:T(8,128)S(1)} custom-call(bf16[256,1024]{1,0:T(8,128)(2,1)} %enc_hbm.1, bf16[1024,512]{1,0:T(8,128)(2,1)} %w1_hbm.1, bf16[32,512]{1,0:T(8,128)(2,1)} %bitcast.2, f32[1,32]{1,0:T(1,128)} %bitcast.3, f32[16,512]{1,0:T(8,128)} %rhs_ref.1), custom_call_target="tpu_custom_call" | custom-call | tf_op jit(solution)/shard_map/features/pallas_call | solution.py:417
  2.8 25.4 %all_to_all.10.own_ref = f32[64,24,128]{2,1,0:T(8,128)S(1)} all-to-all(f32[64,24,128]{2,1,0:T(8,128)S(1)} %features.1), channel_id=1, replica_groups=mesh['g'=32,'c'=2,'xh'=2] {'xh','g'}, dimensions={0} | all-to-all | bytes 1572864 | tf_op jit(solution)/shard_map/all_to_all | solution.py:434
  28.2 2.8 %collective-permute-start = (f32[64,16,128]{2,1,0:T(8,128)S(1)}, f32[64,16,128]{2,1,0:T(8,128)S(1)}, u32[]{:S(2)}, u32[]{:S(2)}) collective-permute-start(f32[64,16,128]{2,1,0:T(8,128)S(1)} %slice.4), channel_id=1, source_target_pairs={{0,2},{2,0},{1,3},{3,1},{4,6},{6,4},{5,7},{7,5},{8,10},{10,8},{9,1... | collective-permute-start | bytes 1572872 | tf_op jit(solution)/shard_map/ppermute | solution.py:435
  30.9 3.5 %own_columns.1 = (bf16[2048,256]{1,0:T(8,128)(2,1)S(1)}, f32[16,32,128]{2,1,0:T(8,128)S(1)}, bf16[64,2048]{1,0:T(8,128)(2,1)S(1)}, f32[16,32,128]{2,1,0:T(8,128)S(1)}, f32[64,2048]{1,0:T(8,128)S(1)}) custom-call(f32[64,24,128]{2,1,0:T(8,128)S(1)} %all_to_all.10.own_ref), custom_call_target="tpu_custom_call" | custom-call | flops 4294967296 | bytes 1048576 | tf_op jit(solution)/shard_map/own_columns/pallas_call | solution.py:437
  34.5 0.0 collective-permute-done.other_ref
  34.5 3.7 %other_columns.1 = (f32[64,8,128]{2,1,0:T(8,128)S(1)}, f32[64,8,128]{2,1,0:T(8,128)S(1)}, f32[65,8,128]{2,1,0:T(8,128)S(1)}) custom-call(f32[64,16,128]{2,1,0:T(8,128)S(1)} %collective-permute-done.other_ref, bf16[2048,256]{1,0:T(8,128)(2,1)S(1)} %get-tuple-element.10.left_ref, f32[16,32,128]{2,1,0:T(8,128)S(1)} %get-tuple-element.11.rows_ref, ...), custom_call_target="tpu_custom_call" | custom-call | flops 4294967296 | bytes 1048576 | tf_op jit(solution)/shard_map/other_columns/pallas_call | solution.py:455
  38.2 0.1 collective-permute-start.1
  39.6 0.2 collective-permute-done.1.near_ref
  39.8 0.1 join.1
  39.9 0.0 copy-start
  39.9 17.3 %all_to_all.11.got_ref = f32[64,16,128]{2,1,0:T(8,128)S(1)} all-to-all(f32[64,16,128]{2,1,0:T(8,128)S(1)} %join.1), channel_id=1, replica_groups=mesh['g'=32,'c'=2,'xh'=2] {'xh','g'}, dimensions={0} | all-to-all | bytes 1048576 | tf_op jit(solution)/shard_map/all_to_all | solution.py:477
  57.1 0.0 copy-done
  57.1 1.1 %update.1 = (f32[16,512]{1,0:T(8,128)}, f32[16,512]{1,0:T(8,128)}) custom-call(f32[64,16,128]{2,1,0:T(8,128)S(1)} %all_to_all.11.got_ref, f32[16,512]{1,0:T(8,128)S(1)} %copy-done), custom_call_target="tpu_custom_call" | custom-call | tf_op jit(solution)/shard_map/update/pallas_call | solution.py:478
  (1 shorter events, 0.0 us)
Async XLA Ops:
  28.2 6.3 %collective-permute-start = (f32[64,16,128]{2,1,0:T(8,128)S(1)}, f32[64,16,128]{2,1,0:T(8,128)S(1)}, u32[]{:S(2)}, u32[]{:S(2)}) collective-permute-start(f32[64,16,128]{2,1,0:T(8,128)S(1)} %slice.4), channel_id=1, source_target_pairs={{0,2},{2,0},{1,3},{3,1},{4,6},{6,4},{5,7},{7,5},{8,10},{10,8},{9,1... | collective-permute-start | bytes 1572872 | tf_op jit(solution)/shard_map/ppermute | solution.py:435
  38.2 1.6 %collective-permute-start.1 = (f32[65,8,128]{2,1,0:T(8,128)S(1)}, f32[65,8,128]{2,1,0:T(8,128)S(1)}, u32[]{:S(2)}, u32[]{:S(2)}) collective-permute-start(f32[65,8,128]{2,1,0:T(8,128)S(1)} %get-tuple-element.17.far_ref), channel_id=1, source_target_pairs={{0,2},{2,0},{1,3},{3,1},{4,6},{6,4},{5,7},{7,5},{8,10},{10,8},{9,1... | collective-permute-start | bytes 798728 | tf_op jit(solution)/shard_map/ppermute | solution.py:468
  39.9 17.3 %copy-start = (f32[16,512]{1,0:T(8,128)S(1)}, f32[16,512]{1,0:T(8,128)}, u32[]{:S(2)}) copy-start(f32[16,512]{1,0:T(8,128)} %rhs_ref.1) | copy-start | bytes 98308

commit v11 on v9

--- a/solution.py
+++ b/solution.py
@@ -15,8 +15,8 @@
 DEPTH = 256
 SHALLOW = 144
 STEPS = 4
-ROWS = 256
-PAIR_ROWS = 512
+FEW_ROWS = 256
+ROWS = 512
 AHEAD = 0
 PAIRS = [(a, b, t) for a in range(GROUPS) for b in range(a + 1, GROUPS) for t in range(2)]
 TILES = CHIPS // 2
@@ -167,18 +167,20 @@
     return lax.axis_index("xh") * CHIPS + lax.axis_index("g") < len(PAIRS)
 
 
-def set_columns(right_ref, vec_ref, at, points, depth):
+def set_columns(right_ref, line_ref, at, points, depth):
     features, columns = points
     right_ref[:depth, at] = operand(features, False, depth)
-    vec_ref[at, :] = jnp.concatenate(halves(columns), axis=0).T
-
-
-def block(depth, left_ref, flat_ref, right_ref, vec_ref, back_ref, strip, at, back_from, first):
+    line_ref[:, at] = jnp.concatenate(halves(columns), axis=0)
+
+
+def block(depth, left_ref, flat_ref, right_ref, line_ref, back_ref, strip, at, back_from, first):
     exponent = jnp.dot(
         left_ref[strip, :depth], right_ref[:depth, at], preferred_element_type=F32
     )
     tile = jnp.exp2(exponent).astype(BF16)
-    total = jnp.dot(tile, vec_ref[at, :], preferred_element_type=F32)
+    total = lax.dot_general(
+        line_ref[:, at], tile, (((1,), (1,)), ((), ())), preferred_element_type=F32
+    )
     if back_from < at.stop:
         to = slice(back_from, at.stop)
         back = jnp.dot(
@@ -189,7 +191,7 @@
 
 
 def near_kernel(
-    own_ref, left_ref, rows_ref, flat_ref, image_ref, back_ref, right_ref, vec_ref
+    own_ref, left_ref, rows_ref, flat_ref, image_ref, back_ref, right_ref, line_ref
 ):
     pair = on_pair()
 
@@ -200,7 +202,7 @@
         rows_ref[k] = columns
         flat_ref[:, at] = jnp.concatenate(halves(columns), axis=0)
 
-    def multiply(depth, rows, prepare, ranges):
+    def multiply(line_ref, depth, rows, prepare, ranges):
         for r in range(2 * HALF // rows):
             strip = slice(rows * r, rows * (r + 1))
             ahead = strip.stop + AHEAD
@@ -208,21 +210,22 @@
                 prepare(k)
             at, back_from = ranges(strip)
             total = block(
-                depth, left_ref, flat_ref, right_ref, vec_ref, back_ref,
+                depth, left_ref, flat_ref, right_ref, line_ref, back_ref,
                 strip, at, back_from, r == 0,
             )
             for n in range(rows // 128):
-                both = total[128 * n : 128 * (n + 1)].T
+                both = total[:, 128 * n : 128 * (n + 1)]
                 image_ref[rows // 128 * r + n] = both[:32] + both[32:]
 
     @pl.when(pair)
     def _():
         for n in range(TILES // 2):
             at = slice(128 * n, 128 * n + 128)
-            set_columns(right_ref, vec_ref, at, half_points_of(own_ref, n, 16), DEPTH)
+            set_columns(right_ref, line_ref, at, half_points_of(own_ref, n, 16), DEPTH)
         multiply(
+            line_ref,
             DEPTH,
-            PAIR_ROWS,
+            FEW_ROWS,
             lambda k: set_rows(k, points_of(own_ref, k, 0), DEPTH),
             lambda strip: (slice(0, HALF), 0),
         )
@@ -232,9 +235,9 @@
         for k in range(TILES):
             points = points_of(own_ref, k, 8)
             set_rows(k, points, SHALLOW)
-            set_columns(right_ref, vec_ref, slice(128 * k, 128 * k + 128), points, SHALLOW)
+            right_ref[:SHALLOW, 128 * k : 128 * k + 128] = operand(points[0], False, SHALLOW)
         multiply(
-            SHALLOW, ROWS, lambda k: None, lambda strip: (slice(strip.start, 2 * HALF), strip.stop)
+            flat_ref, SHALLOW, ROWS, lambda k: None, lambda strip: (slice(strip.start, 2 * HALF), strip.stop)
         )
         for k in range(ROWS // 128, TILES):
             at = slice(128 * k, 128 * (k + 1))
@@ -243,7 +246,7 @@
 
 def far_kernel(
     other_ref, left_ref, rows_ref, flat_ref, image_ref, back_in_ref,
-    whole_ref, low_ref, far_ref, right_ref, vec_ref, back_ref,
+    whole_ref, low_ref, far_ref, right_ref, line_ref, back_ref,
 ):
     pair = on_pair()
     core = lax.axis_index("c")
@@ -258,12 +261,12 @@
             if beside is not None:
                 beside(r, 2 * HALF // step)
             total = block(
-                depth, left_ref, flat_ref, right_ref, vec_ref, back_ref,
+                depth, left_ref, flat_ref, right_ref, line_ref, back_ref,
                 strip, at, at.start, first,
             )
             for n in range(step // 128):
                 k = step // 128 * r + n
-                both = total[128 * n : 128 * (n + 1)].T
+                both = total[:, 128 * n : 128 * (n + 1)]
                 cross = both[:32] + both[32:]
                 rows = rows_ref[k]
                 product = product + rows * (both_times * image_ref[k] + 2.0 * cross)
@@ -289,7 +292,7 @@
     def _():
         for n in range(TILES // 2):
             at = slice(128 * n, 128 * n + 128)
-            set_columns(right_ref, vec_ref, at, half_points_of(other_ref, n, 8), DEPTH)
+            set_columns(right_ref, line_ref, at, half_points_of(other_ref, n, 8), DEPTH)
         blank = jnp.zeros((8, 64), F32)
 
         def give_part(given, ref, k):
@@ -307,7 +310,7 @@
             for k in range(r * (TILES // 2) // steps, (r + 1) * (TILES // 2) // steps):
                 give_part(back_in_ref, low_ref, k)
 
-        multiply(DEPTH, PAIR_ROWS, lambda strip: (slice(0, HALF), strip.start == 0), 2.0, 0, beside)
+        multiply(DEPTH, ROWS, lambda strip: (slice(0, HALF), strip.start == 0), 2.0, 0, beside)
         for k in range(TILES // 2):
             give_part(back_ref, far_ref, k)
 
@@ -318,7 +321,7 @@
             return pl.ds(pl.multiple_of(half * HALF + k % (TILES // 2) * 128, 128), 128)
 
         for k in range(TILES):
-            set_columns(right_ref, vec_ref, place(k), points_of(other_ref, k, 0), SHALLOW)
+            set_columns(right_ref, line_ref, place(k), points_of(other_ref, k, 0), SHALLOW)
 
         def columns_of(strip):
             start = strip.start // HALF * HALF
@@ -435,7 +438,7 @@
         ),
         scratch_shapes=[
             pltpu.VMEM((DEPTH, 2 * HALF), BF16),
-            pltpu.VMEM((2 * HALF, 64), BF16),
+            pltpu.VMEM((64, 2 * HALF), BF16),
         ],
         compiler_params=pltpu.CompilerParams(vmem_limit_bytes=24 << 20),
         cost_estimate=cost,
@@ -446,7 +449,7 @@
         out_shape=tuple(jax.ShapeDtypeStruct((n, 8, 128), F32) for n in (PEERS, PEERS, PEERS + 1)),
         scratch_shapes=[
             pltpu.VMEM((DEPTH, 2 * HALF), BF16),
-            pltpu.VMEM((2 * HALF, 64), BF16),
+            pltpu.VMEM((64, 2 * HALF), BF16),
             pltpu.VMEM((64, 2 * HALF), F32),
         ],
         compiler_params=pltpu.CompilerParams(vmem_limit_bytes=24 << 20),

time: 59.1 us -> 58.8 us (level)
  no operation moved by 1% of the time
where the time goes in v11:
time: 58.8 us; the launch traced here: 57.9 us
  blocking collectives  42.3 us (72%)
  Pallas kernels  10.5 us (18%)
  starting transfers between devices  2.89 us (5%)
  between operations  1.98 us (3%)
    all_to_all x1, blocking collectives, on_device(): own = lax.all_to_all(sent, ('xh', 'g'), 0, 0, tiled=True)  25.4 us
    all_to_all x1, blocking collectives, on_device(): got = lax.all_to_all(partial, ('xh', 'g'), 0, 0, tiled=True)  16.9 us
    pallas_call x1, Pallas kernels, on_device(): pl.pallas_call(far_kernel, out_shape=tuple((jax.ShapeDtypeStruct((n, 8, 1...  3.66 us
    pallas_call x1, Pallas kernels, on_device(): pl.pallas_call(near_kernel, out_shape=(jax.ShapeDtypeStruct((2 * HALF, DE...  3.54 us
    ppermute x1, starting transfers between devices, on_device(): other = lax.ppermute(own[:, 8:], 'c', swap)  2.79 us
    pallas_call x1, Pallas kernels, on_device(): pl.pallas_call(pack_kernel, out_shape=pltpu.VMEM((PEERS, 24, 128), F32),...  2.11 us
  transfers between devices with their start and end apart: 2, of which 1 were waited for; matrix products, arithmetic and copies ran while one was open for 0% of the time, Pallas kernels for 6%

profile of v11, /device:TPU:1, one launch (start us, length us, event | category | flops | bytes accessed | tf_op | source)
XLA Modules:
  0.0 57.9 jit_solution(10172266726544111550)
XLA Ops:
  0.6 2.1 %features.1 = f32[64,24,128]{2,1,0:T(8,128)S(1)} custom-call(bf16[256,1024]{1,0:T(8,128)(2,1)} %enc_hbm.1, bf16[1024,512]{1,0:T(8,128)(2,1)} %w1_hbm.1, bf16[32,512]{1,0:T(8,128)(2,1)} %bitcast.2, f32[1,32]{1,0:T(1,128)} %bitcast.3, f32[16,512]{1,0:T(8,128)} %rhs_ref.1), custom_call_target="tpu_custom_call" | custom-call | tf_op jit(solution)/shard_map/features/pallas_call | solution.py:410
  2.8 25.4 %all_to_all.10.own_ref = f32[64,24,128]{2,1,0:T(8,128)S(1)} all-to-all(f32[64,24,128]{2,1,0:T(8,128)S(1)} %features.1), channel_id=1, replica_groups=mesh['g'=32,'c'=2,'xh'=2] {'xh','g'}, dimensions={0} | all-to-all | bytes 1572864 | tf_op jit(solution)/shard_map/all_to_all | solution.py:427
  28.2 2.8 %collective-permute-start = (f32[64,16,128]{2,1,0:T(8,128)S(1)}, f32[64,16,128]{2,1,0:T(8,128)S(1)}, u32[]{:S(2)}, u32[]{:S(2)}) collective-permute-start(f32[64,16,128]{2,1,0:T(8,128)S(1)} %slice.4), channel_id=1, source_target_pairs={{0,2},{2,0},{1,3},{3,1},{4,6},{6,4},{5,7},{7,5},{8,10},{10,8},{9,1... | collective-permute-start | bytes 1572872 | tf_op jit(solution)/shard_map/ppermute | solution.py:428
  30.9 3.5 %own_columns.1 = (bf16[2048,256]{1,0:T(8,128)(2,1)S(1)}, f32[16,32,128]{2,1,0:T(8,128)S(1)}, bf16[64,2048]{1,0:T(8,128)(2,1)S(1)}, f32[16,32,128]{2,1,0:T(8,128)S(1)}, f32[64,2048]{1,0:T(8,128)S(1)}) custom-call(f32[64,24,128]{2,1,0:T(8,128)S(1)} %all_to_all.10.own_ref), custom_call_target="tpu_custom_call" | custom-call | flops 4294967296 | bytes 1048576 | tf_op jit(solution)/shard_map/own_columns/pallas_call | solution.py:430
  34.5 0.0 collective-permute-done.other_ref
  34.5 3.7 %other_columns.1 = (f32[64,8,128]{2,1,0:T(8,128)S(1)}, f32[64,8,128]{2,1,0:T(8,128)S(1)}, f32[65,8,128]{2,1,0:T(8,128)S(1)}) custom-call(f32[64,16,128]{2,1,0:T(8,128)S(1)} %collective-permute-done.other_ref, bf16[2048,256]{1,0:T(8,128)(2,1)S(1)} %get-tuple-element.10.left_ref, f32[16,32,128]{2,1,0:T(8,128)S(1)} %get-tuple-element.11.rows_ref, ...), custom_call_target="tpu_custom_call" | custom-call | flops 4294967296 | bytes 1048576 | tf_op jit(solution)/shard_map/other_columns/pallas_call | solution.py:447
  38.2 0.1 collective-permute-start.1
  39.6 0.2 collective-permute-done.1.near_ref
  39.8 0.1 join.1
  39.9 0.0 copy-start
  39.9 16.9 %all_to_all.11.got_ref = f32[64,16,128]{2,1,0:T(8,128)S(1)} all-to-all(f32[64,16,128]{2,1,0:T(8,128)S(1)} %join.1), channel_id=1, replica_groups=mesh['g'=32,'c'=2,'xh'=2] {'xh','g'}, dimensions={0} | all-to-all | bytes 1048576 | tf_op jit(solution)/shard_map/all_to_all | solution.py:468
  56.8 0.0 copy-done
  56.8 1.1 %update.1 = (f32[16,512]{1,0:T(8,128)}, f32[16,512]{1,0:T(8,128)}) custom-call(f32[64,16,128]{2,1,0:T(8,128)S(1)} %all_to_all.11.got_ref, f32[16,512]{1,0:T(8,128)S(1)} %copy-done), custom_call_target="tpu_custom_call" | custom-call | tf_op jit(solution)/shard_map/update/pallas_call | solution.py:469
  (1 shorter events, 0.0 us)
Async XLA Ops:
  28.2 6.3 %collective-permute-start = (f32[64,16,128]{2,1,0:T(8,128)S(1)}, f32[64,16,128]{2,1,0:T(8,128)S(1)}, u32[]{:S(2)}, u32[]{:S(2)}) collective-permute-start(f32[64,16,128]{2,1,0:T(8,128)S(1)} %slice.4), channel_id=1, source_target_pairs={{0,2},{2,0},{1,3},{3,1},{4,6},{6,4},{5,7},{7,5},{8,10},{10,8},{9,1... | collective-permute-start | bytes 1572872 | tf_op jit(solution)/shard_map/ppermute | solution.py:428
  38.2 1.6 %collective-permute-start.1 = (f32[65,8,128]{2,1,0:T(8,128)S(1)}, f32[65,8,128]{2,1,0:T(8,128)S(1)}, u32[]{:S(2)}, u32[]{:S(2)}) collective-permute-start(f32[65,8,128]{2,1,0:T(8,128)S(1)} %get-tuple-element.17.far_ref), channel_id=1, source_target_pairs={{0,2},{2,0},{1,3},{3,1},{4,6},{6,4},{5,7},{7,5},{8,10},{10,8},{9,1... | collective-permute-start | bytes 798728 | tf_op jit(solution)/shard_map/ppermute | solution.py:459
  39.9 16.9 %copy-start = (f32[16,512]{1,0:T(8,128)S(1)}, f32[16,512]{1,0:T(8,128)}, u32[]{:S(2)}) copy-start(f32[16,512]{1,0:T(8,128)} %rhs_ref.1) | copy-start | bytes 98308

commit v12 on v11

--- a/solution.py
+++ b/solution.py
@@ -137,7 +137,7 @@
     return features, columns
 
 
-def operand(features, left, depth):
+def operand(features, left):
     y1, y2 = halves(features)
     kept = y1.astype(F32) + y2.astype(F32)
     norm = -0.5 * jnp.sum(kept * kept, axis=0, keepdims=True)
@@ -158,8 +158,6 @@
         ),
     ).astype(BF16)
     parts = ([y1, y1, y2, y2] if left else [y1, y2, y1, y2]) + [tail]
-    if depth > SHALLOW:
-        parts.append(jnp.zeros((depth - SHALLOW, features.shape[1]), BF16))
     return jnp.concatenate(parts, axis=0)
 
 
@@ -169,7 +167,9 @@
 
 def set_columns(right_ref, line_ref, at, points, depth):
     features, columns = points
-    right_ref[:depth, at] = operand(features, False, depth)
+    right_ref[:SHALLOW, at] = operand(features, False)
+    if depth > SHALLOW:
+        right_ref[SHALLOW:, at] = jnp.zeros((depth - SHALLOW, 128), BF16)
     line_ref[:, at] = jnp.concatenate(halves(columns), axis=0)
 
 
@@ -198,7 +198,9 @@
     def set_rows(k, points, depth):
         features, columns = points
         at = slice(k * 128, (k + 1) * 128)
-        left_ref[at, :depth] = operand(features, True, depth).T
+        left_ref[at, :SHALLOW] = operand(features, True).T
+        if depth > SHALLOW:
+            left_ref[at, SHALLOW:] = jnp.zeros((128, depth - SHALLOW), BF16)
         rows_ref[k] = columns
         flat_ref[:, at] = jnp.concatenate(halves(columns), axis=0)
 
@@ -235,7 +237,7 @@
         for k in range(TILES):
             points = points_of(own_ref, k, 8)
             set_rows(k, points, SHALLOW)
-            right_ref[:SHALLOW, 128 * k : 128 * k + 128] = operand(points[0], False, SHALLOW)
+            right_ref[:SHALLOW, 128 * k : 128 * k + 128] = operand(points[0], False)
         multiply(
             flat_ref, SHALLOW, ROWS, lambda k: None, lambda strip: (slice(strip.start, 2 * HALF), strip.stop)
         )

time: 58.8 us -> 58.8 us (level)
  no operation moved by 1% of the time
where the time goes in v12:
time: 58.8 us; the launch traced here: 57.9 us
  blocking collectives  42.3 us (72%)
  Pallas kernels  10.5 us (18%)
  starting transfers between devices  2.89 us (5%)
  between operations  1.98 us (3%)
    all_to_all x1, blocking collectives, on_device(): own = lax.all_to_all(sent, ('xh', 'g'), 0, 0, tiled=True)  25.4 us
    all_to_all x1, blocking collectives, on_device(): got = lax.all_to_all(partial, ('xh', 'g'), 0, 0, tiled=True)  16.9 us
    pallas_call x1, Pallas kernels, on_device(): pl.pallas_call(far_kernel, out_shape=tuple((jax.ShapeDtypeStruct((n, 8, 1...  3.68 us
    pallas_call x1, Pallas kernels, on_device(): pl.pallas_call(near_kernel, out_shape=(jax.ShapeDtypeStruct((2 * HALF, DE...  3.52 us
    ppermute x1, starting transfers between devices, on_device(): other = lax.ppermute(own[:, 8:], 'c', swap)  2.79 us
    pallas_call x1, Pallas kernels, on_device(): pl.pallas_call(pack_kernel, out_shape=pltpu.VMEM((PEERS, 24, 128), F32),...  2.11 us
  transfers between devices with their start and end apart: 2, of which 1 were waited for; matrix products, arithmetic and copies ran while one was open for 0% of the time, Pallas kernels for 6%

profile of v12, /device:TPU:1, one launch (start us, length us, event | category | flops | bytes accessed | tf_op | source)
XLA Modules:
  0.0 57.9 jit_solution(2395201546382682291)
XLA Ops:
  0.6 2.1 %features.1 = f32[64,24,128]{2,1,0:T(8,128)S(1)} custom-call(bf16[256,1024]{1,0:T(8,128)(2,1)} %enc_hbm.1, bf16[1024,512]{1,0:T(8,128)(2,1)} %w1_hbm.1, bf16[32,512]{1,0:T(8,128)(2,1)} %bitcast.2, f32[1,32]{1,0:T(1,128)} %bitcast.3, f32[16,512]{1,0:T(8,128)} %rhs_ref.1), custom_call_target="tpu_custom_call" | custom-call | tf_op jit(solution)/shard_map/features/pallas_call | solution.py:412
  2.8 25.4 %all_to_all.10.own_ref = f32[64,24,128]{2,1,0:T(8,128)S(1)} all-to-all(f32[64,24,128]{2,1,0:T(8,128)S(1)} %features.1), channel_id=1, replica_groups=mesh['g'=32,'c'=2,'xh'=2] {'xh','g'}, dimensions={0} | all-to-all | bytes 1572864 | tf_op jit(solution)/shard_map/all_to_all | solution.py:429
  28.2 2.8 %collective-permute-start = (f32[64,16,128]{2,1,0:T(8,128)S(1)}, f32[64,16,128]{2,1,0:T(8,128)S(1)}, u32[]{:S(2)}, u32[]{:S(2)}) collective-permute-start(f32[64,16,128]{2,1,0:T(8,128)S(1)} %slice.4), channel_id=1, source_target_pairs={{0,2},{2,0},{1,3},{3,1},{4,6},{6,4},{5,7},{7,5},{8,10},{10,8},{9,1... | collective-permute-start | bytes 1572872 | tf_op jit(solution)/shard_map/ppermute | solution.py:430
  30.9 3.5 %own_columns.1 = (bf16[2048,256]{1,0:T(8,128)(2,1)S(1)}, f32[16,32,128]{2,1,0:T(8,128)S(1)}, bf16[64,2048]{1,0:T(8,128)(2,1)S(1)}, f32[16,32,128]{2,1,0:T(8,128)S(1)}, f32[64,2048]{1,0:T(8,128)S(1)}) custom-call(f32[64,24,128]{2,1,0:T(8,128)S(1)} %all_to_all.10.own_ref), custom_call_target="tpu_custom_call" | custom-call | flops 4294967296 | bytes 1048576 | tf_op jit(solution)/shard_map/own_columns/pallas_call | solution.py:432
  34.5 0.0 collective-permute-done.other_ref
  34.5 3.7 %other_columns.1 = (f32[64,8,128]{2,1,0:T(8,128)S(1)}, f32[64,8,128]{2,1,0:T(8,128)S(1)}, f32[65,8,128]{2,1,0:T(8,128)S(1)}) custom-call(f32[64,16,128]{2,1,0:T(8,128)S(1)} %collective-permute-done.other_ref, bf16[2048,256]{1,0:T(8,128)(2,1)S(1)} %get-tuple-element.10.left_ref, f32[16,32,128]{2,1,0:T(8,128)S(1)} %get-tuple-element.11.rows_ref, ...), custom_call_target="tpu_custom_call" | custom-call | flops 4294967296 | bytes 1048576 | tf_op jit(solution)/shard_map/other_columns/pallas_call | solution.py:449
  38.2 0.1 collective-permute-start.1
  39.6 0.2 collective-permute-done.1.near_ref
  39.8 0.1 join.1
  39.9 0.0 copy-start
  39.9 16.9 %all_to_all.11.got_ref = f32[64,16,128]{2,1,0:T(8,128)S(1)} all-to-all(f32[64,16,128]{2,1,0:T(8,128)S(1)} %join.1), channel_id=1, replica_groups=mesh['g'=32,'c'=2,'xh'=2] {'xh','g'}, dimensions={0} | all-to-all | bytes 1048576 | tf_op jit(solution)/shard_map/all_to_all | solution.py:470
  56.8 0.0 copy-done
  56.8 1.1 %update.1 = (f32[16,512]{1,0:T(8,128)}, f32[16,512]{1,0:T(8,128)}) custom-call(f32[64,16,128]{2,1,0:T(8,128)S(1)} %all_to_all.11.got_ref, f32[16,512]{1,0:T(8,128)S(1)} %copy-done), custom_call_target="tpu_custom_call" | custom-call | tf_op jit(solution)/shard_map/update/pallas_call | solution.py:471
  (1 shorter events, 0.0 us)
Async XLA Ops:
  28.2 6.3 %collective-permute-start = (f32[64,16,128]{2,1,0:T(8,128)S(1)}, f32[64,16,128]{2,1,0:T(8,128)S(1)}, u32[]{:S(2)}, u32[]{:S(2)}) collective-permute-start(f32[64,16,128]{2,1,0:T(8,128)S(1)} %slice.4), channel_id=1, source_target_pairs={{0,2},{2,0},{1,3},{3,1},{4,6},{6,4},{5,7},{7,5},{8,10},{10,8},{9,1... | collective-permute-start | bytes 1572872 | tf_op jit(solution)/shard_map/ppermute | solution.py:430
  38.2 1.6 %collective-permute-start.1 = (f32[65,8,128]{2,1,0:T(8,128)S(1)}, f32[65,8,128]{2,1,0:T(8,128)S(1)}, u32[]{:S(2)}, u32[]{:S(2)}) collective-permute-start(f32[65,8,128]{2,1,0:T(8,128)S(1)} %get-tuple-element.17.far_ref), channel_id=1, source_target_pairs={{0,2},{2,0},{1,3},{3,1},{4,6},{6,4},{5,7},{7,5},{8,10},{10,8},{9,1... | collective-permute-start | bytes 798728 | tf_op jit(solution)/shard_map/ppermute | solution.py:461
  39.9 16.9 %copy-start = (f32[16,512]{1,0:T(8,128)S(1)}, f32[16,512]{1,0:T(8,128)}, u32[]{:S(2)}) copy-start(f32[16,512]{1,0:T(8,128)} %rhs_ref.1) | copy-start | bytes 98308
